TPU v7x, 256 devices: a whole 4x4x8 slice. The times are simulated.
256 devices in a mesh: section: 2 (over z_lo), tile: 128 (over y, x, z_hi, core).
Axes of the slice: x: 4, y: 4, z: 8 (z_hi: 4, z_lo: 2; z = z_hi * 2 + z_lo), core: 2. Of those that a mesh axis runs over, the one named last changes fastest.
Arguments:
- features: bfloat16 [128, 12, 1024, 128], P('tile', 'section'), may hold values from -6 to 6
- conv_weight: bfloat16 [5, 5, 128, 128], replicated, may hold values from -0.109375 to 0.109375
- head_weight: bfloat16 [128, 16], replicated, may hold values from -0.5 to 0.5
- kernels: bfloat16 [128, 1024, 2048], P('tile'), may hold values from -0.015625 to 0.015625
- source_weights: float32 [8], replicated, may hold values from 0.3 to 3
Outputs:
- intensity: float32 [128, 12, 1024], P('tile', 'section')
All inputs are finite; a program needn't handle non-finite values.
Results may differ from a plain program's by a relative error of at most 0.0018.
Values may be sent and summed in bfloat16 or wider, within the bound.
No kernel may reach another device: no remote copies, remote signals or barrier semaphores. Data moves between devices by JAX's collectives and lax.ppermute only.
A program may use at most 64 MiB of HBM per device.

v0:
```python
import jax
import jax.numpy as jnp
from jax import lax
from jax.sharding import PartitionSpec as P

ANG = 8


def padded_2(block, sides, width):
    for axis, dim in sides:
        count = lax.axis_size(axis)
        forward = [(i, i + 1) for i in range(count - 1)]
        backward = [(target, source) for source, target in forward]
        low = lax.ppermute(
            lax.slice_in_dim(block, block.shape[dim] - width, None, axis=dim), axis, forward
        )
        high = lax.ppermute(lax.slice_in_dim(block, 0, width, axis=dim), axis, backward)
        block = jnp.concatenate([low, block, high], axis=dim)
    return block


def on_device(features, conv_weight, head_weight, kernels, source_weights):
    tile_count = lax.axis_size("tile")
    groups = tile_count // ANG
    windows = features.shape[0]
    rows_dev = features.shape[1]
    pixels = features.shape[2]
    angle_index = lax.axis_index("tile") // groups
    angle_weight = lax.dynamic_index_in_dim(source_weights, angle_index, 0, keepdims=False)
    padded = padded_2(features, (("section", 1),), 4)
    preact = lax.conv_general_dilated(
        padded,
        conv_weight,
        (1, 1),
        ((0, 0), (4, 4)),
        rhs_dilation=(2, 2),
        dimension_numbers=("NHWC", "HWIO", "NHWC"),
        preferred_element_type=jnp.float32,
    )
    hidden = jax.nn.gelu(preact, approximate=True).astype(jnp.bfloat16)
    near_field = jnp.einsum(
        "nrwc,cd->dnrw", hidden, head_weight, preferred_element_type=jnp.float32
    ).astype(jnp.bfloat16)
    near_field = near_field.reshape(ANG, 2, windows * rows_dev, pixels)
    outgoing = jnp.repeat(near_field, groups, axis=0)
    product = jnp.einsum(
        "sprw,kwv->pksrv",
        lax.all_to_all(outgoing, "tile", split_axis=0, concat_axis=0, tiled=True),
        kernels,
        preferred_element_type=jnp.float32,
    )
    real_part = product[0, :, :, :, :pixels] - product[1, :, :, :, pixels:]
    imag_part = product[0, :, :, :, pixels:] + product[1, :, :, :, :pixels]
    mapped = angle_weight * jnp.sum(real_part * real_part + imag_part * imag_part, axis=0)
    summed = lax.psum_scatter(mapped, "tile", scatter_dimension=0, tiled=True)
    return summed


def solution(mesh):
    in_specs = (P("tile", "section", None, None), P(), P(), P("tile", None, None), P())
    out_specs = P("tile", "section", None)
    return jax.shard_map(
        on_device, mesh=mesh, in_specs=in_specs, out_specs=out_specs, check_vma=False
    )
```

profile of v0, /device:TPU:32, one launch (start us, length us, event | category | flops | bytes accessed | tf_op | source)
XLA Modules:
  0.0 884.6 jit_solution(7466410592684700047)
XLA Ops:
  6.5 0.0 copy-start
  6.5 1.8 fusion.33
  8.4 1.3 collective-permute-start
  9.7 4.7 collective-permute-start.1
  14.4 20.8 %collective-permute-done = bf16[1,4,1024,128]{3,2,1,0:T(8,128)(2,1)S(1)} collective-permute-done((bf16[1,4,1024,128]{3,2,1,0:T(8,128)(2,1)S(1)}, bf16[1,4,1024,128]{3,2,1,0:T(8,128)(2,1)S(1)}, u32[]{:S(2)}, u32[]{:S(2)}) %collective-permute-start) | collective-permute-done | bytes 1048608 | tf_op jit(solution)/shard_map/ppermute | solution.py:14
  35.2 1.2 collective-permute-done.1
  36.4 0.0 copy-done.1
  36.4 0.4 maximum_bitcast_fusion
  36.9 2.8 pad
  39.7 6.5 reshape.47
  46.2 2.6 copy.19
  48.8 0.1 slice.26
  48.8 0.0 copy-done
  48.9 0.0 copy-done.4
  48.9 11.1 %fusion.16 = bf16[6,8,129,128]{3,1,2,0:T(8,128)(2,1)S(1)} fusion(bf16[5,5,128,128]{3,2,1,0:T(8,128)(2,1)S(1)} %copy-done, bf16[14,1,7,8,128]{4,2,3,0,1:T(8,128)(2,1)S(1)} %slice.26, bf16[14,1,8,129,128]{4,2,3,0,1:T(8,128)(2,1)S(1)} %copy.19, pred[8,129]{0,1:T(8,128)(4,1)S(1)} %copy-done.4), kind=kOutput, calls=%fused_computation.19 | convolution fusion | flops 5092196352 | bytes 6304776 | tf_op jit(solution)/shard_map/conv_general_dilated | solution.py:31
  60.0 0.0 copy-start.2
  60.0 0.4 copy.20
  60.4 2.0 reshape.51
  62.4 1.9 fusion.28
  64.3 0.1 reshape.42
  64.4 0.1 copy.21
  64.6 3.6 broadcast_in_dim.3
  68.2 15.5 %all-to-all-start = ((bf16[128,2,6,1024]{3,1,2,0:T(2,128)(2,1)}), bf16[128,2,6,1024]{3,1,2,0:T(2,128)(2,1)}, u32[]{:S(2)}, u32[]{:S(2)}) async-start(bf16[128,2,6,1024]{3,1,2,0:T(2,128)(2,1)} %bitcast.43), calls=%async_computation | async-start | bytes 6291456 | tf_op jit(solution)/shard_map/all_to_all | solution.py:48
  83.7 0.0 reduce-scatter.2.cloned.1.call-start
  83.8 0.6 dynamic_slice.4
  84.3 66.1 %all-to-all-done = bf16[128,2,6,1024]{3,1,2,0:T(2,128)(2,1)} async-done(((bf16[128,2,6,1024]{3,1,2,0:T(2,128)(2,1)}), bf16[128,2,6,1024]{3,1,2,0:T(2,128)(2,1)}, u32[]{:S(2)}, u32[]{:S(2)}) %all-to-all-start) | async-done | bytes 3145760 | tf_op jit(solution)/shard_map/all_to_all | solution.py:48
  150.5 10.8 %convolution_bitcast_fusion = f32[2,1,128,6,2048]{4,2,3,0,1:T(8,128)S(1)} fusion(bf16[1,1024,2048]{2,1,0:T(8,128)(2,1)} %param.8, bf16[128,2,6,1024]{3,1,2,0:T(2,128)(2,1)} %all-to-all-done), kind=kOutput, calls=%fused_computation.2 | convolution fusion | flops 6442450944 | bytes 19922944 | tf_op jit(solution)/shard_map/sprw,kwv->pksrv/dot_general | solution.py:46
  161.3 2.5 fusion.20
  163.8 3.8 copy.23
  167.7 0.0 reduce-scatter.2.cloned.1.call-update
  167.7 708.7 %reduce-scatter.2.cloned.1.call-done = f32[1,6,1024]{2,1,0:T(8,128)} async-done(((f32[128,6,1024]{2,1,0:T(8,128)}), f32[1,6,1024]{2,1,0:T(8,128)}) %reduce-scatter.2.cloned.1.call-update) | async-done | bytes 24592 | tf_op jit(solution)/shard_map/reduce_scatter | solution.py:55
  876.4 1.4 copy.24
  (5 shorter events, 0.0 us)
Async XLA Ops:
  6.5 42.3 %copy-start = (bf16[5,5,128,128]{3,2,1,0:T(8,128)(2,1)S(1)}, bf16[5,5,128,128]{3,2,1,0:T(8,128)(2,1)}, u32[]{:S(2)}) copy-start(bf16[5,5,128,128]{3,2,1,0:T(8,128)(2,1)} %param.6) | copy-start | bytes 2457604
  6.5 29.9 %copy-start.1 = (bf16[1,6,1024,128]{3,2,1,0:T(8,128)(2,1)S(1)}, bf16[1,6,1024,128]{3,2,1,0:T(8,128)(2,1)}, u32[]{:S(2)}) copy-start(bf16[1,6,1024,128]{3,2,1,0:T(8,128)(2,1)} %param.5) | copy-start | bytes 4718596
  8.4 26.8 %collective-permute-start = (bf16[1,4,1024,128]{3,2,1,0:T(8,128)(2,1)S(1)}, bf16[1,4,1024,128]{3,2,1,0:T(8,128)(2,1)S(1)}, u32[]{:S(2)}, u32[]{:S(2)}) collective-permute-start(bf16[1,4,1024,128]{3,2,1,0:T(8,128)(2,1)S(1)} %get-tuple-element.5), channel_id=1, source_target_pairs={{0,128},{1,129},{2,130},{3,131},{4,132},{5,133},{6,134},{7,135},{8... | collective-permute-start | bytes 3145736 | tf_op jit(solution)/shard_map/ppermute | solution.py:14
  9.7 26.7 %collective-permute-start.1 = (bf16[1,4,1024,128]{3,2,1,0:T(8,128)(2,1)S(1)}, bf16[1,4,1024,128]{3,2,1,0:T(8,128)(2,1)S(1)}, u32[]{:S(2)}, u32[]{:S(2)}) collective-permute-start(bf16[1,4,1024,128]{3,2,1,0:T(8,128)(2,1)S(1)} %get-tuple-element.6), channel_id=1, source_target_pairs={{128,0},{129,1},{130,2},{131,3},{132,4},{133,5},{134,6},{135,7},{1... | collective-permute-start | bytes 3145736 | tf_op jit(solution)/shard_map/ppermute | solution.py:17
  46.2 2.7 copy-start.4
  60.0 2.4 copy-start.2
  68.2 15.6 %copy-start.3 = (f32[8]{0:T(128)S(1)}, f32[8]{0:T(128)}, u32[]{:S(2)}) copy-start(f32[8]{0:T(128)} %param.9) | copy-start | bytes 100
  68.2 82.3 %all-to-all-start = ((bf16[128,2,6,1024]{3,1,2,0:T(2,128)(2,1)}), bf16[128,2,6,1024]{3,1,2,0:T(2,128)(2,1)}, u32[]{:S(2)}, u32[]{:S(2)}) async-start(bf16[128,2,6,1024]{3,1,2,0:T(2,128)(2,1)} %bitcast.43), calls=%async_computation | async-start | bytes 6291456 | tf_op jit(solution)/shard_map/all_to_all | solution.py:48
  83.7 792.7 %reduce-scatter.2.cloned.1.call-start = ((), (), s32[]{:S(2)}) async-start(), calls=%async_computation.2 | async-start | bytes 4227072 | tf_op jit(solution)/shard_map/reduce_scatter | solution.py:55
Sparse Core Ops, SparseCore 0:
  167.8 708.4 reduce-scatter.1
where the time goes:
time: 885 us
  waiting for transfers between devices  797 us (90%)
  local copies, waits for them, and re-layouts  25.9 us (3%)
  matrix products  23.9 us (3%)
  starting transfers between devices  21.5 us (2%)
  between operations  13.5 us (2%)
    reduce_scatter x1, waiting for transfers between devices, on_device(): summed = lax.psum_scatter(mapped, 'tile', scatter_dimension=0, tiled=True)  709 us
    all_to_all x1, waiting for transfers between devices, on_device(): lax.all_to_all(outgoing, 'tile', split_axis=0, concat_axis=0, tiled=True)  66.1 us
    ppermute x1, waiting for transfers between devices, padded_2(): lax.ppermute(lax.slice_in_dim(block, block.shape[dim] - width, None, axis...  20.8 us
  transfers between devices with their start and end apart: 4, of which 4 were waited for; matrix products, arithmetic and copies ran while one was open for 0% of the time, Pallas kernels for 0%

commit v1 on v0

v1 whole, which is shorter than its diff:
```python
import jax
import jax.numpy as jnp
from jax import lax
from jax.sharding import Mesh, PartitionSpec as P

ANG = 8
TILE = ("y", "xh", "xl", "z", "c")


def padded_2(block, axis, dim, width):
    low = lax.ppermute(
        lax.slice_in_dim(block, block.shape[dim] - width, None, axis=dim), axis, [(0, 1)]
    )
    high = lax.ppermute(lax.slice_in_dim(block, 0, width, axis=dim), axis, [(1, 0)])
    return jnp.concatenate([low, block, high], axis=dim)


def on_device(features, conv_weight, head_weight, kernels, source_weights):
    pixels = features.shape[2]
    rows = features.shape[1]
    angle = lax.axis_index(("y", "xh"))
    weight = lax.dynamic_index_in_dim(source_weights, angle, 0, keepdims=False)
    swap = [(0, 1), (1, 0)]
    both = jnp.concatenate([kernels, lax.ppermute(kernels, "c", swap)], axis=0)
    padded = padded_2(features, "s", 1, 4)
    preact = lax.conv_general_dilated(
        padded,
        conv_weight,
        (1, 1),
        ((0, 0), (4, 4)),
        rhs_dilation=(2, 2),
        dimension_numbers=("NHWC", "HWIO", "NHWC"),
        preferred_element_type=jnp.float32,
    )
    hidden = jax.nn.gelu(preact, approximate=True).astype(jnp.bfloat16)
    near = jnp.einsum(
        "rwc,cd->drw", hidden[0], head_weight, preferred_element_type=jnp.float32
    ).astype(jnp.bfloat16)
    near = near.reshape(ANG, 2, rows, pixels)
    field = lax.all_to_all(near, ("y", "xh"), 0, 0, tiled=True)
    field = lax.all_gather(field, "z", axis=1, tiled=False)
    other = lax.ppermute(field, "xl", swap)

    def image(part):
        product = jnp.einsum(
            "azprw,kwv->pkazrv", part, both, preferred_element_type=jnp.float32
        )
        re = product[0, ..., :pixels] - product[1, ..., pixels:]
        im = product[0, ..., pixels:] + product[1, ..., :pixels]
        return weight * jnp.sum(re * re + im * im, axis=0)

    sent = lax.ppermute(image(other).astype(jnp.bfloat16), "xl", swap)
    total = image(field) + sent.astype(jnp.float32)
    total = total.astype(jnp.bfloat16).reshape(-1, rows, pixels)
    pieces = lax.all_to_all(total, ("y", "xh", "z"), 0, 0, tiled=True)
    return jnp.sum(pieces.astype(jnp.float32), axis=0, keepdims=True)


def solution(mesh):
    fine = Mesh(mesh.devices.reshape(2, 4, 2, 2, 4, 2), ("s",) + TILE)
    in_specs = (P(TILE, "s", None, None), P(), P(), P(TILE, None, None), P())
    return jax.shard_map(
        on_device, mesh=fine, in_specs=in_specs, out_specs=P(TILE, "s", None), check_vma=False
    )
```

time: 885 us -> 152 us (0.17)
  waiting for transfers between devices: 797 us -> 40.5 us
  blocking collectives: 0 us -> 57.2 us
  starting transfers between devices: 21.5 us -> 6.4 us
  between operations: 13.5 us -> 0.19 us
    reduce_scatter x1 -> x0, waiting for transfers between devices: 709 us -> none  [on_device(): summed = lax.psum_scatter(mapped, 'tile', scatter_dimension=0, tiled=True)]
    all_to_all x1 -> x0, waiting for transfers between devices: 66.1 us -> none  [on_device(): lax.all_to_all(outgoing, 'tile', split_axis=0, concat_axis=0, tiled=True)]
    ppermute x1 -> x4, waiting for transfers between devices: 1.24 us -> 36.3 us  [the longest x1 21.5 us: padded_2(): lax.ppermute(lax.slice_in_dim(block, 0, width, axis=dim), axis, [(1, 0)])]
    all_to_all x0 -> x2, blocking collectives: none -> 34.6 us  [the longest x1 21.2 us: on_device(): pieces = lax.all_to_all(total, ('y', 'xh', 'z'), 0, 0, tiled=True)]
    all_gather x0 -> x1, blocking collectives: none -> 22.6 us  [on_device(): field = lax.all_gather(field, 'z', axis=1, tiled=False)]
    ppermute x1, waiting for transfers between devices: 20.8 us -> 4.18 us  [padded_2(): lax.ppermute(lax.slice_in_dim(block, block.shape[dim] - width, None, axis...]
    all_to_all x1 -> x0, starting transfers between devices: 15.5 us -> none  [on_device(): lax.all_to_all(outgoing, 'tile', split_axis=0, concat_axis=0, tiled=True)]
  transfers between devices with their start and end apart: 4 -> 5, of which waited for: 4 -> 4; matrix products, arithmetic and copies ran while one was open for 0% -> 25% of each run, Pallas kernels for 0% -> 0%
where the time goes in v1:
time: 152 us; the launch traced here: 151 us
  blocking collectives  57.2 us (38%)
  waiting for transfers between devices  40.5 us (27%)
  matrix products  25 us (16%)
  local copies, waits for them, and re-layouts  18.1 us (12%)
  starting transfers between devices  6.4 us (4%)
  other arithmetic  4.05 us (3%)
    all_gather x1, blocking collectives, on_device(): field = lax.all_gather(field, 'z', axis=1, tiled=False)  22.6 us
    ppermute x1, waiting for transfers between devices, padded_2(): lax.ppermute(lax.slice_in_dim(block, 0, width, axis=dim), axis, [(1, 0)])  21.5 us
    all_to_all x1, blocking collectives, on_device(): pieces = lax.all_to_all(total, ('y', 'xh', 'z'), 0, 0, tiled=True)  21.2 us
    ppermute x1, waiting for transfers between devices, on_device(): other = lax.ppermute(field, 'xl', swap)  14.4 us
    all_to_all x1, blocking collectives, on_device(): field = lax.all_to_all(near, ('y', 'xh'), 0, 0, tiled=True)  13.5 us
    dot_general x2, matrix products, image(): jnp.einsum('azprw,kwv->pkazrv', part, both, preferred_element_type=jnp.fl...  12 us
    conv_general_dilated x1, matrix products, on_device(): lax.conv_general_dilated(padded, conv_weight, (1, 1), ((0, 0), (4, 4)), r...  11.1 us
    conv_general_dilated x3, local copies, waits for them, and re-layouts, on_device(): lax.conv_general_dilated(padded, conv_weight, (1, 1), ((0, 0), (4, 4)), r...  9.17 us
  transfers between devices with their start and end apart: 5, of which 4 were waited for; matrix products, arithmetic and copies ran while one was open for 25% of the time, Pallas kernels for 0%

profile of v1, /device:TPU:32, one launch (start us, length us, event | category | flops | bytes accessed | tf_op | source)
XLA Modules:
  0.0 151.5 jit_solution(15257540184752605005)
XLA Ops:
  0.0 1.8 %fusion.41 = (bf16[1,4,1024,128]{3,2,1,0:T(8,128)(2,1)S(1)}, bf16[1,4,1024,128]{3,2,1,0:T(8,128)(2,1)S(1)}) fusion(bf16[1,6,1024,128]{3,2,1,0:T(8,128)(2,1)} %param.5), kind=kLoop, calls=%fused_computation.50 | loop fusion | bytes 4194304 | tf_op jit(solution)/shard_map/slice | solution.py:12
  1.9 3.8 %collective-permute-start.2 = (bf16[1,4,1024,128]{3,2,1,0:T(8,128)(2,1)S(1)}, bf16[1,4,1024,128]{3,2,1,0:T(8,128)(2,1)S(1)}, u32[]{:S(2)}, u32[]{:S(2)}) collective-permute-start(bf16[1,4,1024,128]{3,2,1,0:T(8,128)(2,1)S(1)} %get-tuple-element.6), channel_id=1, source_target_pairs={{128,0},{129,1},{130,2},{131,3},{132,4},{133,5},{134,6},{135,7},{1... | collective-permute-start | bytes 3145736 | tf_op jit(solution)/shard_map/ppermute | solution.py:14
  5.7 1.3 collective-permute-start.1
  7.0 21.5 %collective-permute-done.2 = bf16[1,4,1024,128]{3,2,1,0:T(8,128)(2,1)S(1)} collective-permute-done((bf16[1,4,1024,128]{3,2,1,0:T(8,128)(2,1)S(1)}, bf16[1,4,1024,128]{3,2,1,0:T(8,128)(2,1)S(1)}, u32[]{:S(2)}, u32[]{:S(2)}) %collective-permute-start.2) | collective-permute-done | bytes 1048608 | tf_op jit(solution)/shard_map/ppermute | solution.py:14
  28.5 4.2 %collective-permute-done.1 = bf16[1,4,1024,128]{3,2,1,0:T(8,128)(2,1)S(1)} collective-permute-done((bf16[1,4,1024,128]{3,2,1,0:T(8,128)(2,1)S(1)}, bf16[1,4,1024,128]{3,2,1,0:T(8,128)(2,1)S(1)}, u32[]{:S(2)}, u32[]{:S(2)}) %collective-permute-start.1) | collective-permute-done | bytes 1048608 | tf_op jit(solution)/shard_map/ppermute | solution.py:11
  32.7 0.4 maximum_bitcast_fusion.7
  33.2 2.9 %pad = bf16[14,1,1032,128]{3,2,0,1:T(8,128)(2,1)} pad(bf16[14,1,1024,128]{3,2,0,1:T(8,128)(2,1)S(1)} %maximum_bitcast_fusion.7, bf16[]{:T(256)} %constant.32), padding=0_0x0_0x4_4x0_0 | pad | bytes 7368706 | tf_op jit(solution)/shard_map/concatenate | solution.py:15
  36.0 6.5 %reshape.20 = bf16[14,1,8,129,128]{4,3,2,0,1:T(8,128)(2,1)} reshape(bf16[14,1,1032,128]{3,2,0,1:T(8,128)(2,1)} %pad) | data formatting | bytes 7397376 | tf_op jit(solution)/shard_map/conv_general_dilated | solution.py:26
  42.5 2.6 %copy.23 = bf16[14,1,8,129,128]{4,2,3,0,1:T(8,128)(2,1)S(1)} copy(bf16[14,1,8,129,128]{4,3,2,0,1:T(8,128)(2,1)} %reshape.20) | data formatting | bytes 7397376 | tf_op jit(solution)/shard_map/conv_general_dilated | solution.py:26
  45.2 11.1 %fusion.19 = bf16[6,8,129,128]{3,1,2,0:T(8,128)(2,1)S(1)} fusion(bf16[5,5,128,128]{3,2,1,0:T(8,128)(2,1)S(1)} %copy-done, bf16[14,1,7,8,128]{4,2,3,0,1:T(8,128)(2,1)S(1)} %slice.42, bf16[14,1,8,129,128]{4,2,3,0,1:T(8,128)(2,1)S(1)} %copy.23, pred[8,129]{0,1:T(8,128)(4,1)S(1)} %copy-done.5), kind=kOutput, calls=%fused_computation.22 | convolution fusion | flops 5092196352 | bytes 6304776 | tf_op jit(solution)/shard_map/conv_general_dilated | solution.py:26
  56.4 0.4 copy.24
  56.9 2.0 %reshape.24 = bf16[6,1,1032,128]{3,2,0,1:T(8,128)(2,1)} reshape(bf16[6,8,129,128]{3,2,1,0:T(8,128)(2,1)S(1)} %copy.24) | data formatting | bytes 3170304 | tf_op jit(solution)/shard_map/convert_element_type | solution.py:35
  58.8 1.9 %fusion.33 = bf16[16,6,1024]{2,0,1:T(8,128)(2,1)S(1)} fusion(bf16[6,1,1032,128]{3,2,0,1:T(8,128)(2,1)} %reshape.24, bf16[128,16]{0,1:T(8,128)(2,1)S(1)} %copy-done.3), kind=kOutput, calls=%fused_computation.39 | convolution fusion | flops 25264128 | bytes 1773568 | tf_op jit(solution)/shard_map/rwc,cd->drw/dot_general | solution.py:36
  60.8 0.1 reshape.16
  60.9 0.1 copy.25
  61.0 13.5 %all_to_all.10 = bf16[8,2,6,1024]{3,1,2,0:T(2,128)(2,1)S(1)} all-to-all(bf16[8,2,6,1024]{3,1,2,0:T(2,128)(2,1)S(1)} %copy.25), channel_id=1, replica_groups=mesh['s'=2,'y'=4,'xh'=2,'xl'=2,'z'=4,'c'=2] {'y','xh'}, dimensions={0} | all-to-all | bytes 393216 | tf_op jit(solution)/shard_map/all_to_all | solution.py:40
  74.5 22.6 %all-gather = bf16[8,8,6,1024]{3,0,2,1:T(8,128)(2,1)S(1)} all-gather(bf16[8,2,6,1024]{3,0,2,1:T(8,128)(2,1)S(1)} %copy.26), channel_id=2, replica_groups=mesh['s'=2,'y'=4,'xh'=2,'xl'=2,'z'=4,'c'=2] {'z'}, dimensions={1}, use_global_device_ids=true | all-gather | bytes 983040 | tf_op jit(solution)/shard_map/all_gather | solution.py:41
  97.1 0.6 collective-permute-start.3
  97.7 0.6 dynamic_slice.4
  98.3 14.4 %collective-permute-done.3 = bf16[8,4,2,6,1024]{4,0,3,2,1:T(8,128)(2,1)S(1)} collective-permute-done((bf16[8,4,2,6,1024]{4,0,3,2,1:T(8,128)(2,1)S(1)}, bf16[8,4,2,6,1024]{4,0,3,2,1:T(8,128)(2,1)S(1)}, u32[]{:S(2)}, u32[]{:S(2)}) %collective-permute-start.3) | collective-permute-done | bytes 786464 | tf_op jit(solution)/shard_map/ppermute | solution.py:42
  112.7 6.0 %fusion.11 = f32[2,2,8,4,6,2048]{5,2,4,0,3,1:T(8,128)S(1)} fusion(bf16[1,1024,2048]{2,1,0:T(8,128)(2,1)} %collective-permute-done, bf16[1,1024,2048]{2,1,0:T(8,128)(2,1)} %param.8, bf16[8,4,2,6,1024]{4,0,3,2,1:T(8,128)(2,1)S(1)} %collective-permute-done.3), kind=kOutput, calls=%fused_computation.13 | convolution fusion | flops 3238002688 | bytes 15466496 | tf_op jit(solution)/shard_map/azprw,kwv->pkazrv/dot_general | solution.py:45
  118.8 0.8 fusion.25
  119.6 1.1 multiply_convert_fusion
  120.7 0.7 collective-permute-start.4
  121.4 6.0 %fusion.10 = f32[2,2,8,4,6,2048]{5,2,4,0,3,1:T(8,128)S(1)} fusion(bf16[8,4,2,6,1024,1]{4,0,3,2,1,5:T(8,128)(2,1)S(1)} %bitcast.51, bf16[1,1024,2048]{2,1,0:T(8,128)(2,1)} %collective-permute-done, bf16[1,1024,2048]{2,1,0:T(8,128)(2,1)S(1)} %copy-done.2), kind=kOutput, calls=%fused_computation.12 | convolution fusion | flops 3238002688 | bytes 15466496 | tf_op jit(solution)/shard_map/azprw,kwv->pkazrv/dot_general | solution.py:45
  127.4 0.8 fusion.29
  128.2 0.4 collective-permute-done.4
  128.6 0.8 add_convert_fusion
  129.3 0.2 copy.30
  129.6 21.2 %all_to_all.11 = bf16[32,6,1024]{2,1,0:T(8,128)(2,1)S(1)} all-to-all(bf16[32,6,1024]{2,1,0:T(8,128)(2,1)S(1)} %bitcast.49), channel_id=1, replica_groups=mesh['s'=2,'y'=4,'xh'=2,'xl'=2,'z'=4,'c'=2] {'y','xh','z'}, dimensions={0} | all-to-all | bytes 786432 | tf_op jit(solution)/shard_map/all_to_all | solution.py:55
  150.8 0.1 convert_reduce_fusion
  150.9 0.6 broadcast_in_dim.3
  (16 shorter events, 0.2 us)
Async XLA Ops:
  0.0 45.2 %copy-start = (bf16[5,5,128,128]{3,2,1,0:T(8,128)(2,1)S(1)}, bf16[5,5,128,128]{3,2,1,0:T(8,128)(2,1)}, u32[]{:S(2)}) copy-start(bf16[5,5,128,128]{3,2,1,0:T(8,128)(2,1)} %param.6) | copy-start | bytes 2457604
  0.0 32.7 %copy-start.1 = (bf16[1,6,1024,128]{3,2,1,0:T(8,128)(2,1)S(1)}, bf16[1,6,1024,128]{3,2,1,0:T(8,128)(2,1)}, u32[]{:S(2)}) copy-start(bf16[1,6,1024,128]{3,2,1,0:T(8,128)(2,1)} %param.5) | copy-start | bytes 4718596
  0.0 112.7 %collective-permute-start = (bf16[1,1024,2048]{2,1,0:T(8,128)(2,1)}, bf16[1,1024,2048]{2,1,0:T(8,128)(2,1)}, u32[]{:S(2)}, u32[]{:S(2)}) collective-permute-start(bf16[1,1024,2048]{2,1,0:T(8,128)(2,1)} %param.8), channel_id=1, source_target_pairs={{0,1},{1,0},{2,3},{3,2},{4,5},{5,4},{6,7},{7,6},{8,9},{9,8},{10,11... | collective-permute-start | bytes 12582920 | tf_op jit(solution)/shard_map/ppermute | solution.py:24
  1.9 26.7 %collective-permute-start.2 = (bf16[1,4,1024,128]{3,2,1,0:T(8,128)(2,1)S(1)}, bf16[1,4,1024,128]{3,2,1,0:T(8,128)(2,1)S(1)}, u32[]{:S(2)}, u32[]{:S(2)}) collective-permute-start(bf16[1,4,1024,128]{3,2,1,0:T(8,128)(2,1)S(1)} %get-tuple-element.6), channel_id=1, source_target_pairs={{128,0},{129,1},{130,2},{131,3},{132,4},{133,5},{134,6},{135,7},{1... | collective-permute-start | bytes 3145736 | tf_op jit(solution)/shard_map/ppermute | solution.py:14
  5.7 27.0 %collective-permute-start.1 = (bf16[1,4,1024,128]{3,2,1,0:T(8,128)(2,1)S(1)}, bf16[1,4,1024,128]{3,2,1,0:T(8,128)(2,1)S(1)}, u32[]{:S(2)}, u32[]{:S(2)}) collective-permute-start(bf16[1,4,1024,128]{3,2,1,0:T(8,128)(2,1)S(1)} %get-tuple-element.5), channel_id=1, source_target_pairs={{0,128},{1,129},{2,130},{3,131},{4,132},{5,133},{6,134},{7,135},{8... | collective-permute-start | bytes 3145736 | tf_op jit(solution)/shard_map/ppermute | solution.py:11
  42.5 2.7 %copy-start.5 = (pred[8,129]{0,1:T(8,128)(4,1)S(1)}, pred[8,129]{0,1:T(8,128)(4,1)}, u32[]{:S(2)}) copy-start(pred[8,129]{0,1:T(8,128)(4,1)} %constant.36) | copy-start | bytes 3100
  56.4 2.5 %copy-start.3 = (bf16[128,16]{0,1:T(8,128)(2,1)S(1)}, bf16[128,16]{0,1:T(8,128)(2,1)}, u32[]{:S(2)}) copy-start(bf16[128,16]{0,1:T(8,128)(2,1)} %param.7) | copy-start | bytes 12292
  56.8 40.9 %copy-start.4 = (f32[8]{0:T(128)S(1)}, f32[8]{0:T(128)}, u32[]{:S(2)}) copy-start(f32[8]{0:T(128)} %param.9) | copy-start | bytes 100
  97.1 15.6 %collective-permute-start.3 = (bf16[8,4,2,6,1024]{4,0,3,2,1:T(8,128)(2,1)S(1)}, bf16[8,4,2,6,1024]{4,0,3,2,1:T(8,128)(2,1)S(1)}, u32[]{:S(2)}, u32[]{:S(2)}) collective-permute-start(bf16[8,4,2,6,1024]{4,0,3,2,1:T(8,128)(2,1)S(1)} %bitcast.50), channel_id=1, source_target_pairs={{0,8},{8,0},{1,9},{9,1},{2,10},{10,2},{3,11},{11,3},{4,12},{12,4},... | collective-permute-start | bytes 2359304 | tf_op jit(solution)/shard_map/ppermute | solution.py:42
  118.8 2.7 %copy-start.2 = (bf16[1,1024,2048]{2,1,0:T(8,128)(2,1)S(1)}, bf16[1,1024,2048]{2,1,0:T(8,128)(2,1)}, u32[]{:S(2)}) copy-start(bf16[1,1024,2048]{2,1,0:T(8,128)(2,1)} %param.8) | copy-start | bytes 12582916
  120.7 7.9 %collective-permute-start.4 = (bf16[8,4,6,1024]{3,0,2,1:T(8,128)(2,1)S(1)}, bf16[8,4,6,1024]{3,0,2,1:T(8,128)(2,1)S(1)}, u32[]{:S(2)}, u32[]{:S(2)}) collective-permute-start(bf16[8,4,6,1024]{3,0,2,1:T(8,128)(2,1)S(1)} %multiply_convert_fusion), channel_id=1, source_target_pairs={{0,8},{8,0},{1,9},{9,1},{2,10},{10,2},{3,11},{11,3},{4,12},{12,4},... | collective-permute-start | bytes 1179656 | tf_op jit(solution)/shard_map/ppermute | solution.py:52

commit v2 on v1

v2 whole, which is shorter than its diff:
```python
import functools

import jax
import jax.numpy as jnp
from jax import lax
from jax.experimental import pallas as pl
from jax.experimental.pallas import tpu as pltpu
from jax.sharding import Mesh, PartitionSpec as P

ANG = 8
TILE = ("y", "xh", "xl", "z", "c")
SWAP = [(0, 1), (1, 0)]
BF = jnp.bfloat16
F32 = jnp.float32


def sources(out):
    return [(e, (e - out) // 2 + 2) for e in range(out - 4, out + 5, 2) if e >= 0]


def conv_kernel(outs, rows, pixels, block, flip_ref, *refs):
    remotes, (w_ref, h_ref, o_ref, xp) = refs[1:-4], refs[-4:]
    x_ref = refs[0]
    flip = flip_ref[0]
    taps = w_ref.shape[0]
    used = sorted({e for o in outs for e, _ in sources(o)})
    xp[:, 0:8, :] = jnp.zeros((len(used), 8, xp.shape[2]), xp.dtype)
    xp[:, pixels + 8 :, :] = jnp.zeros((len(used), 8, xp.shape[2]), xp.dtype)
    for slot, e in enumerate(used):
        if e < rows:
            row = x_ref[e + flip * (rows - 1 - 2 * e)]
        else:
            at = (e - rows) % 2
            row = remotes[(e - rows) // 2][at + flip * (1 - 2 * at)]
        xp[slot, 8 : pixels + 8, :] = row
    for i, o in enumerate(outs):
        for m in range(0, pixels, block):
            acc = jnp.zeros((block, w_ref.shape[2]), F32)
            for e, d in sources(o):
                slot = used.index(e)
                left = jnp.concatenate(
                    [xp[slot, m + 4 + 2 * j : m + 4 + 2 * j + block, :] for j in range(taps)], axis=1
                )
                acc += jnp.dot(left, w_ref[d + flip * (4 - 2 * d)], preferred_element_type=F32)
            hidden = jax.nn.gelu(acc, approximate=True).astype(BF)
            near = lax.dot_general(
                h_ref[...], hidden, (((1,), (1,)), ((), ())), preferred_element_type=F32
            )
            o_ref[i, :, m : m + block] = near.astype(BF)


def near_rows(outs, flip, features, remotes, weights, head):
    rows, pixels, channels = features.shape
    used = sorted({e for o in outs for e, _ in sources(o)})
    flops = sum(len(sources(o)) for o in outs) * 2 * pixels * weights.shape[1] * channels
    vmem = pl.BlockSpec(memory_space=pltpu.VMEM)
    return pl.pallas_call(
        functools.partial(conv_kernel, outs, rows, pixels, 256),
        out_shape=jax.ShapeDtypeStruct((len(outs), head.shape[0], pixels), BF),
        in_specs=[pl.BlockSpec(memory_space=pltpu.SMEM)] + [vmem] * (3 + len(remotes)),
        out_specs=vmem,
        scratch_shapes=[pltpu.VMEM((len(used), pixels + 16, channels), BF)],
        compiler_params=pltpu.CompilerParams(vmem_limit_bytes=24 << 20),
        cost_estimate=pl.CostEstimate(
            flops=2 * flops, bytes_accessed=4 << 20, transcendentals=len(outs) * pixels * channels
        ),
        name="near_rows",
    )(flip, features, *remotes, weights, head)


def on_device(features, conv_weight, head_weight, kernels, source_weights):
    rows, pixels, channels = features.shape[1:]
    angle = lax.axis_index(("y", "xh"))
    section = lax.axis_index("s")
    weight = lax.dynamic_index_in_dim(source_weights, angle, 0, keepdims=False)
    window = features[0]
    edge = lax.dynamic_slice_in_dim(window, (1 - section) * (rows - 2), 2, 0)
    remote1 = lax.ppermute(edge, "s", SWAP)
    remote2 = lax.ppermute(window[2:4], "s", SWAP)
    both = jnp.concatenate([kernels, lax.ppermute(kernels, "c", SWAP)], axis=0)
    flip = section.astype(jnp.int32).reshape(1)
    taps = conv_weight.reshape(conv_weight.shape[0], -1, channels)
    head = head_weight.T
    near = jnp.concatenate(
        [
            near_rows((0, 1), flip, window, [], taps, head),
            near_rows((2, 3), flip, window, [remote1], taps, head),
            near_rows((4, 5), flip, window, [remote1, remote2], taps, head),
        ],
        axis=0,
    )
    near = near.reshape(rows, ANG, 2, pixels).transpose(1, 2, 0, 3)
    field = lax.all_to_all(near, ("y", "xh"), 0, 0, tiled=True)
    field = lax.all_gather(field, "z", axis=1, tiled=False)
    other = lax.ppermute(field, "xl", SWAP)

    def image(part):
        product = jnp.einsum(
            "azprw,kwv->pkazrv", part, both, preferred_element_type=jnp.float32
        )
        re = product[0, ..., :pixels] - product[1, ..., pixels:]
        im = product[0, ..., pixels:] + product[1, ..., :pixels]
        return weight * jnp.sum(re * re + im * im, axis=0)

    sent = lax.ppermute(image(other).astype(BF), "xl", SWAP)
    total = image(field) + sent.astype(F32)
    total = total.astype(BF).reshape(-1, rows, pixels)
    pieces = lax.all_to_all(total, ("y", "xh", "z"), 0, 0, tiled=True)
    image_rows = jnp.sum(pieces.astype(F32), axis=0, keepdims=True)
    return jnp.where(section == 0, image_rows, image_rows[:, ::-1])


def solution(mesh):
    fine = Mesh(mesh.devices.reshape(2, 4, 2, 2, 4, 2), ("s",) + TILE)
    in_specs = (P(TILE, "s", None, None), P(), P(), P(TILE, None, None), P())
    return jax.shard_map(
        on_device, mesh=fine, in_specs=in_specs, out_specs=P(TILE, "s", None), check_vma=False
    )
```

time: 152 us -> 126 us (0.83)
  blocking collectives: 57.2 us -> 37 us
  Pallas kernels: 0 us -> 14.1 us
  matrix products: 25 us -> 12 us
  local copies, waits for them, and re-layouts: 18.1 us -> 7.32 us
  starting transfers between devices: 6.4 us -> 9.25 us
  waiting for transfers between devices: 40.5 us -> 42.8 us
    all_to_all x1 -> x0, blocking collectives: 21.2 us -> none  [on_device(): pieces = lax.all_to_all(total, ('y', 'xh', 'z'), 0, 0, tiled=True)]
    all_to_all x0 -> x1, waiting for transfers between devices: none -> 15.8 us  [on_device(): pieces = lax.all_to_all(total, ('y', 'xh', 'z'), 0, 0, tiled=True)]
    pallas_call x0 -> x3, Pallas kernels: none -> 14.1 us  [near_rows(): pl.pallas_call(functools.partial(conv_kernel, outs, rows, pixels, 256), o...]
    ppermute x5, waiting for transfers between devices: 40.5 us -> 27 us  [the longest x1 14.3 us: on_device(): other = lax.ppermute(field, 'xl', SWAP)]
    conv_general_dilated x1 -> x0, matrix products: 11.1 us -> none  [on_device(): lax.conv_general_dilated(padded, conv_weight, (1, 1), ((0, 0), (4, 4)), r...]
    conv_general_dilated x3 -> x0, local copies, waits for them, and re-layouts: 9.17 us -> none  [on_device(): lax.conv_general_dilated(padded, conv_weight, (1, 1), ((0, 0), (4, 4)), r...]
    all_to_all x0 -> x1, starting transfers between devices: none -> 6.29 us  [on_device(): pieces = lax.all_to_all(total, ('y', 'xh', 'z'), 0, 0, tiled=True)]
    ppermute x5, starting transfers between devices: 6.4 us -> 2.96 us  [the longest x1 1.93 us: on_device(): remote1 = lax.ppermute(edge, 's', SWAP)]
  transfers between devices with their start and end apart: 5 -> 6, of which waited for: 4 -> 5; matrix products, arithmetic and copies ran while one was open for 25% -> 7% of each run, Pallas kernels for 0% -> 11%
where the time goes in v2:
time: 126 us
  waiting for transfers between devices  42.8 us (34%)
  blocking collectives  37 us (29%)
  Pallas kernels  14.1 us (11%)
  matrix products  12 us (10%)
  starting transfers between devices  9.25 us (7%)
  local copies, waits for them, and re-layouts  7.32 us (6%)
  other arithmetic  3.6 us (3%)
    all_gather x1, blocking collectives, on_device(): field = lax.all_gather(field, 'z', axis=1, tiled=False)  21.8 us
    all_to_all x1, waiting for transfers between devices, on_device(): pieces = lax.all_to_all(total, ('y', 'xh', 'z'), 0, 0, tiled=True)  15.8 us
    all_to_all x1, blocking collectives, on_device(): field = lax.all_to_all(near, ('y', 'xh'), 0, 0, tiled=True)  15.1 us
    ppermute x1, waiting for transfers between devices, on_device(): other = lax.ppermute(field, 'xl', SWAP)  14.3 us
    pallas_call x3, Pallas kernels, near_rows(): pl.pallas_call(functools.partial(conv_kernel, outs, rows, pixels, 256), o...  14.1 us
    dot_general x2, matrix products, image(): jnp.einsum('azprw,kwv->pkazrv', part, both, preferred_element_type=jnp.fl...  12 us
    ppermute x1, waiting for transfers between devices, on_device(): remote2 = lax.ppermute(window[2:4], 's', SWAP)  6.69 us
    all_to_all x1, starting transfers between devices, on_device(): pieces = lax.all_to_all(total, ('y', 'xh', 'z'), 0, 0, tiled=True)  6.29 us
  transfers between devices with their start and end apart: 6, of which 5 were waited for; matrix products, arithmetic and copies ran while one was open for 7% of the time, Pallas kernels for 11%

profile of v2, /device:TPU:32, one launch (start us, length us, event | category | flops | bytes accessed | tf_op | source)
XLA Modules:
  0.0 126.1 jit_solution(2722122946792584792)
XLA Ops:
  0.0 1.3 %slice_bitcast_fusion = (bf16[2,1024,128]{2,1,0:T(8,128)(2,1)S(1)}, bf16[2,1024,128]{2,1,0:T(8,128)(2,1)S(1)}) fusion(bf16[1,6,1024,128]{3,2,1,0:T(8,128)(2,1)} %param.5, s32[]{:T(128)S(6)} %select_n.20), kind=kLoop, calls=%fused_computation.21 | loop fusion | bytes 2097156 | tf_op jit(solution)/shard_map/slice | solution.py:79
  1.4 1.9 %collective-permute-start.1 = (bf16[2,1024,128]{2,1,0:T(8,128)(2,1)S(1)}, bf16[2,1024,128]{2,1,0:T(8,128)(2,1)S(1)}, u32[]{:S(2)}, u32[]{:S(2)}) collective-permute-start(bf16[2,1024,128]{2,1,0:T(8,128)(2,1)S(1)} %get-tuple-element.6), channel_id=1, source_target_pairs={{0,128},{128,0},{1,129},{129,1},{2,130},{130,2},{3,131},{131,3},{4... | collective-permute-start | bytes 1572872 | tf_op jit(solution)/shard_map/ppermute | solution.py:78
  3.3 0.2 collective-permute-start.2
  3.5 1.4 %copy-done = bf16[1,6,1024,128]{3,2,1,0:T(8,128)(2,1)S(1)} copy-done((bf16[1,6,1024,128]{3,2,1,0:T(8,128)(2,1)S(1)}, bf16[1,6,1024,128]{3,2,1,0:T(8,128)(2,1)}, u32[]{:S(2)}) %copy-start) | copy-done | bytes 1572888
  4.9 1.1 copy-done.1
  6.0 0.7 copy-done.3
  6.7 4.1 %near_rows.3 = bf16[2,16,1024]{2,1,0:T(8,128)(2,1)S(1)} custom-call(s32[1]{0:T(128)} %bitcast.3.flip_ref, bf16[6,1024,128]{2,1,0:T(8,128)(2,1)S(1)} %bitcast.34, bf16[5,640,128]{2,1,0:T(8,128)(2,1)S(1)} %bitcast.37, bf16[16,128]{1,0:T(8,128)(2,1)S(1)} %bitcast.40), custom_call_target="tpu_custom_call" | custom-call | flops 2013265920 | bytes 4194304 | tf_op jit(solution)/shard_map/near_rows/pallas_call | solution.py:57
  10.8 5.3 %collective-permute-done.1.refs_1_ = bf16[2,1024,128]{2,1,0:T(8,128)(2,1)S(1)} collective-permute-done((bf16[2,1024,128]{2,1,0:T(8,128)(2,1)S(1)}, bf16[2,1024,128]{2,1,0:T(8,128)(2,1)S(1)}, u32[]{:S(2)}, u32[]{:S(2)}) %collective-permute-start.1) | collective-permute-done | bytes 524320 | tf_op jit(solution)/shard_map/ppermute | solution.py:78
  16.2 4.3 %near_rows.4 = bf16[2,16,1024]{2,1,0:T(8,128)(2,1)S(1)} custom-call(s32[1]{0:T(128)} %bitcast.3.flip_ref, bf16[6,1024,128]{2,1,0:T(8,128)(2,1)S(1)} %bitcast.35, bf16[2,1024,128]{2,1,0:T(8,128)(2,1)S(1)} %collective-permute-done.1.refs_1_, bf16[5,640,128]{2,1,0:T(8,128)(2,1)S(1)} %bitcast.38, bf16[16,128]{1,0:T(8,128)(2,1)S(1)} %bitcast.41), custom_call_target="tpu_custom_call" | custom-call | flops 2684354560 | bytes 4194304 | tf_op jit(solution)/shard_map/near_rows/pallas_call | solution.py:57
  20.4 6.7 %collective-permute-done.2.refs_2_ = bf16[2,1024,128]{2,1,0:T(8,128)(2,1)S(1)} collective-permute-done((bf16[2,1024,128]{2,1,0:T(8,128)(2,1)S(1)}, bf16[2,1024,128]{2,1,0:T(8,128)(2,1)S(1)}, u32[]{:S(2)}, u32[]{:S(2)}) %collective-permute-start.2) | collective-permute-done | bytes 524320 | tf_op jit(solution)/shard_map/ppermute | solution.py:79
  27.1 5.7 %near_rows.5 = bf16[2,16,1024]{2,1,0:T(8,128)(2,1)S(1)} custom-call(s32[1]{0:T(128)} %bitcast.3.flip_ref, bf16[6,1024,128]{2,1,0:T(8,128)(2,1)S(1)} %bitcast.36, bf16[2,1024,128]{2,1,0:T(8,128)(2,1)S(1)} %collective-permute-done.1.refs_1_, bf16[2,1024,128]{2,1,0:T(8,128)(2,1)S(1)} %collective-permute-done.2.refs_2_, bf16[5,640,128]{2,1,0:T(8,128)(2,1)S(1)} %bitcast.39, ...), custom_call_target="tpu_custom_call" | custom-call | flops 3355443200 | bytes 4194304 | tf_op jit(solution)/shard_map/near_rows/pallas_call | solution.py:57
  32.9 0.1 reshape.28
  33.0 0.1 copy.20
  33.1 15.1 %all_to_all.10 = bf16[8,2,6,1024]{3,1,2,0:T(2,128)(2,1)S(1)} all-to-all(bf16[8,2,6,1024]{3,1,2,0:T(2,128)(2,1)S(1)} %bitcast.43), channel_id=1, replica_groups=mesh['s'=2,'y'=4,'xh'=2,'xl'=2,'z'=4,'c'=2] {'y','xh'}, dimensions={0} | all-to-all | bytes 393216 | tf_op jit(solution)/shard_map/all_to_all | solution.py:93
  48.3 21.8 %all-gather = bf16[8,8,6,1024]{3,0,2,1:T(8,128)(2,1)S(1)} all-gather(bf16[8,2,6,1024]{3,0,2,1:T(8,128)(2,1)S(1)} %copy.13), channel_id=2, replica_groups=mesh['s'=2,'y'=4,'xh'=2,'xl'=2,'z'=4,'c'=2] {'z'}, dimensions={1}, use_global_device_ids=true | all-gather | bytes 983040 | tf_op jit(solution)/shard_map/all_gather | solution.py:94
  70.1 0.4 collective-permute-start.3
  70.5 0.6 dynamic_slice.9
  71.1 14.3 %collective-permute-done.3 = bf16[8,4,2,6,1024]{4,0,3,2,1:T(8,128)(2,1)S(1)} collective-permute-done((bf16[8,4,2,6,1024]{4,0,3,2,1:T(8,128)(2,1)S(1)}, bf16[8,4,2,6,1024]{4,0,3,2,1:T(8,128)(2,1)S(1)}, u32[]{:S(2)}, u32[]{:S(2)}) %collective-permute-start.3) | collective-permute-done | bytes 786464 | tf_op jit(solution)/shard_map/ppermute | solution.py:95
  85.4 6.0 %fusion.3 = f32[2,2,8,4,6,2048]{5,2,4,0,3,1:T(8,128)S(1)} fusion(bf16[1,1024,2048]{2,1,0:T(8,128)(2,1)} %collective-permute-done, bf16[1,1024,2048]{2,1,0:T(8,128)(2,1)} %param.8, bf16[8,4,2,6,1024]{4,0,3,2,1:T(8,128)(2,1)S(1)} %collective-permute-done.3), kind=kOutput, calls=%fused_computation.4 | convolution fusion | flops 3238002688 | bytes 15466496 | tf_op jit(solution)/shard_map/azprw,kwv->pkazrv/dot_general | solution.py:98
  91.4 0.8 fusion.6
  92.3 1.1 multiply_convert_fusion
  93.3 0.4 collective-permute-start.4
  93.8 6.0 %fusion.2 = f32[2,2,8,4,6,2048]{5,2,4,0,3,1:T(8,128)S(1)} fusion(bf16[8,4,2,6,1024,1]{4,0,3,2,1,5:T(8,128)(2,1)S(1)} %bitcast.45, bf16[1,1024,2048]{2,1,0:T(8,128)(2,1)} %collective-permute-done, bf16[1,1024,2048]{2,1,0:T(8,128)(2,1)S(1)} %copy-done.5), kind=kOutput, calls=%fused_computation.3 | convolution fusion | flops 3238002688 | bytes 15466496 | tf_op jit(solution)/shard_map/azprw,kwv->pkazrv/dot_general | solution.py:98
  99.8 0.8 fusion.10
  100.6 0.6 collective-permute-done.4
  101.2 0.7 add_convert_fusion
  101.9 1.0 copy.17
  103.0 6.3 %all-to-all-start.1 = ((bf16[32,6,1024]{2,1,0:T(8,128)(2,1)}), bf16[32,6,1024]{2,1,0:T(8,128)(2,1)S(1)}, u32[]{:S(2)}, u32[]{:S(2)}) async-start(bf16[32,6,1024]{2,1,0:T(8,128)(2,1)} %bitcast.16), calls=%async_computation.1 | async-start | bytes 1048576 | tf_op jit(solution)/shard_map/all_to_all | solution.py:108
  109.3 15.8 %all-to-all-done.1 = bf16[32,6,1024]{2,1,0:T(8,128)(2,1)S(1)} async-done(((bf16[32,6,1024]{2,1,0:T(8,128)(2,1)}), bf16[32,6,1024]{2,1,0:T(8,128)(2,1)S(1)}, u32[]{:S(2)}, u32[]{:S(2)}) %all-to-all-start.1) | async-done | bytes 393248 | tf_op jit(solution)/shard_map/all_to_all | solution.py:108
  125.1 0.1 convert_reduce_fusion
  125.2 0.2 reverse.3
  125.4 0.6 select_n.22
  (16 shorter events, 0.1 us)
Async XLA Ops:
  0.0 85.4 %collective-permute-start = (bf16[1,1024,2048]{2,1,0:T(8,128)(2,1)}, bf16[1,1024,2048]{2,1,0:T(8,128)(2,1)}, u32[]{:S(2)}, u32[]{:S(2)}) collective-permute-start(bf16[1,1024,2048]{2,1,0:T(8,128)(2,1)} %param.8), channel_id=1, source_target_pairs={{0,1},{1,0},{2,3},{3,2},{4,5},{5,4},{6,7},{7,6},{8,9},{9,8},{10,11... | collective-permute-start | bytes 12582920 | tf_op jit(solution)/shard_map/ppermute | solution.py:80
  0.0 16.2 %copy-start.2 = (bf16[5,5,128,128]{3,2,1,0:T(8,128)(2,1)S(1)}, bf16[5,5,128,128]{3,2,1,0:T(8,128)(2,1)}, u32[]{:S(2)}) copy-start(bf16[5,5,128,128]{3,2,1,0:T(8,128)(2,1)} %param.6) | copy-start | bytes 2457604
  1.4 14.8 %copy-start.4 = (bf16[128,16]{0,1:T(8,128)(2,1)S(1)}, bf16[128,16]{0,1:T(8,128)(2,1)}, u32[]{:S(2)}) copy-start(bf16[128,16]{0,1:T(8,128)(2,1)} %param.7) | copy-start | bytes 12292
  1.4 14.8 %collective-permute-start.1 = (bf16[2,1024,128]{2,1,0:T(8,128)(2,1)S(1)}, bf16[2,1024,128]{2,1,0:T(8,128)(2,1)S(1)}, u32[]{:S(2)}, u32[]{:S(2)}) collective-permute-start(bf16[2,1024,128]{2,1,0:T(8,128)(2,1)S(1)} %get-tuple-element.6), channel_id=1, source_target_pairs={{0,128},{128,0},{1,129},{129,1},{2,130},{130,2},{3,131},{131,3},{4... | collective-permute-start | bytes 1572872 | tf_op jit(solution)/shard_map/ppermute | solution.py:78
  3.3 23.8 %collective-permute-start.2 = (bf16[2,1024,128]{2,1,0:T(8,128)(2,1)S(1)}, bf16[2,1024,128]{2,1,0:T(8,128)(2,1)S(1)}, u32[]{:S(2)}, u32[]{:S(2)}) collective-permute-start(bf16[2,1024,128]{2,1,0:T(8,128)(2,1)S(1)} %get-tuple-element.5), channel_id=1, source_target_pairs={{0,128},{128,0},{1,129},{129,1},{2,130},{130,2},{3,131},{131,3},{4... | collective-permute-start | bytes 1572872 | tf_op jit(solution)/shard_map/ppermute | solution.py:79
  3.5 1.4 %copy-start = (bf16[1,6,1024,128]{3,2,1,0:T(8,128)(2,1)S(1)}, bf16[1,6,1024,128]{3,2,1,0:T(8,128)(2,1)}, u32[]{:S(2)}) copy-start(bf16[1,6,1024,128]{3,2,1,0:T(8,128)(2,1)} %param.5) | copy-start | bytes 4718596
  4.9 1.1 copy-start.1
  6.0 0.7 copy-start.3
  20.4 50.1 %copy-start.6 = (f32[8]{0:T(128)S(1)}, f32[8]{0:T(128)}, u32[]{:S(2)}) copy-start(f32[8]{0:T(128)} %param.9) | copy-start | bytes 100
  70.1 15.3 %collective-permute-start.3 = (bf16[8,4,2,6,1024]{4,0,3,2,1:T(8,128)(2,1)S(1)}, bf16[8,4,2,6,1024]{4,0,3,2,1:T(8,128)(2,1)S(1)}, u32[]{:S(2)}, u32[]{:S(2)}) collective-permute-start(bf16[8,4,2,6,1024]{4,0,3,2,1:T(8,128)(2,1)S(1)} %bitcast.44), channel_id=1, source_target_pairs={{0,8},{8,0},{1,9},{9,1},{2,10},{10,2},{3,11},{11,3},{4,12},{12,4},... | collective-permute-start | bytes 2359304 | tf_op jit(solution)/shard_map/ppermute | solution.py:95
  91.4 2.4 %copy-start.5 = (bf16[1,1024,2048]{2,1,0:T(8,128)(2,1)S(1)}, bf16[1,1024,2048]{2,1,0:T(8,128)(2,1)}, u32[]{:S(2)}) copy-start(bf16[1,1024,2048]{2,1,0:T(8,128)(2,1)} %param.8) | copy-start | bytes 12582916
  93.3 7.9 %collective-permute-start.4 = (bf16[8,4,6,1024]{3,0,2,1:T(8,128)(2,1)S(1)}, bf16[8,4,6,1024]{3,0,2,1:T(8,128)(2,1)S(1)}, u32[]{:S(2)}, u32[]{:S(2)}) collective-permute-start(bf16[8,4,6,1024]{3,0,2,1:T(8,128)(2,1)S(1)} %multiply_convert_fusion), channel_id=1, source_target_pairs={{0,8},{8,0},{1,9},{9,1},{2,10},{10,2},{3,11},{11,3},{4,12},{12,4},... | collective-permute-start | bytes 1179656 | tf_op jit(solution)/shard_map/ppermute | solution.py:105
  103.0 22.1 %all-to-all-start.1 = ((bf16[32,6,1024]{2,1,0:T(8,128)(2,1)}), bf16[32,6,1024]{2,1,0:T(8,128)(2,1)S(1)}, u32[]{:S(2)}, u32[]{:S(2)}) async-start(bf16[32,6,1024]{2,1,0:T(8,128)(2,1)} %bitcast.16), calls=%async_computation.1 | async-start | bytes 1048576 | tf_op jit(solution)/shard_map/all_to_all | solution.py:108

commit v3 on v2

--- a/solution.py
+++ b/solution.py
@@ -68,46 +68,102 @@
     )(flip, features, *remotes, weights, head)
 
 
+def socs_kernel(block, weight_ref, own_ref, other_ref, first_ref, second_ref, o_ref):
+    half = own_ref.shape[1] // 2
+    pixels = own_ref.shape[2]
+    pieces = [r[k, p * half : (p + 1) * half, :] for p in (0, 1) for r in (own_ref, other_ref) for k in range(own_ref.shape[0])]
+    left = jnp.concatenate(pieces, axis=0)
+    rows = left.shape[0] // 2
+    for n in range(0, pixels, block):
+        total = jnp.zeros((rows, block), F32)
+        for g_ref in (first_ref, second_ref):
+            by_re = jnp.dot(left, g_ref[:, n : n + block], preferred_element_type=F32)
+            by_im = jnp.dot(left, g_ref[:, pixels + n : pixels + n + block], preferred_element_type=F32)
+            re = by_re[:rows] - by_im[rows:]
+            im = by_im[:rows] + by_re[rows:]
+            total += re * re + im * im
+        o_ref[:, n : n + block] = (total * weight_ref[0]).astype(BF)
+
+
+def socs_image(weight, own, other, first, second):
+    groups, lines, pixels = own.shape
+    rows = groups * lines
+    vmem = pl.BlockSpec(memory_space=pltpu.VMEM)
+    return pl.pallas_call(
+        functools.partial(socs_kernel, 256),
+        out_shape=jax.ShapeDtypeStruct((rows, pixels), BF),
+        in_specs=[pl.BlockSpec(memory_space=pltpu.SMEM)] + [vmem] * 4,
+        out_specs=vmem,
+        compiler_params=pltpu.CompilerParams(vmem_limit_bytes=24 << 20),
+        cost_estimate=pl.CostEstimate(
+            flops=16 * rows * pixels * pixels, bytes_accessed=9 << 20, transcendentals=0
+        ),
+        name="socs_image",
+    )(weight, own, other, first, second)
+
+
+def ring(count, step):
+    return [(i, (i + step) % count) for i in range(count)]
+
+
+def hold(value, *others):
+    return lax.optimization_barrier((value,) + others)[0]
+
+
+def to_angles(near):
+    pixels = near.shape[2]
+    near = near.reshape(2, ANG, 2, pixels).transpose(1, 2, 0, 3)
+    field = lax.all_to_all(near, ("y", "xh"), 0, 0, tiled=True)
+    return field.transpose(1, 2, 0, 3).reshape(4 * ANG, pixels)
+
+
+def along_z(field):
+    count = lax.axis_size("z")
+    return jnp.stack([field] + [lax.ppermute(field, "z", ring(count, k)) for k in range(1, count)])
+
+
 def on_device(features, conv_weight, head_weight, kernels, source_weights):
     rows, pixels, channels = features.shape[1:]
     angle = lax.axis_index(("y", "xh"))
     section = lax.axis_index("s")
-    weight = lax.dynamic_index_in_dim(source_weights, angle, 0, keepdims=False)
+    weight = lax.dynamic_slice_in_dim(source_weights, angle, 1, 0)
     window = features[0]
     edge = lax.dynamic_slice_in_dim(window, (1 - section) * (rows - 2), 2, 0)
     remote1 = lax.ppermute(edge, "s", SWAP)
     remote2 = lax.ppermute(window[2:4], "s", SWAP)
-    both = jnp.concatenate([kernels, lax.ppermute(kernels, "c", SWAP)], axis=0)
+    mine = kernels[0]
+    sibling = lax.ppermute(mine, "c", SWAP)
     flip = section.astype(jnp.int32).reshape(1)
     taps = conv_weight.reshape(conv_weight.shape[0], -1, channels)
     head = head_weight.T
-    near = jnp.concatenate(
-        [
-            near_rows((0, 1), flip, window, [], taps, head),
-            near_rows((2, 3), flip, window, [remote1], taps, head),
-            near_rows((4, 5), flip, window, [remote1, remote2], taps, head),
-        ],
-        axis=0,
-    )
-    near = near.reshape(rows, ANG, 2, pixels).transpose(1, 2, 0, 3)
-    field = lax.all_to_all(near, ("y", "xh"), 0, 0, tiled=True)
-    field = lax.all_gather(field, "z", axis=1, tiled=False)
-    other = lax.ppermute(field, "xl", SWAP)
-
-    def image(part):
-        product = jnp.einsum(
-            "azprw,kwv->pkazrv", part, both, preferred_element_type=jnp.float32
-        )
-        re = product[0, ..., :pixels] - product[1, ..., pixels:]
-        im = product[0, ..., pixels:] + product[1, ..., :pixels]
-        return weight * jnp.sum(re * re + im * im, axis=0)
-
-    sent = lax.ppermute(image(other).astype(BF), "xl", SWAP)
-    total = image(field) + sent.astype(F32)
-    total = total.astype(BF).reshape(-1, rows, pixels)
-    pieces = lax.all_to_all(total, ("y", "xh", "z"), 0, 0, tiled=True)
-    image_rows = jnp.sum(pieces.astype(F32), axis=0, keepdims=True)
-    return jnp.where(section == 0, image_rows, image_rows[:, ::-1])
+    near_a = near_rows((0, 1), flip, window, [], taps, head)
+    field_a = to_angles(near_a)
+    own_a = along_z(field_a)
+    remote1 = hold(remote1, field_a, sibling)
+    near_b = near_rows((2, 3), flip, window, [remote1], taps, head)
+    field_b = to_angles(near_b)
+    own_b = along_z(field_b)
+    other_a = lax.ppermute(own_a, "xl", SWAP)
+    remote2 = hold(remote2, field_b, own_a)
+    near_c = near_rows((4, 5), flip, window, [remote1, remote2], taps, head)
+    near_c = hold(near_c, own_b, other_a)
+    other_b = lax.ppermute(own_b, "xl", SWAP)
+    field_c = hold(to_angles(near_c), other_b)
+    own_c = along_z(field_c)
+    other_c = lax.ppermute(own_c, "xl", SWAP)
+    fields = [(own_a, other_a), (own_b, other_b), (own_c, other_c)]
+    images = [socs_image(weight, own, other, mine, sibling) for own, other in fields]
+    count = lax.axis_size("z")
+    image = jnp.stack(images).reshape(rows // 2, 2, count, 2, ANG, pixels)
+    image = image.transpose(4, 1, 2, 0, 3, 5)
+    image = jnp.where(lax.axis_index("xl") == 0, image, image[:, ::-1])
+    image = image.reshape(2 * ANG, count * rows, pixels)
+    pieces = lax.all_to_all(image, ("y", "xh", "xl"), 0, 0, tiled=True)
+    parts = jnp.sum(pieces.astype(F32), axis=0).reshape(count, rows, pixels)
+    total = parts[0]
+    for k in range(1, count):
+        total = total + lax.ppermute(parts[k], "z", ring(count, count - k))
+    return jnp.where(section == 0, total, total[::-1])[None]
 
 
 def solution(mesh):

time: 126 us -> 138 us (1.095)
  waiting for transfers between devices: 42.8 us -> 16.3 us
  starting transfers between devices: 9.25 us -> 31.1 us
  Pallas kernels: 14.1 us -> 30 us
  blocking collectives: 37 us -> 50.4 us
  matrix products: 12 us -> 0 us
  other arithmetic: 3.6 us -> 2.2 us
    all_to_all x1 -> x4, blocking collectives: 15.1 us -> 50.4 us  [the longest x3 35.7 us: to_angles(): field = lax.all_to_all(near, ('y', 'xh'), 0, 0, tiled=True)]
    ppermute x3 -> x16, starting transfers between devices: 0.84 us -> 29 us  [the longest x9 20.9 us: along_z(): lax.ppermute(field, 'z', ring(count, k))]
    all_gather x1 -> x0, blocking collectives: 21.8 us -> none  [on_device(): field = lax.all_gather(field, 'z', axis=1, tiled=False)]
    pallas_call x0 -> x3, Pallas kernels: none -> 16.1 us  [socs_image(): pl.pallas_call(functools.partial(socs_kernel, 256), out_shape=jax.ShapeDt...]
    all_to_all x1 -> x0, waiting for transfers between devices: 15.8 us -> none  [on_device(): pieces = lax.all_to_all(total, ('y', 'xh', 'z'), 0, 0, tiled=True)]
    dot_general x2 -> x0, matrix products: 12 us -> none  [image(): jnp.einsum('azprw,kwv->pkazrv', part, both, preferred_element_type=jnp.fl...]
    ppermute x1, waiting for transfers between devices: 6.69 us -> 0.01 us  [on_device(): remote2 = lax.ppermute(window[2:4], 's', SWAP)]
    all_to_all x1 -> x0, starting transfers between devices: 6.29 us -> none  [on_device(): pieces = lax.all_to_all(total, ('y', 'xh', 'z'), 0, 0, tiled=True)]
  transfers between devices with their start and end apart: 6 -> 18, of which waited for: 5 -> 6; matrix products, arithmetic and copies ran while one was open for 7% -> 2% of each run, Pallas kernels for 11% -> 18%
where the time goes in v3:
time: 138 us
  blocking collectives  50.4 us (37%)
  starting transfers between devices  31.1 us (23%)
  Pallas kernels  30 us (22%)
  waiting for transfers between devices  16.3 us (12%)
  local copies, waits for them, and re-layouts  7.61 us (6%)
  other arithmetic  2.2 us (2%)
    all_to_all x3, blocking collectives, to_angles(): field = lax.all_to_all(near, ('y', 'xh'), 0, 0, tiled=True)  35.7 us
    ppermute x9, starting transfers between devices, along_z(): lax.ppermute(field, 'z', ring(count, k))  20.9 us
    pallas_call x3, Pallas kernels, socs_image(): pl.pallas_call(functools.partial(socs_kernel, 256), out_shape=jax.ShapeDt...  16.1 us
    all_to_all x1, blocking collectives, on_device(): pieces = lax.all_to_all(image, ('y', 'xh', 'xl'), 0, 0, tiled=True)  14.7 us
    pallas_call x3, Pallas kernels, near_rows(): pl.pallas_call(functools.partial(conv_kernel, outs, rows, pixels, 256), o...  13.9 us
    ppermute x9, waiting for transfers between devices, along_z(): lax.ppermute(field, 'z', ring(count, k))  11.1 us
    ppermute x3, starting transfers between devices, on_device(): total = total + lax.ppermute(parts[k], 'z', ring(count, count - k))  5.58 us
    ppermute x3, waiting for transfers between devices, on_device(): total = total + lax.ppermute(parts[k], 'z', ring(count, count - k))  5.24 us
  transfers between devices with their start and end apart: 18, of which 6 were waited for; matrix products, arithmetic and copies ran while one was open for 2% of the time, Pallas kernels for 18%

profile of v3, /device:TPU:32, one launch (start us, length us, event | category | flops | bytes accessed | tf_op | source)
XLA Modules:
  0.0 137.9 jit_solution(758037578377881657)
XLA Ops:
  0.0 1.4 %slice_bitcast_fusion = (bf16[2,1024,128]{2,1,0:T(8,128)(2,1)S(1)}, bf16[2,1024,128]{2,1,0:T(8,128)(2,1)S(1)}) fusion(bf16[1,6,1024,128]{3,2,1,0:T(8,128)(2,1)} %param.5, s32[]{:T(128)S(6)} %select_n.25), kind=kLoop, calls=%fused_computation.3 | loop fusion | bytes 2097156 | tf_op jit(solution)/shard_map/slice | solution.py:133
  1.4 1.9 %collective-permute-start.5 = (bf16[2,1024,128]{2,1,0:T(8,128)(2,1)S(1)}, bf16[2,1024,128]{2,1,0:T(8,128)(2,1)S(1)}, u32[]{:S(2)}, u32[]{:S(2)}) collective-permute-start(bf16[2,1024,128]{2,1,0:T(8,128)(2,1)S(1)} %get-tuple-element.14), channel_id=1, source_target_pairs={{0,128},{128,0},{1,129},{129,1},{2,130},{130,2},{3,131},{131,3},{4... | collective-permute-start | bytes 1572872 | tf_op jit(solution)/shard_map/ppermute | solution.py:132
  3.5 1.1 copy-done.3
  4.7 4.1 %near_rows.3 = bf16[2,16,1024]{2,1,0:T(8,128)(2,1)S(1)} custom-call(s32[1]{0:T(128)} %bitcast.flip_ref, bf16[6,1024,128]{2,1,0:T(8,128)(2,1)S(1)} %bitcast.48, bf16[5,640,128]{2,1,0:T(8,128)(2,1)S(1)} %bitcast.51, bf16[16,128]{1,0:T(8,128)(2,1)S(1)} %bitcast.54), custom_call_target="tpu_custom_call" | custom-call | flops 2013265920 | bytes 4194304 | tf_op jit(solution)/shard_map/near_rows/pallas_call | solution.py:57
  8.9 14.6 %all_to_all.20 = bf16[8,2,2,1024]{3,2,1,0:T(2,128)(2,1)S(1)} all-to-all(bf16[8,2,2,1024]{3,2,1,0:T(2,128)(2,1)S(1)} %bitcast.57), channel_id=1, replica_groups=mesh['s'=2,'y'=4,'xh'=2,'xl'=2,'z'=4,'c'=2] {'y','xh'}, dimensions={0} | all-to-all | bytes 131072 | tf_op jit(solution)/shard_map/all_to_all | solution.py:116
  23.5 5.5 %collective-permute-start.2 = (bf16[32,1024]{1,0:T(8,128)(2,1)S(1)}, bf16[32,1024]{1,0:T(8,128)(2,1)S(1)}, u32[]{:S(2)}, u32[]{:S(2)}) collective-permute-start(bf16[32,1024]{1,0:T(8,128)(2,1)S(1)} %bitcast.67), channel_id=1, source_target_pairs={{0,6},{2,0},{4,2},{6,4},{1,7},{3,1},{5,3},{7,5},{8,14},{10,8},{12,... | collective-permute-start | bytes 196616 | tf_op jit(solution)/shard_map/ppermute | solution.py:122
  29.0 1.4 %collective-permute-start.1 = (bf16[32,1024]{1,0:T(8,128)(2,1)S(1)}, bf16[32,1024]{1,0:T(8,128)(2,1)S(1)}, u32[]{:S(2)}, u32[]{:S(2)}) collective-permute-start(bf16[32,1024]{1,0:T(8,128)(2,1)S(1)} %bitcast.68), channel_id=1, source_target_pairs={{0,4},{2,6},{4,0},{6,2},{1,5},{3,7},{5,1},{7,3},{8,12},{10,14},{12... | collective-permute-start | bytes 196616 | tf_op jit(solution)/shard_map/ppermute | solution.py:122
  30.4 2.4 %collective-permute-start = (bf16[32,1024]{1,0:T(8,128)(2,1)S(1)}, bf16[32,1024]{1,0:T(8,128)(2,1)S(1)}, u32[]{:S(2)}, u32[]{:S(2)}) collective-permute-start(bf16[32,1024]{1,0:T(8,128)(2,1)S(1)} %bitcast.69), channel_id=1, source_target_pairs={{0,2},{2,4},{4,6},{6,0},{1,3},{3,5},{5,7},{7,1},{8,10},{10,12},{12... | collective-permute-start | bytes 196616 | tf_op jit(solution)/shard_map/ppermute | solution.py:122
  32.8 4.3 %near_rows.4 = bf16[2,16,1024]{2,1,0:T(8,128)(2,1)S(1)} custom-call(s32[1]{0:T(128)} %bitcast.flip_ref, bf16[6,1024,128]{2,1,0:T(8,128)(2,1)S(1)} %bitcast.49, bf16[2,1024,128]{2,1,0:T(8,128)(2,1)S(1)} %collective-permute-done.5.refs_1_, bf16[5,640,128]{2,1,0:T(8,128)(2,1)S(1)} %bitcast.52, bf16[16,128]{1,0:T(8,128)(2,1)S(1)} %bitcast.55), custom_call_target="tpu_custom_call" | custom-call | flops 2684354560 | bytes 4194304 | tf_op jit(solution)/shard_map/near_rows/pallas_call | solution.py:57
  37.2 10.3 %all_to_all.21 = bf16[8,2,2,1024]{3,2,1,0:T(2,128)(2,1)S(1)} all-to-all(bf16[8,2,2,1024]{3,2,1,0:T(2,128)(2,1)S(1)} %bitcast.59), channel_id=1, replica_groups=mesh['s'=2,'y'=4,'xh'=2,'xl'=2,'z'=4,'c'=2] {'y','xh'}, dimensions={0} | all-to-all | bytes 131072 | tf_op jit(solution)/shard_map/all_to_all | solution.py:116
  47.4 2.0 %collective-permute-start.8 = (bf16[32,1024]{1,0:T(8,128)(2,1)S(1)}, bf16[32,1024]{1,0:T(8,128)(2,1)S(1)}, u32[]{:S(2)}, u32[]{:S(2)}) collective-permute-start(bf16[32,1024]{1,0:T(8,128)(2,1)S(1)} %bitcast.71), channel_id=1, source_target_pairs={{0,6},{2,0},{4,2},{6,4},{1,7},{3,1},{5,3},{7,5},{8,14},{10,8},{12,... | collective-permute-start | bytes 196616 | tf_op jit(solution)/shard_map/ppermute | solution.py:122
  49.5 4.5 %collective-permute-start.7 = (bf16[32,1024]{1,0:T(8,128)(2,1)S(1)}, bf16[32,1024]{1,0:T(8,128)(2,1)S(1)}, u32[]{:S(2)}, u32[]{:S(2)}) collective-permute-start(bf16[32,1024]{1,0:T(8,128)(2,1)S(1)} %bitcast.72), channel_id=1, source_target_pairs={{0,4},{2,6},{4,0},{6,2},{1,5},{3,7},{5,1},{7,3},{8,12},{10,14},{12... | collective-permute-start | bytes 196616 | tf_op jit(solution)/shard_map/ppermute | solution.py:122
  54.7 3.6 %collective-permute-done.7 = bf16[32,1024]{1,0:T(8,128)(2,1)S(1)} collective-permute-done((bf16[32,1024]{1,0:T(8,128)(2,1)S(1)}, bf16[32,1024]{1,0:T(8,128)(2,1)S(1)}, u32[]{:S(2)}, u32[]{:S(2)}) %collective-permute-start.7) | collective-permute-done | bytes 65568 | tf_op jit(solution)/shard_map/ppermute | solution.py:122
  58.3 2.7 %collective-permute-done.6 = bf16[32,1024]{1,0:T(8,128)(2,1)S(1)} collective-permute-done((bf16[32,1024]{1,0:T(8,128)(2,1)S(1)}, bf16[32,1024]{1,0:T(8,128)(2,1)S(1)}, u32[]{:S(2)}, u32[]{:S(2)}) %collective-permute-start.6) | collective-permute-done | bytes 65568 | tf_op jit(solution)/shard_map/ppermute | solution.py:122
  61.8 5.5 %near_rows.5 = bf16[2,16,1024]{2,1,0:T(8,128)(2,1)S(1)} custom-call(s32[1]{0:T(128)} %bitcast.flip_ref, bf16[6,1024,128]{2,1,0:T(8,128)(2,1)S(1)} %bitcast.50, bf16[2,1024,128]{2,1,0:T(8,128)(2,1)S(1)} %collective-permute-done.5.refs_1_, bf16[2,1024,128]{2,1,0:T(8,128)(2,1)S(1)} %collective-permute-done.10.refs_2_, bf16[5,640,128]{2,1,0:T(8,128)(2,1)S(1)} %bitcast.53, ...), custom_call_target="tpu_custom_call" | custom-call | flops 3355443200 | bytes 4194304 | tf_op jit(solution)/shard_map/near_rows/pallas_call | solution.py:57
  67.4 10.9 %all_to_all.22 = bf16[8,2,2,1024]{3,2,1,0:T(2,128)(2,1)S(1)} all-to-all(bf16[8,2,2,1024]{3,2,1,0:T(2,128)(2,1)S(1)} %bitcast.61), channel_id=1, replica_groups=mesh['s'=2,'y'=4,'xh'=2,'xl'=2,'z'=4,'c'=2] {'y','xh'}, dimensions={0} | all-to-all | bytes 131072 | tf_op jit(solution)/shard_map/all_to_all | solution.py:116
  78.4 3.8 %collective-permute-start.12 = (bf16[32,1024]{1,0:T(8,128)(2,1)S(1)}, bf16[32,1024]{1,0:T(8,128)(2,1)S(1)}, u32[]{:S(2)}, u32[]{:S(2)}) collective-permute-start(bf16[32,1024]{1,0:T(8,128)(2,1)S(1)} %bitcast.64), channel_id=1, source_target_pairs={{0,4},{2,6},{4,0},{6,2},{1,5},{3,7},{5,1},{7,3},{8,12},{10,14},{12... | collective-permute-start | bytes 196616 | tf_op jit(solution)/shard_map/ppermute | solution.py:122
  82.2 1.3 collective-permute-start.11
  84.0 2.6 %collective-permute-done.12 = bf16[32,1024]{1,0:T(8,128)(2,1)S(1)} collective-permute-done((bf16[32,1024]{1,0:T(8,128)(2,1)S(1)}, bf16[32,1024]{1,0:T(8,128)(2,1)S(1)}, u32[]{:S(2)}, u32[]{:S(2)}) %collective-permute-start.12) | collective-permute-done | bytes 65568 | tf_op jit(solution)/shard_map/ppermute | solution.py:122
  86.7 2.1 %collective-permute-done.11 = bf16[32,1024]{1,0:T(8,128)(2,1)S(1)} collective-permute-done((bf16[32,1024]{1,0:T(8,128)(2,1)S(1)}, bf16[32,1024]{1,0:T(8,128)(2,1)S(1)}, u32[]{:S(2)}, u32[]{:S(2)}) %collective-permute-start.11) | collective-permute-done | bytes 65568 | tf_op jit(solution)/shard_map/ppermute | solution.py:122
  88.8 1.1 collective-permute-start.14
  89.9 2.2 %copy-done = bf16[1,1024,2048]{2,1,0:T(8,128)(2,1)S(1)} copy-done((bf16[1,1024,2048]{2,1,0:T(8,128)(2,1)S(1)}, bf16[1,1024,2048]{2,1,0:T(8,128)(2,1)}, u32[]{:S(2)}) %copy-start) | copy-done | bytes 4194328
  92.1 5.3 %socs_image.3 = bf16[128,1024]{1,0:T(8,128)(2,1)S(1)} custom-call(f32[1]{0:T(128)} %dynamic_slice.8.weight_ref, bf16[4,32,1024]{2,1,0:T(8,128)(2,1)S(1)} %pad_maximum_fusion.own_ref, bf16[4,32,1024]{2,1,0:T(8,128)(2,1)S(1)} %collective-permute-done.3.other_ref, bf16[1024,2048]{1,0:T(8,128)(2,1)S(1)} %bitcast.42, ...), custom_call_target="tpu_custom_call" | custom-call | flops 2147483648 | bytes 9437184 | tf_op jit(solution)/shard_map/socs_image/pallas_call | solution.py:92
  97.6 5.6 %socs_image.4 = bf16[128,1024]{1,0:T(8,128)(2,1)S(1)} custom-call(f32[1]{0:T(128)} %dynamic_slice.8.weight_ref, bf16[4,32,1024]{2,1,0:T(8,128)(2,1)S(1)} %pad_maximum_fusion.1.own_ref, bf16[4,32,1024]{2,1,0:T(8,128)(2,1)S(1)} %collective-permute-done.9.other_ref, bf16[1024,2048]{1,0:T(8,128)(2,1)S(1)} %bitcast.43, ...), custom_call_target="tpu_custom_call" | custom-call | flops 2147483648 | bytes 9437184 | tf_op jit(solution)/shard_map/socs_image/pallas_call | solution.py:92
  103.5 5.3 %socs_image.5 = bf16[128,1024]{1,0:T(8,128)(2,1)S(1)} custom-call(f32[1]{0:T(128)} %dynamic_slice.8.weight_ref, bf16[4,32,1024]{2,1,0:T(8,128)(2,1)S(1)} %pad_maximum_fusion.2.own_ref, bf16[4,32,1024]{2,1,0:T(8,128)(2,1)S(1)} %collective-permute-done.14.other_ref, bf16[1024,2048]{1,0:T(8,128)(2,1)S(1)} %bitcast.44, ...), custom_call_target="tpu_custom_call" | custom-call | flops 2147483648 | bytes 9437184 | tf_op jit(solution)/shard_map/socs_image/pallas_call | solution.py:92
  109.1 1.1 maximum_bitcast_fusion
  111.3 14.7 %all_to_all.23 = bf16[16,24,1024]{2,1,0:T(8,128)(2,1)S(1)} all-to-all(bf16[16,24,1024]{2,1,0:T(8,128)(2,1)S(1)} %reshape.53), channel_id=1, replica_groups=mesh['s'=2,'y'=4,'xh'=2,'xl'=2,'z'=4,'c'=2] {'y','xh','xl'}, dimensions={0} | all-to-all | bytes 1572864 | tf_op jit(solution)/shard_map/all_to_all | solution.py:161
  126.2 1.9 %collective-permute-start.15 = (f32[6,1024]{1,0:T(8,128)S(1)}, f32[6,1024]{1,0:T(8,128)S(1)}, u32[]{:S(2)}, u32[]{:S(2)}) collective-permute-start(f32[6,1024]{1,0:T(8,128)S(1)} %get-tuple-element.15), channel_id=1, source_target_pairs={{0,6},{2,0},{4,2},{6,4},{1,7},{3,1},{5,3},{7,5},{8,14},{10,8},{12,... | collective-permute-start | bytes 73736 | tf_op jit(solution)/shard_map/ppermute | solution.py:165
  128.1 1.1 collective-permute-start.17
  129.2 2.6 %collective-permute-start.16 = (f32[6,1024]{1,0:T(8,128)S(1)}, f32[6,1024]{1,0:T(8,128)S(1)}, u32[]{:S(2)}, u32[]{:S(2)}) collective-permute-start(f32[6,1024]{1,0:T(8,128)S(1)} %get-tuple-element.17), channel_id=1, source_target_pairs={{0,4},{2,6},{4,0},{6,2},{1,5},{3,7},{5,1},{7,3},{8,12},{10,14},{12... | collective-permute-start | bytes 73736 | tf_op jit(solution)/shard_map/ppermute | solution.py:165
  131.7 2.4 %collective-permute-done.17 = f32[6,1024]{1,0:T(8,128)S(1)} collective-permute-done((f32[6,1024]{1,0:T(8,128)S(1)}, f32[6,1024]{1,0:T(8,128)S(1)}, u32[]{:S(2)}, u32[]{:S(2)}) %collective-permute-start.17) | collective-permute-done | bytes 24608 | tf_op jit(solution)/shard_map/ppermute | solution.py:165
  134.1 2.8 %collective-permute-done.16 = f32[6,1024]{1,0:T(8,128)S(1)} collective-permute-done((f32[6,1024]{1,0:T(8,128)S(1)}, f32[6,1024]{1,0:T(8,128)S(1)}, u32[]{:S(2)}, u32[]{:S(2)}) %collective-permute-start.16) | collective-permute-done | bytes 24608 | tf_op jit(solution)/shard_map/ppermute | solution.py:165
  (49 shorter events, 5.7 us)
Async XLA Ops:
  0.0 3.5 %copy-start.2 = (bf16[1,6,1024,128]{3,2,1,0:T(8,128)(2,1)S(1)}, bf16[1,6,1024,128]{3,2,1,0:T(8,128)(2,1)}, u32[]{:S(2)}) copy-start(bf16[1,6,1024,128]{3,2,1,0:T(8,128)(2,1)} %param.5) | copy-start | bytes 4718596
  0.0 3.5 %copy-start.4 = (bf16[128,16]{0,1:T(8,128)(2,1)S(1)}, bf16[128,16]{0,1:T(8,128)(2,1)}, u32[]{:S(2)}) copy-start(bf16[128,16]{0,1:T(8,128)(2,1)} %param.7) | copy-start | bytes 12292
  0.0 32.8 %collective-permute-start.4 = (bf16[1024,2048]{1,0:T(8,128)(2,1)}, bf16[1024,2048]{1,0:T(8,128)(2,1)}, u32[]{:S(2)}, u32[]{:S(2)}) collective-permute-start(bf16[1024,2048]{1,0:T(8,128)(2,1)} %bitcast.41), channel_id=1, source_target_pairs={{0,1},{1,0},{2,3},{3,2},{4,5},{5,4},{6,7},{7,6},{8,9},{9,8},{10,11... | collective-permute-start | bytes 12582920 | tf_op jit(solution)/shard_map/ppermute | solution.py:135
  1.4 29.0 %collective-permute-start.5 = (bf16[2,1024,128]{2,1,0:T(8,128)(2,1)S(1)}, bf16[2,1024,128]{2,1,0:T(8,128)(2,1)S(1)}, u32[]{:S(2)}, u32[]{:S(2)}) collective-permute-start(bf16[2,1024,128]{2,1,0:T(8,128)(2,1)S(1)} %get-tuple-element.14), channel_id=1, source_target_pairs={{0,128},{128,0},{1,129},{129,1},{2,130},{130,2},{3,131},{131,3},{4... | collective-permute-start | bytes 1572872 | tf_op jit(solution)/shard_map/ppermute | solution.py:132
  3.4 51.4 %collective-permute-start.10 = (bf16[2,1024,128]{2,1,0:T(8,128)(2,1)S(1)}, bf16[2,1024,128]{2,1,0:T(8,128)(2,1)S(1)}, u32[]{:S(2)}, u32[]{:S(2)}) collective-permute-start(bf16[2,1024,128]{2,1,0:T(8,128)(2,1)S(1)} %get-tuple-element.13), channel_id=1, source_target_pairs={{0,128},{128,0},{1,129},{129,1},{2,130},{130,2},{3,131},{131,3},{4... | collective-permute-start | bytes 1572872 | tf_op jit(solution)/shard_map/ppermute | solution.py:133
  3.5 1.1 copy-start.3
  23.5 26.0 %collective-permute-start.2 = (bf16[32,1024]{1,0:T(8,128)(2,1)S(1)}, bf16[32,1024]{1,0:T(8,128)(2,1)S(1)}, u32[]{:S(2)}, u32[]{:S(2)}) collective-permute-start(bf16[32,1024]{1,0:T(8,128)(2,1)S(1)} %bitcast.67), channel_id=1, source_target_pairs={{0,6},{2,0},{4,2},{6,4},{1,7},{3,1},{5,3},{7,5},{8,14},{10,8},{12,... | collective-permute-start | bytes 196616 | tf_op jit(solution)/shard_map/ppermute | solution.py:122
  29.0 25.0 %collective-permute-start.1 = (bf16[32,1024]{1,0:T(8,128)(2,1)S(1)}, bf16[32,1024]{1,0:T(8,128)(2,1)S(1)}, u32[]{:S(2)}, u32[]{:S(2)}) collective-permute-start(bf16[32,1024]{1,0:T(8,128)(2,1)S(1)} %bitcast.68), channel_id=1, source_target_pairs={{0,4},{2,6},{4,0},{6,2},{1,5},{3,7},{5,1},{7,3},{8,12},{10,14},{12... | collective-permute-start | bytes 196616 | tf_op jit(solution)/shard_map/ppermute | solution.py:122
  30.4 23.6 %collective-permute-start = (bf16[32,1024]{1,0:T(8,128)(2,1)S(1)}, bf16[32,1024]{1,0:T(8,128)(2,1)S(1)}, u32[]{:S(2)}, u32[]{:S(2)}) collective-permute-start(bf16[32,1024]{1,0:T(8,128)(2,1)S(1)} %bitcast.69), channel_id=1, source_target_pairs={{0,2},{2,4},{4,6},{6,0},{1,3},{3,5},{5,7},{7,1},{8,10},{10,12},{12... | collective-permute-start | bytes 196616 | tf_op jit(solution)/shard_map/ppermute | solution.py:122
  47.4 7.3 %collective-permute-start.8 = (bf16[32,1024]{1,0:T(8,128)(2,1)S(1)}, bf16[32,1024]{1,0:T(8,128)(2,1)S(1)}, u32[]{:S(2)}, u32[]{:S(2)}) collective-permute-start(bf16[32,1024]{1,0:T(8,128)(2,1)S(1)} %bitcast.71), channel_id=1, source_target_pairs={{0,6},{2,0},{4,2},{6,4},{1,7},{3,1},{5,3},{7,5},{8,14},{10,8},{12,... | collective-permute-start | bytes 196616 | tf_op jit(solution)/shard_map/ppermute | solution.py:122
  49.5 8.9 %collective-permute-start.7 = (bf16[32,1024]{1,0:T(8,128)(2,1)S(1)}, bf16[32,1024]{1,0:T(8,128)(2,1)S(1)}, u32[]{:S(2)}, u32[]{:S(2)}) collective-permute-start(bf16[32,1024]{1,0:T(8,128)(2,1)S(1)} %bitcast.72), channel_id=1, source_target_pairs={{0,4},{2,6},{4,0},{6,2},{1,5},{3,7},{5,1},{7,3},{8,12},{10,14},{12... | collective-permute-start | bytes 196616 | tf_op jit(solution)/shard_map/ppermute | solution.py:122
  54.0 7.1 %collective-permute-start.6 = (bf16[32,1024]{1,0:T(8,128)(2,1)S(1)}, bf16[32,1024]{1,0:T(8,128)(2,1)S(1)}, u32[]{:S(2)}, u32[]{:S(2)}) collective-permute-start(bf16[32,1024]{1,0:T(8,128)(2,1)S(1)} %bitcast.73), channel_id=1, source_target_pairs={{0,2},{2,4},{4,6},{6,0},{1,3},{3,5},{5,7},{7,1},{8,10},{10,12},{12... | collective-permute-start | bytes 196616 | tf_op jit(solution)/shard_map/ppermute | solution.py:122
  54.0 13.3 %collective-permute-start.3 = (bf16[4,32,1024]{2,1,0:T(8,128)(2,1)S(1)}, bf16[4,32,1024]{2,1,0:T(8,128)(2,1)S(1)}, u32[]{:S(2)}, u32[]{:S(2)}) collective-permute-start(bf16[4,32,1024]{2,1,0:T(8,128)(2,1)S(1)} %pad_maximum_fusion.own_ref), channel_id=1, source_target_pairs={{0,8},{8,0},{1,9},{9,1},{2,10},{10,2},{3,11},{11,3},{4,12},{12,4},... | collective-permute-start | bytes 786440 | tf_op jit(solution)/shard_map/ppermute | solution.py:146
  61.1 22.4 %copy-start.5 = (f32[8]{0:T(128)S(1)}, f32[8]{0:T(128)}, u32[]{:S(2)}) copy-start(f32[8]{0:T(128)} %param.9) | copy-start | bytes 100
  61.1 17.2 %collective-permute-start.9 = (bf16[4,32,1024]{2,1,0:T(8,128)(2,1)S(1)}, bf16[4,32,1024]{2,1,0:T(8,128)(2,1)S(1)}, u32[]{:S(2)}, u32[]{:S(2)}) collective-permute-start(bf16[4,32,1024]{2,1,0:T(8,128)(2,1)S(1)} %pad_maximum_fusion.1.own_ref), channel_id=1, source_target_pairs={{0,8},{8,0},{1,9},{9,1},{2,10},{10,2},{3,11},{11,3},{4,12},{12,4},... | collective-permute-start | bytes 786440 | tf_op jit(solution)/shard_map/ppermute | solution.py:150
  78.3 5.7 %collective-permute-start.13 = (bf16[32,1024]{1,0:T(8,128)(2,1)S(1)}, bf16[32,1024]{1,0:T(8,128)(2,1)S(1)}, u32[]{:S(2)}, u32[]{:S(2)}) collective-permute-start(bf16[32,1024]{1,0:T(8,128)(2,1)S(1)} %bitcast.63), channel_id=1, source_target_pairs={{0,6},{2,0},{4,2},{6,4},{1,7},{3,1},{5,3},{7,5},{8,14},{10,8},{12,... | collective-permute-start | bytes 196616 | tf_op jit(solution)/shard_map/ppermute | solution.py:122
  78.4 8.3 %collective-permute-start.12 = (bf16[32,1024]{1,0:T(8,128)(2,1)S(1)}, bf16[32,1024]{1,0:T(8,128)(2,1)S(1)}, u32[]{:S(2)}, u32[]{:S(2)}) collective-permute-start(bf16[32,1024]{1,0:T(8,128)(2,1)S(1)} %bitcast.64), channel_id=1, source_target_pairs={{0,4},{2,6},{4,0},{6,2},{1,5},{3,7},{5,1},{7,3},{8,12},{10,14},{12... | collective-permute-start | bytes 196616 | tf_op jit(solution)/shard_map/ppermute | solution.py:122
  82.2 6.6 %collective-permute-start.11 = (bf16[32,1024]{1,0:T(8,128)(2,1)S(1)}, bf16[32,1024]{1,0:T(8,128)(2,1)S(1)}, u32[]{:S(2)}, u32[]{:S(2)}) collective-permute-start(bf16[32,1024]{1,0:T(8,128)(2,1)S(1)} %bitcast.65), channel_id=1, source_target_pairs={{0,2},{2,4},{4,6},{6,0},{1,3},{3,5},{5,7},{7,1},{8,10},{10,12},{12... | collective-permute-start | bytes 196616 | tf_op jit(solution)/shard_map/ppermute | solution.py:122
  88.8 14.7 %collective-permute-start.14 = (bf16[4,32,1024]{2,1,0:T(8,128)(2,1)S(1)}, bf16[4,32,1024]{2,1,0:T(8,128)(2,1)S(1)}, u32[]{:S(2)}, u32[]{:S(2)}) collective-permute-start(bf16[4,32,1024]{2,1,0:T(8,128)(2,1)S(1)} %pad_maximum_fusion.2.own_ref), channel_id=1, source_target_pairs={{0,8},{8,0},{1,9},{9,1},{2,10},{10,2},{3,11},{11,3},{4,12},{12,4},... | collective-permute-start | bytes 786440 | tf_op jit(solution)/shard_map/ppermute | solution.py:153
  89.9 2.2 %copy-start = (bf16[1,1024,2048]{2,1,0:T(8,128)(2,1)S(1)}, bf16[1,1024,2048]{2,1,0:T(8,128)(2,1)}, u32[]{:S(2)}) copy-start(bf16[1,1024,2048]{2,1,0:T(8,128)(2,1)} %param.8) | copy-start | bytes 12582916
  97.6 5.9 %copy-start.1 = (bf16[1,1024,2048]{2,1,0:T(8,128)(2,1)S(1)}, bf16[1,1024,2048]{2,1,0:T(8,128)(2,1)}, u32[]{:S(2)}) copy-start(bf16[1,1024,2048]{2,1,0:T(8,128)(2,1)} %param.8) | copy-start | bytes 12582916
  126.2 5.6 %collective-permute-start.15 = (f32[6,1024]{1,0:T(8,128)S(1)}, f32[6,1024]{1,0:T(8,128)S(1)}, u32[]{:S(2)}, u32[]{:S(2)}) collective-permute-start(f32[6,1024]{1,0:T(8,128)S(1)} %get-tuple-element.15), channel_id=1, source_target_pairs={{0,6},{2,0},{4,2},{6,4},{1,7},{3,1},{5,3},{7,5},{8,14},{10,8},{12,... | collective-permute-start | bytes 73736 | tf_op jit(solution)/shard_map/ppermute | solution.py:165
  128.1 6.1 %collective-permute-start.17 = (f32[6,1024]{1,0:T(8,128)S(1)}, f32[6,1024]{1,0:T(8,128)S(1)}, u32[]{:S(2)}, u32[]{:S(2)}) collective-permute-start(f32[6,1024]{1,0:T(8,128)S(1)} %get-tuple-element.16), channel_id=1, source_target_pairs={{0,2},{2,4},{4,6},{6,0},{1,3},{3,5},{5,7},{7,1},{8,10},{10,12},{12... | collective-permute-start | bytes 73736 | tf_op jit(solution)/shard_map/ppermute | solution.py:165
  129.2 7.8 %collective-permute-start.16 = (f32[6,1024]{1,0:T(8,128)S(1)}, f32[6,1024]{1,0:T(8,128)S(1)}, u32[]{:S(2)}, u32[]{:S(2)}) collective-permute-start(f32[6,1024]{1,0:T(8,128)S(1)} %get-tuple-element.17), channel_id=1, source_target_pairs={{0,4},{2,6},{4,0},{6,2},{1,5},{3,7},{5,1},{7,3},{8,12},{10,14},{12... | collective-permute-start | bytes 73736 | tf_op jit(solution)/shard_map/ppermute | solution.py:165

commit v4 on v1

v4 whole, which is shorter than its diff:
```python
import functools

import jax
import jax.numpy as jnp
from jax import lax
from jax.experimental import pallas as pl
from jax.experimental.pallas import tpu as pltpu
from jax.sharding import Mesh, PartitionSpec as P

ANG = 8
TILE = ("y", "xh", "xl", "z", "c")
SWAP = [(0, 1), (1, 0)]
BF = jnp.bfloat16
F32 = jnp.float32
LINES = 6
OWN = 3
STAGES = (((0, 1, 2), (0,)), ((3, 4), (1, 2)), ((5,), (3, 4, 5)))


def touched(lines):
    return [o for o in range(LINES) if any(abs(i - o) <= 2 for i in lines)]


def conv_kernel(lines, done, before, pixels, block, flip_ref, *refs):
    x_ref, w_ref, h_ref = refs[:3]
    held = refs[3] if before else None
    outputs = refs[4 if before else 3 :]
    near_ref, xp = outputs[0], outputs[-1]
    later = [o for o in touched(lines) if o not in done]
    flip = flip_ref[0]
    taps = w_ref.shape[0]
    for slot, i in enumerate(lines):
        if i < OWN:
            row = x_ref[2 * i + flip * (LINES - 1 - 4 * i)]
        else:
            at = i - lines[0]
            row = x_ref[at + flip * (len(lines) - 1 - 2 * at)]
        xp[slot, 0:8, :] = jnp.zeros((8, xp.shape[2]), xp.dtype)
        xp[slot, pixels + 8 :, :] = jnp.zeros((8, xp.shape[2]), xp.dtype)
        xp[slot, 8 : pixels + 8, :] = row
    for m in range(0, pixels, block):
        lefts = [
            jnp.concatenate(
                [xp[slot, m + 4 + 2 * j : m + 4 + 2 * j + block, :] for j in range(taps)], axis=1
            )
            for slot in range(len(lines))
        ]
        for o in touched(lines):
            acc = held[before.index(o), m : m + block, :] if o in before else None
            for slot, i in enumerate(lines):
                d = i - o + 2
                if 0 <= d <= 4:
                    part = jnp.dot(
                        lefts[slot], w_ref[d + flip * (4 - 2 * d)], preferred_element_type=F32
                    )
                    acc = part if acc is None else acc + part
            if o in done:
                hidden = jax.nn.gelu(acc, approximate=True).astype(BF)
                near = lax.dot_general(
                    h_ref[...], hidden, (((1,), (1,)), ((), ())), preferred_element_type=F32
                )
                near_ref[done.index(o), :, m : m + block] = near.astype(BF)
            else:
                outputs[1][later.index(o), m : m + block, :] = acc


def conv_stage(stage, flip, rows, weights, head, held):
    lines, done = STAGES[stage]
    pixels, channels = rows.shape[1:]
    before = [o for o in touched(STAGES[stage - 1][0]) if o not in STAGES[stage - 1][1]] if stage else []
    later = [o for o in touched(lines) if o not in done]
    out_shape = [jax.ShapeDtypeStruct((len(done), head.shape[0], pixels), BF)]
    if later:
        out_shape.append(jax.ShapeDtypeStruct((len(later), pixels, channels), F32))
    terms = sum(abs(i - o) <= 2 for i in lines for o in range(LINES))
    vmem = pl.BlockSpec(memory_space=pltpu.VMEM)
    out = pl.pallas_call(
        functools.partial(conv_kernel, lines, done, before, pixels, 256),
        out_shape=out_shape,
        in_specs=[pl.BlockSpec(memory_space=pltpu.SMEM)] + [vmem] * (3 + len(held)),
        out_specs=[vmem] * len(out_shape),
        scratch_shapes=[pltpu.VMEM((len(lines), pixels + 16, channels), BF)],
        compiler_params=pltpu.CompilerParams(vmem_limit_bytes=24 << 20),
        cost_estimate=pl.CostEstimate(
            flops=4 * terms * pixels * weights.shape[1] * channels,
            bytes_accessed=4 << 20,
            transcendentals=len(done) * pixels * channels,
        ),
        name="conv_stage",
    )(flip, rows, weights, head, *held)
    return out[0], list(out[1:])


def socs_kernel(block, weight_ref, left_ref, first_ref, second_ref, o_ref):
    rows, pixels = o_ref.shape
    left = left_ref[...]
    for n in range(0, pixels, block):
        total = jnp.zeros((rows, block), F32)
        for g_ref in (first_ref, second_ref):
            by_re = jnp.dot(left, g_ref[:, n : n + block], preferred_element_type=F32)
            by_im = jnp.dot(left, g_ref[:, pixels + n : pixels + n + block], preferred_element_type=F32)
            re = by_re[:rows] - by_im[rows:]
            im = by_im[:rows] + by_re[rows:]
            total += re * re + im * im
        o_ref[:, n : n + block] = (total * weight_ref[0]).astype(BF)


def socs_image(weight, field, first, second):
    rows, pixels = field.shape[0] // 2, field.shape[1]
    vmem = pl.BlockSpec(memory_space=pltpu.VMEM)
    return pl.pallas_call(
        functools.partial(socs_kernel, 256),
        out_shape=jax.ShapeDtypeStruct((rows, pixels), BF),
        in_specs=[pl.BlockSpec(memory_space=pltpu.SMEM)] + [vmem] * 3,
        out_specs=vmem,
        compiler_params=pltpu.CompilerParams(vmem_limit_bytes=32 << 20),
        cost_estimate=pl.CostEstimate(
            flops=16 * rows * pixels * pixels, bytes_accessed=9 << 20, transcendentals=0
        ),
        name="socs_image",
    )(weight, field, first, second)


def on_device(features, conv_weight, head_weight, kernels, source_weights):
    rows, pixels, channels = features.shape[1:]
    angle = lax.axis_index(("y", "xh"))
    section = lax.axis_index("s")
    depth = lax.axis_size("z")
    weight = lax.dynamic_slice_in_dim(source_weights, angle, 1, 0)
    window = features[0]
    pairs = window.reshape(rows // 2, 2, pixels, channels)

    def halo(start, count):
        block = lax.dynamic_slice(pairs, (start, 1 - section, 0, 0), (count, 1, pixels, channels))
        return lax.ppermute(block[:, 0], "s", SWAP)

    first = halo(1 - section, 2)
    last = halo(2 * section, 1)
    mine = kernels[0]
    sibling = lax.ppermute(mine, "c", SWAP)
    flip = section.astype(jnp.int32).reshape(1)
    taps = conv_weight.reshape(conv_weight.shape[0], -1, channels)
    head = head_weight.T
    near, held = [], []
    for stage, read in enumerate((window, first, last)):
        done, held = conv_stage(stage, flip, read, taps, head, held)
        near.append(done)
    near = jnp.concatenate(near, axis=0).reshape(LINES, ANG, 2, pixels).transpose(1, 2, 0, 3)
    near = jnp.broadcast_to(near[:, None], (ANG, depth, 2, LINES, pixels))
    near = near.reshape(ANG * depth, 2, LINES, pixels)
    field = lax.all_to_all(near, ("y", "xh", "z"), 0, 0, tiled=True)
    field = field.transpose(1, 2, 0, 3).reshape(-1, pixels)
    other = lax.ppermute(field, "xl", SWAP)

    def image(part):
        part = socs_image(weight, part, mine, sibling)
        return part.reshape(LINES, ANG, depth, pixels).transpose(1, 2, 0, 3)

    own, other = image(field), image(other)
    low = lax.axis_index("xl") == 0
    images = jnp.stack([jnp.where(low, own, other), jnp.where(low, other, own)], axis=1)
    images = images.reshape(2 * ANG, depth * LINES, pixels)
    pieces = lax.all_to_all(images, ("y", "xh", "xl"), 0, 0, tiled=True)
    total = jnp.sum(pieces.astype(F32), axis=0).reshape(depth, 2, OWN, pixels)
    kept, given = total[:, 0], total[:, 1]
    stays = section == 0
    total = jnp.stack([jnp.where(stays, kept, given), jnp.where(stays, given, kept)])
    total = total.reshape(2 * depth, OWN * pixels // 128, 128)
    total = lax.all_to_all(total, ("s", "z"), 0, 0, tiled=True)
    even, odd = jnp.sum(total.reshape(2, depth, OWN, pixels), axis=1)
    return jnp.stack([even, odd[::-1]], axis=1).reshape(1, LINES, pixels)


def solution(mesh):
    fine = Mesh(mesh.devices.reshape(2, 4, 2, 2, 4, 2), ("s",) + TILE)
    in_specs = (P(TILE, "s", None, None), P(), P(), P(TILE, None, None), P())
    return jax.shard_map(
        on_device, mesh=fine, in_specs=in_specs, out_specs=P(TILE, "s", None), check_vma=False
    )
```

time: 152 us -> 120 us (0.79)
  Pallas kernels: 0 us -> 26.1 us
  matrix products: 25 us -> 0 us
  waiting for transfers between devices: 40.5 us -> 24.3 us
  local copies, waits for them, and re-layouts: 18.1 us -> 10.3 us
  blocking collectives: 57.2 us -> 49.8 us
  other arithmetic: 4.05 us -> 0.43 us
  starting transfers between devices: 6.4 us -> 8.23 us
    ppermute x5 -> x4, waiting for transfers between devices: 40.5 us -> 12.8 us  [the longest x1 7.1 us: on_device(): other = lax.ppermute(field, 'xl', SWAP)]
    pallas_call x0 -> x5, Pallas kernels: none -> 26.1 us  [the longest x3 13.5 us: conv_stage(): pl.pallas_call(functools.partial(conv_kernel, lines, done, before, pixels...]
    all_gather x1 -> x0, blocking collectives: 22.6 us -> none  [on_device(): field = lax.all_gather(field, 'z', axis=1, tiled=False)]
    all_to_all x2, blocking collectives: 34.6 us -> 49.8 us  [the longest x1 36.5 us: on_device(): field = lax.all_to_all(near, ('y', 'xh', 'z'), 0, 0, tiled=True)]
    dot_general x3 -> x0, matrix products: 13.9 us -> none  [the longest x2 12 us: image(): jnp.einsum('azprw,kwv->pkazrv', part, both, preferred_element_type=jnp.fl...]
    all_to_all x0 -> x1, waiting for transfers between devices: none -> 11.5 us  [on_device(): pieces = lax.all_to_all(images, ('y', 'xh', 'xl'), 0, 0, tiled=True)]
    conv_general_dilated x1 -> x0, matrix products: 11.1 us -> none  [on_device(): lax.conv_general_dilated(padded, conv_weight, (1, 1), ((0, 0), (4, 4)), r...]
    conv_general_dilated x3 -> x0, local copies, waits for them, and re-layouts: 9.17 us -> none  [on_device(): lax.conv_general_dilated(padded, conv_weight, (1, 1), ((0, 0), (4, 4)), r...]
  transfers between devices with their start and end apart: 5 -> 5, of which waited for: 4 -> 4; matrix products, arithmetic and copies ran while one was open for 25% -> 3% of each run, Pallas kernels for 0% -> 17%
where the time goes in v4:
time: 120 us; the launch traced here: 119 us
  blocking collectives  49.8 us (42%)
  Pallas kernels  26.1 us (22%)
  waiting for transfers between devices  24.3 us (20%)
  local copies, waits for them, and re-layouts  10.3 us (9%)
  starting transfers between devices  8.23 us (7%)
    all_to_all x1, blocking collectives, on_device(): field = lax.all_to_all(near, ('y', 'xh', 'z'), 0, 0, tiled=True)  36.5 us
    pallas_call x3, Pallas kernels, conv_stage(): pl.pallas_call(functools.partial(conv_kernel, lines, done, before, pixels...  13.5 us
    all_to_all x1, blocking collectives, on_device(): total = lax.all_to_all(total, ('s', 'z'), 0, 0, tiled=True)  13.3 us
    pallas_call x2, Pallas kernels, socs_image(): pl.pallas_call(functools.partial(socs_kernel, 256), out_shape=jax.ShapeDt...  12.7 us
    all_to_all x1, waiting for transfers between devices, on_device(): pieces = lax.all_to_all(images, ('y', 'xh', 'xl'), 0, 0, tiled=True)  11.5 us
    ppermute x1, waiting for transfers between devices, on_device(): other = lax.ppermute(field, 'xl', SWAP)  7.1 us
    ppermute x2, waiting for transfers between devices, halo(): return lax.ppermute(block[:, 0], 's', SWAP)  5.67 us
    all_to_all x1, starting transfers between devices, on_device(): pieces = lax.all_to_all(images, ('y', 'xh', 'xl'), 0, 0, tiled=True)  5.34 us
  transfers between devices with their start and end apart: 5, of which 4 were waited for; matrix products, arithmetic and copies ran while one was open for 3% of the time, Pallas kernels for 17%

profile of v4, /device:TPU:32, one launch (start us, length us, event | category | flops | bytes accessed | tf_op | source)
XLA Modules:
  0.0 119.5 jit_solution(13912302173207154182)
XLA Ops:
  0.0 1.2 %dynamic-slice_bitcast_fusion = bf16[2,1024,128]{2,1,0:T(8,128)(2,1)S(1)} fusion(bf16[3,2,1024,128]{3,2,1,0:T(8,128)(2,1)} %bitcast.42, s32[]{:T(128)S(6)} %select_n.72, s32[]{:T(128)S(6)} %select_n.73), kind=kLoop, calls=%fused_computation.2 | loop fusion | bytes 1048584 | tf_op jit(solution)/shard_map/squeeze | solution.py:135
  1.2 1.9 %collective-permute-start = (bf16[2,1024,128]{2,1,0:T(8,128)(2,1)S(1)}, bf16[2,1024,128]{2,1,0:T(8,128)(2,1)S(1)}, u32[]{:S(2)}, u32[]{:S(2)}) collective-permute-start(bf16[2,1024,128]{2,1,0:T(8,128)(2,1)S(1)} %dynamic-slice_bitcast_fusion), channel_id=1, source_target_pairs={{0,128},{128,0},{1,129},{129,1},{2,130},{130,2},{3,131},{131,3},{4... | collective-permute-start | bytes 1572872 | tf_op jit(solution)/shard_map/ppermute | solution.py:135
  3.2 1.0 dynamic-slice_bitcast_fusion.1
  4.1 0.3 collective-permute-start.1
  4.4 1.1 copy-done.2
  5.6 5.3 %conv_stage.3 = (bf16[1,16,1024]{2,1,0:T(8,128)(2,1)S(1)}, f32[4,1024,128]{2,1,0:T(8,128)S(1)}) custom-call(s32[1]{0:T(128)} %bitcast.flip_ref, bf16[6,1024,128]{2,1,0:T(8,128)(2,1)S(1)} %bitcast.44, bf16[5,640,128]{2,1,0:T(8,128)(2,1)S(1)} %bitcast.48, bf16[16,128]{1,0:T(8,128)(2,1)S(1)} %bitcast.51), custom_call_target="tpu_custom_call" | custom-call | flops 4026531840 | bytes 4194304 | tf_op jit(solution)/shard_map/conv_stage/pallas_call | solution.py:77
  10.8 5.2 %collective-permute-done.refs_0_ = bf16[2,1024,128]{2,1,0:T(8,128)(2,1)S(1)} collective-permute-done((bf16[2,1024,128]{2,1,0:T(8,128)(2,1)S(1)}, bf16[2,1024,128]{2,1,0:T(8,128)(2,1)S(1)}, u32[]{:S(2)}, u32[]{:S(2)}) %collective-permute-start) | collective-permute-done | bytes 524320 | tf_op jit(solution)/shard_map/ppermute | solution.py:135
  16.1 4.7 %conv_stage.4 = (bf16[2,16,1024]{2,1,0:T(8,128)(2,1)S(1)}, f32[3,1024,128]{2,1,0:T(8,128)S(1)}) custom-call(s32[1]{0:T(128)} %bitcast.flip_ref, bf16[2,1024,128]{2,1,0:T(8,128)(2,1)S(1)} %collective-permute-done.refs_0_, bf16[5,640,128]{2,1,0:T(8,128)(2,1)S(1)} %bitcast.49, bf16[16,128]{1,0:T(8,128)(2,1)S(1)} %bitcast.52, ...), custom_call_target="tpu_custom_call" | custom-call | flops 3019898880 | bytes 4194304 | tf_op jit(solution)/shard_map/conv_stage/pallas_call | solution.py:77
  20.8 0.5 collective-permute-done.1.refs_0_
  21.2 3.5 %conv_stage.5 = bf16[3,16,1024]{2,1,0:T(8,128)(2,1)S(1)} custom-call(s32[1]{0:T(128)} %bitcast.flip_ref, bf16[1,1024,128]{2,1,0:T(8,128)(2,1)S(1)} %collective-permute-done.1.refs_0_, bf16[5,640,128]{2,1,0:T(8,128)(2,1)S(1)} %bitcast.50, bf16[16,128]{1,0:T(8,128)(2,1)S(1)} %bitcast.53, f32[3,1024,128]{2,1,0:T(8,128)S(1)} %get-tuple-element.12.refs_3_), custom_call_target="tpu_custom_call" | custom-call | flops 1006632960 | bytes 4194304 | tf_op jit(solution)/shard_map/conv_stage/pallas_call | solution.py:77
  24.8 0.1 reshape.77
  24.8 0.3 copy.39
  25.2 0.5 broadcast_in_dim.2
  25.7 36.5 %all_to_all.15 = bf16[32,2,6,1024]{3,1,2,0:T(2,128)(2,1)S(1)} all-to-all(bf16[32,2,6,1024]{3,1,2,0:T(2,128)(2,1)S(1)} %bitcast.55), channel_id=1, replica_groups=mesh['s'=2,'y'=4,'xh'=2,'xl'=2,'z'=4,'c'=2] {'y','xh','z'}, dimensions={0} | all-to-all | bytes 1572864 | tf_op jit(solution)/shard_map/all_to_all | solution.py:151
  62.2 0.2 copy.40
  62.4 0.7 collective-permute-start.3
  63.1 0.6 dynamic_slice.9.weight_ref
  63.7 2.2 %copy-done.1 = bf16[1,1024,2048]{2,1,0:T(8,128)(2,1)S(1)} copy-done((bf16[1,1024,2048]{2,1,0:T(8,128)(2,1)S(1)}, bf16[1,1024,2048]{2,1,0:T(8,128)(2,1)}, u32[]{:S(2)}) %copy-start.1) | copy-done | bytes 4194328
  65.9 6.3 %socs_image.2 = bf16[192,1024]{1,0:T(8,128)(2,1)S(1)} custom-call(f32[1]{0:T(128)} %dynamic_slice.9.weight_ref, bf16[384,1024]{1,0:T(8,128)(2,1)S(1)} %bitcast.41, bf16[1024,2048]{1,0:T(8,128)(2,1)S(1)} %bitcast.46, bf16[1024,2048]{1,0:T(8,128)(2,1)} %collective-permute-done.2.second_ref), custom_call_target="tpu_custom_call" | custom-call | flops 3221225472 | bytes 9437184 | tf_op jit(solution)/shard_map/socs_image/pallas_call | solution.py:111
  72.2 7.1 %collective-permute-done.3.left_ref = bf16[384,1024]{1,0:T(8,128)(2,1)S(1)} collective-permute-done((bf16[384,1024]{1,0:T(8,128)(2,1)S(1)}, bf16[384,1024]{1,0:T(8,128)(2,1)S(1)}, u32[]{:S(2)}, u32[]{:S(2)}) %collective-permute-start.3) | collective-permute-done | bytes 786464 | tf_op jit(solution)/shard_map/ppermute | solution.py:153
  79.3 6.3 %socs_image.3 = bf16[192,1024]{1,0:T(8,128)(2,1)S(1)} custom-call(f32[1]{0:T(128)} %dynamic_slice.9.weight_ref, bf16[384,1024]{1,0:T(8,128)(2,1)S(1)} %collective-permute-done.3.left_ref, bf16[1024,2048]{1,0:T(8,128)(2,1)S(1)} %bitcast.47, bf16[1024,2048]{1,0:T(8,128)(2,1)} %collective-permute-done.2.second_ref), custom_call_target="tpu_custom_call" | custom-call | flops 3221225472 | bytes 9437184 | tf_op jit(solution)/shard_map/socs_image/pallas_call | solution.py:111
  85.7 0.1 select_n.76
  85.9 0.1 select_n.79
  86.0 0.2 copy_bitcast_fusion
  86.3 0.4 copy.50
  86.8 1.1 reshape.85
  87.9 5.3 %all-to-all-start.1 = ((bf16[16,24,1024]{2,1,0:T(8,128)(2,1)}), bf16[16,24,1024]{2,1,0:T(8,128)(2,1)S(1)}, u32[]{:S(2)}, u32[]{:S(2)}) async-start(bf16[16,24,1024]{2,1,0:T(8,128)(2,1)} %reshape.85), calls=%async_computation.1 | async-start | bytes 1572864 | tf_op jit(solution)/shard_map/all_to_all | solution.py:163
  93.3 11.5 %all-to-all-done.1 = bf16[16,24,1024]{2,1,0:T(8,128)(2,1)S(1)} async-done(((bf16[16,24,1024]{2,1,0:T(8,128)(2,1)}), bf16[16,24,1024]{2,1,0:T(8,128)(2,1)S(1)}, u32[]{:S(2)}, u32[]{:S(2)}) %all-to-all-start.1) | async-done | bytes 786464 | tf_op jit(solution)/shard_map/all_to_all | solution.py:163
  104.8 0.1 convert_reduce_fusion
  105.1 13.3 %all_to_all.16 = f32[8,24,128]{2,1,0:T(8,128)S(1)} all-to-all(f32[8,24,128]{2,1,0:T(8,128)S(1)} %reshape.82), channel_id=1, replica_groups=mesh['s'=2,'y'=4,'xh'=2,'xl'=2,'z'=4,'c'=2] {'s','z'}, dimensions={0} | all-to-all | bytes 196608 | tf_op jit(solution)/shard_map/all_to_all | solution.py:169
  118.5 0.2 rev.3
  118.8 0.6 reshape.84
  (24 shorter events, 0.5 us)
Async XLA Ops:
  0.0 4.4 %copy-start = (bf16[1,6,1024,128]{3,2,1,0:T(8,128)(2,1)S(1)}, bf16[1,6,1024,128]{3,2,1,0:T(8,128)(2,1)}, u32[]{:S(2)}) copy-start(bf16[1,6,1024,128]{3,2,1,0:T(8,128)(2,1)} %param.5) | copy-start | bytes 4718596
  0.0 4.4 %copy-start.3 = (bf16[128,16]{0,1:T(8,128)(2,1)S(1)}, bf16[128,16]{0,1:T(8,128)(2,1)}, u32[]{:S(2)}) copy-start(bf16[128,16]{0,1:T(8,128)(2,1)} %param.7) | copy-start | bytes 12292
  0.0 63.7 %collective-permute-start.2 = (bf16[1024,2048]{1,0:T(8,128)(2,1)}, bf16[1024,2048]{1,0:T(8,128)(2,1)}, u32[]{:S(2)}, u32[]{:S(2)}) collective-permute-start(bf16[1024,2048]{1,0:T(8,128)(2,1)} %bitcast.45), channel_id=1, source_target_pairs={{0,1},{1,0},{2,3},{3,2},{4,5},{5,4},{6,7},{7,6},{8,9},{9,8},{10,11... | collective-permute-start | bytes 12582920 | tf_op jit(solution)/shard_map/ppermute | solution.py:140
  1.2 14.8 %collective-permute-start = (bf16[2,1024,128]{2,1,0:T(8,128)(2,1)S(1)}, bf16[2,1024,128]{2,1,0:T(8,128)(2,1)S(1)}, u32[]{:S(2)}, u32[]{:S(2)}) collective-permute-start(bf16[2,1024,128]{2,1,0:T(8,128)(2,1)S(1)} %dynamic-slice_bitcast_fusion), channel_id=1, source_target_pairs={{0,128},{128,0},{1,129},{129,1},{2,130},{130,2},{3,131},{131,3},{4... | collective-permute-start | bytes 1572872 | tf_op jit(solution)/shard_map/ppermute | solution.py:135
  4.1 17.1 %collective-permute-start.1 = (bf16[1,1024,128]{2,1,0:T(8,128)(2,1)S(1)}, bf16[1,1024,128]{2,1,0:T(8,128)(2,1)S(1)}, u32[]{:S(2)}, u32[]{:S(2)}) collective-permute-start(bf16[1,1024,128]{2,1,0:T(8,128)(2,1)S(1)} %dynamic-slice_bitcast_fusion.1), channel_id=1, source_target_pairs={{0,128},{128,0},{1,129},{129,1},{2,130},{130,2},{3,131},{131,3},{4... | collective-permute-start | bytes 786440 | tf_op jit(solution)/shard_map/ppermute | solution.py:135
  4.4 1.1 copy-start.2
  25.6 37.5 %copy-start.4 = (f32[8]{0:T(128)S(1)}, f32[8]{0:T(128)}, u32[]{:S(2)}) copy-start(f32[8]{0:T(128)} %param.9) | copy-start | bytes 100
  62.4 16.9 %collective-permute-start.3 = (bf16[384,1024]{1,0:T(8,128)(2,1)S(1)}, bf16[384,1024]{1,0:T(8,128)(2,1)S(1)}, u32[]{:S(2)}, u32[]{:S(2)}) collective-permute-start(bf16[384,1024]{1,0:T(8,128)(2,1)S(1)} %bitcast.40), channel_id=1, source_target_pairs={{0,8},{8,0},{1,9},{9,1},{2,10},{10,2},{3,11},{11,3},{4,12},{12,4},... | collective-permute-start | bytes 2359304 | tf_op jit(solution)/shard_map/ppermute | solution.py:153
  63.7 2.2 %copy-start.1 = (bf16[1,1024,2048]{2,1,0:T(8,128)(2,1)S(1)}, bf16[1,1024,2048]{2,1,0:T(8,128)(2,1)}, u32[]{:S(2)}) copy-start(bf16[1,1024,2048]{2,1,0:T(8,128)(2,1)} %param.8) | copy-start | bytes 12582916
  87.9 16.8 %all-to-all-start.1 = ((bf16[16,24,1024]{2,1,0:T(8,128)(2,1)}), bf16[16,24,1024]{2,1,0:T(8,128)(2,1)S(1)}, u32[]{:S(2)}, u32[]{:S(2)}) async-start(bf16[16,24,1024]{2,1,0:T(8,128)(2,1)} %reshape.85), calls=%async_computation.1 | async-start | bytes 1572864 | tf_op jit(solution)/shard_map/all_to_all | solution.py:163

commit v5 on v4

--- a/solution.py
+++ b/solution.py
@@ -2,6 +2,7 @@
 
 import jax
 import jax.numpy as jnp
+import numpy as np
 from jax import lax
 from jax.experimental import pallas as pl
 from jax.experimental.pallas import tpu as pltpu
@@ -91,34 +92,58 @@
     return out[0], list(out[1:])
 
 
-def socs_kernel(block, weight_ref, left_ref, first_ref, second_ref, o_ref):
-    rows, pixels = o_ref.shape
+def socs_kernel(weight_ref, low_ref, order_ref, left_ref, *refs):
+    re1, im1, re2, im2 = refs[:4]
+    o_ref = refs[-1]
+    rows = left_ref.shape[0] // 2
     left = left_ref[...]
-    for n in range(0, pixels, block):
-        total = jnp.zeros((rows, block), F32)
-        for g_ref in (first_ref, second_ref):
-            by_re = jnp.dot(left, g_ref[:, n : n + block], preferred_element_type=F32)
-            by_im = jnp.dot(left, g_ref[:, pixels + n : pixels + n + block], preferred_element_type=F32)
-            re = by_re[:rows] - by_im[rows:]
-            im = by_im[:rows] + by_re[rows:]
-            total += re * re + im * im
-        o_ref[:, n : n + block] = (total * weight_ref[0]).astype(BF)
-
-
-def socs_image(weight, field, first, second):
+    total = jnp.zeros((rows, re1.shape[1]), F32)
+    for re_ref, im_ref in ((re1, im1), (re2, im2)):
+        by_re = jnp.dot(left, re_ref[...], preferred_element_type=F32)
+        by_im = jnp.dot(left, im_ref[...], preferred_element_type=F32)
+        re = by_re[:rows] - by_im[rows:]
+        im = by_im[:rows] + by_re[rows:]
+        total += re * re + im * im
+    total = jnp.dot(order_ref[...], (total * weight_ref[0]).astype(BF), preferred_element_type=F32)
+    if len(refs) == 5:
+        o_ref[...] = total
+        return
+    low = low_ref[0]
+    step = rows // ANG
+    for g in range(ANG):
+        o_ref[g, low] = refs[4][g * step : (g + 1) * step, :].astype(BF)
+        o_ref[g, 1 - low] = total[g * step : (g + 1) * step].astype(BF)
+
+
+def socs_image(weight, low, order, field, first, second, own=()):
     rows, pixels = field.shape[0] // 2, field.shape[1]
-    vmem = pl.BlockSpec(memory_space=pltpu.VMEM)
+    block = 256
+    steps = pixels // block
+    scalar = pl.BlockSpec(memory_space=pltpu.SMEM)
+
+    def whole(array):
+        return pl.BlockSpec(array.shape, lambda n: (0, 0))
+
+    re = pl.BlockSpec((pixels, block), lambda n: (0, n))
+    im = pl.BlockSpec((pixels, block), lambda n: (0, n + steps))
+    image = pl.BlockSpec((rows, block), lambda n: (0, n))
+    if own:
+        out_shape = jax.ShapeDtypeStruct((ANG, 2, rows // ANG, pixels), BF)
+        out_spec = pl.BlockSpec((ANG, 2, rows // ANG, block), lambda n: (0, 0, 0, n))
+    else:
+        out_shape, out_spec = jax.ShapeDtypeStruct((rows, pixels), F32), image
     return pl.pallas_call(
-        functools.partial(socs_kernel, 256),
-        out_shape=jax.ShapeDtypeStruct((rows, pixels), BF),
-        in_specs=[pl.BlockSpec(memory_space=pltpu.SMEM)] + [vmem] * 3,
-        out_specs=vmem,
-        compiler_params=pltpu.CompilerParams(vmem_limit_bytes=32 << 20),
+        socs_kernel,
+        grid=(steps,),
+        out_shape=out_shape,
+        in_specs=[scalar, scalar, whole(order), whole(field), re, im, re, im] + [image] * len(own),
+        out_specs=out_spec,
+        compiler_params=pltpu.CompilerParams(vmem_limit_bytes=24 << 20),
         cost_estimate=pl.CostEstimate(
             flops=16 * rows * pixels * pixels, bytes_accessed=9 << 20, transcendentals=0
         ),
         name="socs_image",
-    )(weight, field, first, second)
+    )(weight, low, order, field, first, first, second, second, *own)
 
 
 def on_device(features, conv_weight, head_weight, kernels, source_weights):
@@ -137,7 +162,7 @@
     first = halo(1 - section, 2)
     last = halo(2 * section, 1)
     mine = kernels[0]
-    sibling = lax.ppermute(mine, "c", SWAP)
+    sibling = lax.ppermute(lax.optimization_barrier((mine, first))[0], "c", SWAP)
     flip = section.astype(jnp.int32).reshape(1)
     taps = conv_weight.reshape(conv_weight.shape[0], -1, channels)
     head = head_weight.T
@@ -152,13 +177,12 @@
     field = field.transpose(1, 2, 0, 3).reshape(-1, pixels)
     other = lax.ppermute(field, "xl", SWAP)
 
-    def image(part):
-        part = socs_image(weight, part, mine, sibling)
-        return part.reshape(LINES, ANG, depth, pixels).transpose(1, 2, 0, 3)
-
-    own, other = image(field), image(other)
-    low = lax.axis_index("xl") == 0
-    images = jnp.stack([jnp.where(low, own, other), jnp.where(low, other, own)], axis=1)
+    low = lax.axis_index("xl").astype(jnp.int32).reshape(1)
+    sources = ANG * depth
+    order = np.eye(LINES * sources).reshape(LINES, sources, -1).transpose(1, 0, 2)
+    order = jnp.asarray(order.reshape(LINES * sources, -1), BF)
+    own = socs_image(weight, low, order, field, mine, sibling)
+    images = socs_image(weight, low, order, other, mine, sibling, (own,))
     images = images.reshape(2 * ANG, depth * LINES, pixels)
     pieces = lax.all_to_all(images, ("y", "xh", "xl"), 0, 0, tiled=True)
     total = jnp.sum(pieces.astype(F32), axis=0).reshape(depth, 2, OWN, pixels)

time: 120 us -> 128 us (1.067)
  waiting for transfers between devices: 24.3 us -> 31.1 us
  local copies, waits for them, and re-layouts: 10.3 us -> 8.24 us
  Pallas kernels: 26.1 us -> 28.1 us
  blocking collectives: 49.8 us -> 51.2 us
    ppermute x2, waiting for transfers between devices: 5.67 us -> 11.8 us  [halo(): return lax.ppermute(block[:, 0], 's', SWAP)]
    pallas_call x2, Pallas kernels: 12.7 us -> 14.8 us  [socs_image(): pl.pallas_call(socs_kernel, grid=(steps,), out_shape=out_shape, in_specs=...]
    reshape x2 -> x0, local copies, waits for them, and re-layouts: 1.58 us -> none  [on_device(): images = images.reshape(2 * ANG, depth * LINES, pixels)]
    all_to_all x1, blocking collectives: 36.5 us -> 37.8 us  [on_device(): field = lax.all_to_all(near, ('y', 'xh', 'z'), 0, 0, tiled=True)]
    unnamed x10 -> x14, local copies, waits for them, and re-layouts: 3.35 us -> 3.36 us
  transfers between devices with their start and end apart: 5 -> 5, of which waited for: 4 -> 3; matrix products, arithmetic and copies ran while one was open for 3% -> 2% of each run, Pallas kernels for 17% -> 16%
where the time goes in v5:
time: 128 us; the launch traced here: 127 us
  blocking collectives  51.2 us (40%)
  waiting for transfers between devices  31.1 us (24%)
  Pallas kernels  28.1 us (22%)
  local copies, waits for them, and re-layouts  8.24 us (6%)
  starting transfers between devices  7.92 us (6%)
    all_to_all x1, blocking collectives, on_device(): field = lax.all_to_all(near, ('y', 'xh', 'z'), 0, 0, tiled=True)  37.8 us
    pallas_call x2, Pallas kernels, socs_image(): pl.pallas_call(socs_kernel, grid=(steps,), out_shape=out_shape, in_specs=...  14.8 us
    all_to_all x1, blocking collectives, on_device(): total = lax.all_to_all(total, ('s', 'z'), 0, 0, tiled=True)  13.4 us
    pallas_call x3, Pallas kernels, conv_stage(): pl.pallas_call(functools.partial(conv_kernel, lines, done, before, pixels...  13.3 us
    all_to_all x1, waiting for transfers between devices, on_device(): pieces = lax.all_to_all(images, ('y', 'xh', 'xl'), 0, 0, tiled=True)  11.9 us
    ppermute x2, waiting for transfers between devices, halo(): return lax.ppermute(block[:, 0], 's', SWAP)  11.8 us
    ppermute x1, waiting for transfers between devices, on_device(): other = lax.ppermute(field, 'xl', SWAP)  7.4 us
    all_to_all x1, starting transfers between devices, on_device(): pieces = lax.all_to_all(images, ('y', 'xh', 'xl'), 0, 0, tiled=True)  4.93 us
  transfers between devices with their start and end apart: 5, of which 3 were waited for; matrix products, arithmetic and copies ran while one was open for 2% of the time, Pallas kernels for 16%

profile of v5, /device:TPU:32, one launch (start us, length us, event | category | flops | bytes accessed | tf_op | source)
XLA Modules:
  0.0 127.1 jit_solution(5487908102698879266)
XLA Ops:
  0.0 1.2 dynamic-slice_bitcast_fusion
  1.2 1.9 %collective-permute-start = (bf16[2,1024,128]{2,1,0:T(8,128)(2,1)S(1)}, bf16[2,1024,128]{2,1,0:T(8,128)(2,1)S(1)}, u32[]{:S(2)}, u32[]{:S(2)}) collective-permute-start(bf16[2,1024,128]{2,1,0:T(8,128)(2,1)S(1)} %dynamic-slice_bitcast_fusion), channel_id=1, source_target_pairs={{0,128},{128,0},{1,129},{129,1},{2,130},{130,2},{3,131},{131,3},{4... | collective-permute-start | bytes 1572872 | tf_op jit(solution)/shard_map/ppermute | solution.py:160
  3.1 11.8 %collective-permute-done.refs_0_ = bf16[2,1024,128]{2,1,0:T(8,128)(2,1)S(1)} collective-permute-done((bf16[2,1024,128]{2,1,0:T(8,128)(2,1)S(1)}, bf16[2,1024,128]{2,1,0:T(8,128)(2,1)S(1)}, u32[]{:S(2)}, u32[]{:S(2)}) %collective-permute-start) | collective-permute-done | bytes 524320 | tf_op jit(solution)/shard_map/ppermute | solution.py:160
  15.0 0.0 collective-permute-start.3
  15.0 1.0 dynamic-slice_bitcast_fusion.1
  15.9 0.4 collective-permute-start.1
  16.3 1.1 copy-done.3
  17.5 5.2 %conv_stage.3 = (bf16[1,16,1024]{2,1,0:T(8,128)(2,1)S(1)}, f32[4,1024,128]{2,1,0:T(8,128)S(1)}) custom-call(s32[1]{0:T(128)} %bitcast.1.flip_ref, bf16[6,1024,128]{2,1,0:T(8,128)(2,1)S(1)} %bitcast.43, bf16[5,640,128]{2,1,0:T(8,128)(2,1)S(1)} %bitcast.44, bf16[16,128]{1,0:T(8,128)(2,1)S(1)} %bitcast.47), custom_call_target="tpu_custom_call" | custom-call | flops 4026531840 | bytes 4194304 | tf_op jit(solution)/shard_map/conv_stage/pallas_call | solution.py:78
  22.7 4.6 %conv_stage.4 = (bf16[2,16,1024]{2,1,0:T(8,128)(2,1)S(1)}, f32[3,1024,128]{2,1,0:T(8,128)S(1)}) custom-call(s32[1]{0:T(128)} %bitcast.1.flip_ref, bf16[2,1024,128]{2,1,0:T(8,128)(2,1)S(1)} %collective-permute-done.refs_0_, bf16[5,640,128]{2,1,0:T(8,128)(2,1)S(1)} %bitcast.45, bf16[16,128]{1,0:T(8,128)(2,1)S(1)} %bitcast.48, ...), custom_call_target="tpu_custom_call" | custom-call | flops 3019898880 | bytes 4194304 | tf_op jit(solution)/shard_map/conv_stage/pallas_call | solution.py:78
  27.3 0.0 collective-permute-done.1.refs_0_
  27.3 3.5 %conv_stage.5 = bf16[3,16,1024]{2,1,0:T(8,128)(2,1)S(1)} custom-call(s32[1]{0:T(128)} %bitcast.1.flip_ref, bf16[1,1024,128]{2,1,0:T(8,128)(2,1)S(1)} %collective-permute-done.1.refs_0_, bf16[5,640,128]{2,1,0:T(8,128)(2,1)S(1)} %bitcast.46, bf16[16,128]{1,0:T(8,128)(2,1)S(1)} %bitcast.49, f32[3,1024,128]{2,1,0:T(8,128)S(1)} %get-tuple-element.13.refs_3_), custom_call_target="tpu_custom_call" | custom-call | flops 1006632960 | bytes 4194304 | tf_op jit(solution)/shard_map/conv_stage/pallas_call | solution.py:78
  30.8 0.1 reshape.75
  30.9 0.3 copy.25
  31.2 0.5 broadcast_in_dim.2
  31.7 0.0 copy-start.6
  31.7 0.0 copy-start.1
  31.7 37.8 %all_to_all.15 = bf16[32,2,6,1024]{3,1,2,0:T(2,128)(2,1)S(1)} all-to-all(bf16[32,2,6,1024]{3,1,2,0:T(2,128)(2,1)S(1)} %bitcast.51), channel_id=1, replica_groups=mesh['s'=2,'y'=4,'xh'=2,'xl'=2,'z'=4,'c'=2] {'y','xh','z'}, dimensions={0} | all-to-all | bytes 1572864 | tf_op jit(solution)/shard_map/all_to_all | solution.py:176
  69.5 0.2 copy.26
  69.8 0.7 collective-permute-start.2
  70.5 0.6 dynamic_slice.9.weight_ref
  71.0 0.0 collective-permute-done.3.refs_2_.refs_3_
  71.0 2.2 %copy-done = bf16[1,1024,2048]{2,1,0:T(8,128)(2,1)S(1)} copy-done((bf16[1,1024,2048]{2,1,0:T(8,128)(2,1)S(1)}, bf16[1,1024,2048]{2,1,0:T(8,128)(2,1)}, u32[]{:S(2)}) %copy-start) | copy-done | bytes 4194328
  73.2 7.0 %socs_image.2.refs_4_ = f32[192,1024]{1,0:T(8,128)S(1)} custom-call(f32[1]{0:T(128)} %dynamic_slice.9.weight_ref, s32[1]{0:T(128)} %bitcast.low_ref, bf16[192,192]{1,0:T(8,128)(2,1)S(1)} %copy-done.1, bf16[384,1024]{1,0:T(8,128)(2,1)S(1)} %bitcast.40, bf16[1024,2048]{1,0:T(8,128)(2,1)S(1)} %bitcast.35, bf16[1024,2048]{1,0:T(8,128)(2,1)S(1)} %bitcast.36, ...), custom_call_target="tpu_custom_call" | custom-call | flops 3221225472 | bytes 9437184 | tf_op jit(solution)/shard_map/socs_image/pallas_call | solution.py:135
  80.3 7.4 %collective-permute-done.2.left_ref = bf16[384,1024]{1,0:T(8,128)(2,1)S(1)} collective-permute-done((bf16[384,1024]{1,0:T(8,128)(2,1)S(1)}, bf16[384,1024]{1,0:T(8,128)(2,1)S(1)}, u32[]{:S(2)}, u32[]{:S(2)}) %collective-permute-start.2) | collective-permute-done | bytes 786464 | tf_op jit(solution)/shard_map/ppermute | solution.py:178
  87.7 7.8 %socs_image.3 = bf16[8,2,24,1024]{3,2,1,0:T(8,128)(2,1)} custom-call(f32[1]{0:T(128)} %dynamic_slice.9.weight_ref, s32[1]{0:T(128)} %bitcast.low_ref, bf16[192,192]{1,0:T(8,128)(2,1)S(1)} %copy-done.1, bf16[384,1024]{1,0:T(8,128)(2,1)S(1)} %collective-permute-done.2.left_ref, bf16[1024,2048]{1,0:T(8,128)(2,1)S(1)} %bitcast.37, ...), custom_call_target="tpu_custom_call" | custom-call | flops 3221225472 | bytes 9437184 | tf_op jit(solution)/shard_map/socs_image/pallas_call | solution.py:135
  95.5 4.9 %all-to-all-start.1 = ((bf16[16,24,1024]{2,1,0:T(8,128)(2,1)}), bf16[16,24,1024]{2,1,0:T(8,128)(2,1)S(1)}, u32[]{:S(2)}, u32[]{:S(2)}) async-start(bf16[16,24,1024]{2,1,0:T(8,128)(2,1)} %bitcast.13), calls=%async_computation.1 | async-start | bytes 1572864 | tf_op jit(solution)/shard_map/all_to_all | solution.py:187
  100.4 11.9 %all-to-all-done.1 = bf16[16,24,1024]{2,1,0:T(8,128)(2,1)S(1)} async-done(((bf16[16,24,1024]{2,1,0:T(8,128)(2,1)}), bf16[16,24,1024]{2,1,0:T(8,128)(2,1)S(1)}, u32[]{:S(2)}, u32[]{:S(2)}) %all-to-all-start.1) | async-done | bytes 786464 | tf_op jit(solution)/shard_map/all_to_all | solution.py:187
  112.3 0.1 convert_reduce_fusion
  112.6 0.1 reshape.80
  112.6 13.4 %all_to_all.16 = f32[8,24,128]{2,1,0:T(8,128)S(1)} all-to-all(f32[8,24,128]{2,1,0:T(8,128)S(1)} %reshape.80), channel_id=1, replica_groups=mesh['s'=2,'y'=4,'xh'=2,'xl'=2,'z'=4,'c'=2] {'s','z'}, dimensions={0} | all-to-all | bytes 196608 | tf_op jit(solution)/shard_map/all_to_all | solution.py:193
  126.2 0.2 rev.3
  126.5 0.6 reshape.82
  (21 shorter events, 0.3 us)
Async XLA Ops:
  0.0 16.3 %copy-start.2 = (bf16[1,6,1024,128]{3,2,1,0:T(8,128)(2,1)S(1)}, bf16[1,6,1024,128]{3,2,1,0:T(8,128)(2,1)}, u32[]{:S(2)}) copy-start(bf16[1,6,1024,128]{3,2,1,0:T(8,128)(2,1)} %param.6) | copy-start | bytes 4718596
  0.0 16.3 %copy-start.5 = (bf16[128,16]{0,1:T(8,128)(2,1)S(1)}, bf16[128,16]{0,1:T(8,128)(2,1)}, u32[]{:S(2)}) copy-start(bf16[128,16]{0,1:T(8,128)(2,1)} %param.8) | copy-start | bytes 12292
  1.2 13.8 %collective-permute-start = (bf16[2,1024,128]{2,1,0:T(8,128)(2,1)S(1)}, bf16[2,1024,128]{2,1,0:T(8,128)(2,1)S(1)}, u32[]{:S(2)}, u32[]{:S(2)}) collective-permute-start(bf16[2,1024,128]{2,1,0:T(8,128)(2,1)S(1)} %dynamic-slice_bitcast_fusion), channel_id=1, source_target_pairs={{0,128},{128,0},{1,129},{129,1},{2,130},{130,2},{3,131},{131,3},{4... | collective-permute-start | bytes 1572872 | tf_op jit(solution)/shard_map/ppermute | solution.py:160
  15.0 56.1 %collective-permute-start.3 = (bf16[1024,2048]{1,0:T(8,128)(2,1)}, bf16[1024,2048]{1,0:T(8,128)(2,1)}, u32[]{:S(2)}, u32[]{:S(2)}) collective-permute-start(bf16[1024,2048]{1,0:T(8,128)(2,1)} %bitcast.34), channel_id=1, source_target_pairs={{0,1},{1,0},{2,3},{3,2},{4,5},{5,4},{6,7},{7,6},{8,9},{9,8},{10,11... | collective-permute-start | bytes 12582920 | tf_op jit(solution)/shard_map/ppermute | solution.py:165
  15.9 11.4 %collective-permute-start.1 = (bf16[1,1024,128]{2,1,0:T(8,128)(2,1)S(1)}, bf16[1,1024,128]{2,1,0:T(8,128)(2,1)S(1)}, u32[]{:S(2)}, u32[]{:S(2)}) collective-permute-start(bf16[1,1024,128]{2,1,0:T(8,128)(2,1)S(1)} %dynamic-slice_bitcast_fusion.1), channel_id=1, source_target_pairs={{0,128},{128,0},{1,129},{129,1},{2,130},{130,2},{3,131},{131,3},{4... | collective-permute-start | bytes 786440 | tf_op jit(solution)/shard_map/ppermute | solution.py:160
  16.3 1.1 copy-start.3
  17.5 5.2 %copy-start.4 = (bf16[5,5,128,128]{3,2,1,0:T(8,128)(2,1)S(1)}, bf16[5,5,128,128]{3,2,1,0:T(8,128)(2,1)}, u32[]{:S(2)}) copy-start(bf16[5,5,128,128]{3,2,1,0:T(8,128)(2,1)} %param.7) | copy-start | bytes 2457604
  31.7 38.8 %copy-start.6 = (f32[8]{0:T(128)S(1)}, f32[8]{0:T(128)}, u32[]{:S(2)}) copy-start(f32[8]{0:T(128)} %param.10) | copy-start | bytes 100
  31.7 39.3 %copy-start.1 = (bf16[192,192]{1,0:T(8,128)(2,1)S(1)}, bf16[192,192]{1,0:T(8,128)(2,1)}, u32[]{:S(2)}) copy-start(bf16[192,192]{1,0:T(8,128)(2,1)} %constant.36.clone.order_ref) | copy-start | bytes 221188
  69.8 17.9 %collective-permute-start.2 = (bf16[384,1024]{1,0:T(8,128)(2,1)S(1)}, bf16[384,1024]{1,0:T(8,128)(2,1)S(1)}, u32[]{:S(2)}, u32[]{:S(2)}) collective-permute-start(bf16[384,1024]{1,0:T(8,128)(2,1)S(1)} %bitcast.39), channel_id=1, source_target_pairs={{0,8},{8,0},{1,9},{9,1},{2,10},{10,2},{3,11},{11,3},{4,12},{12,4},... | collective-permute-start | bytes 2359304 | tf_op jit(solution)/shard_map/ppermute | solution.py:178
  71.0 2.2 %copy-start = (bf16[1,1024,2048]{2,1,0:T(8,128)(2,1)S(1)}, bf16[1,1024,2048]{2,1,0:T(8,128)(2,1)}, u32[]{:S(2)}) copy-start(bf16[1,1024,2048]{2,1,0:T(8,128)(2,1)} %param.9) | copy-start | bytes 12582916
  95.5 16.9 %all-to-all-start.1 = ((bf16[16,24,1024]{2,1,0:T(8,128)(2,1)}), bf16[16,24,1024]{2,1,0:T(8,128)(2,1)S(1)}, u32[]{:S(2)}, u32[]{:S(2)}) async-start(bf16[16,24,1024]{2,1,0:T(8,128)(2,1)} %bitcast.13), calls=%async_computation.1 | async-start | bytes 1572864 | tf_op jit(solution)/shard_map/all_to_all | solution.py:187

commit v6 on v4

--- a/solution.py
+++ b/solution.py
@@ -2,6 +2,7 @@
 
 import jax
 import jax.numpy as jnp
+import numpy as np
 from jax import lax
 from jax.experimental import pallas as pl
 from jax.experimental.pallas import tpu as pltpu
@@ -91,9 +92,12 @@
     return out[0], list(out[1:])
 
 
-def socs_kernel(block, weight_ref, left_ref, first_ref, second_ref, o_ref):
-    rows, pixels = o_ref.shape
+def socs_kernel(block, weight_ref, low_ref, order_ref, left_ref, first_ref, second_ref, *refs):
+    o_ref = refs[-1]
+    rows, pixels = left_ref.shape[0] // 2, left_ref.shape[1]
+    step = rows // ANG
     left = left_ref[...]
+    low = low_ref[0]
     for n in range(0, pixels, block):
         total = jnp.zeros((rows, block), F32)
         for g_ref in (first_ref, second_ref):
@@ -102,23 +106,58 @@
             re = by_re[:rows] - by_im[rows:]
             im = by_im[:rows] + by_re[rows:]
             total += re * re + im * im
-        o_ref[:, n : n + block] = (total * weight_ref[0]).astype(BF)
-
-
-def socs_image(weight, field, first, second):
+        total = jnp.dot(order_ref[...], (total * weight_ref[0]).astype(BF), preferred_element_type=F32)
+        if len(refs) == 1:
+            o_ref[:, n : n + block] = total
+        else:
+            for g in range(ANG):
+                held = refs[0][g * step : (g + 1) * step, n : n + block]
+                o_ref[g, low, :, n : n + block] = held.astype(BF)
+                o_ref[g, 1 - low, :, n : n + block] = total[g * step : (g + 1) * step].astype(BF)
+
+
+def socs_image(weight, low, order, field, first, second, own=()):
     rows, pixels = field.shape[0] // 2, field.shape[1]
+    scalar = pl.BlockSpec(memory_space=pltpu.SMEM)
     vmem = pl.BlockSpec(memory_space=pltpu.VMEM)
+    if own:
+        out_shape = jax.ShapeDtypeStruct((ANG, 2, rows // ANG, pixels), BF)
+    else:
+        out_shape = jax.ShapeDtypeStruct((rows, pixels), F32)
     return pl.pallas_call(
         functools.partial(socs_kernel, 256),
-        out_shape=jax.ShapeDtypeStruct((rows, pixels), BF),
-        in_specs=[pl.BlockSpec(memory_space=pltpu.SMEM)] + [vmem] * 3,
+        out_shape=out_shape,
+        in_specs=[scalar, scalar] + [vmem] * (4 + len(own)),
         out_specs=vmem,
-        compiler_params=pltpu.CompilerParams(vmem_limit_bytes=32 << 20),
+        compiler_params=pltpu.CompilerParams(vmem_limit_bytes=16 << 20),
         cost_estimate=pl.CostEstimate(
             flops=16 * rows * pixels * pixels, bytes_accessed=9 << 20, transcendentals=0
         ),
         name="socs_image",
-    )(weight, field, first, second)
+    )(weight, low, order, field, first, second, *own)
+
+
+def resident_kernel(first_ref, second_ref, a_ref, b_ref, sems):
+    copies = [
+        pltpu.make_async_copy(first_ref, a_ref, sems.at[0]),
+        pltpu.make_async_copy(second_ref, b_ref, sems.at[1]),
+    ]
+    for copy in copies:
+        copy.start()
+    for copy in copies:
+        copy.wait()
+
+
+def resident(first, second):
+    return pl.pallas_call(
+        resident_kernel,
+        out_shape=[jax.ShapeDtypeStruct(first.shape, first.dtype)] * 2,
+        in_specs=[pl.BlockSpec(memory_space=pl.ANY)] * 2,
+        out_specs=[pl.BlockSpec(memory_space=pltpu.VMEM)] * 2,
+        scratch_shapes=[pltpu.SemaphoreType.DMA((2,))],
+        compiler_params=pltpu.CompilerParams(vmem_limit_bytes=12 << 20),
+        name="resident",
+    )(first, second)
 
 
 def on_device(features, conv_weight, head_weight, kernels, source_weights):
@@ -137,7 +176,6 @@
     first = halo(1 - section, 2)
     last = halo(2 * section, 1)
     mine = kernels[0]
-    sibling = lax.ppermute(mine, "c", SWAP)
     flip = section.astype(jnp.int32).reshape(1)
     taps = conv_weight.reshape(conv_weight.shape[0], -1, channels)
     head = head_weight.T
@@ -145,6 +183,8 @@
     for stage, read in enumerate((window, first, last)):
         done, held = conv_stage(stage, flip, read, taps, head, held)
         near.append(done)
+        if stage == 2:
+            sibling = lax.ppermute(lax.optimization_barrier((mine, done))[0], "c", SWAP)
     near = jnp.concatenate(near, axis=0).reshape(LINES, ANG, 2, pixels).transpose(1, 2, 0, 3)
     near = jnp.broadcast_to(near[:, None], (ANG, depth, 2, LINES, pixels))
     near = near.reshape(ANG * depth, 2, LINES, pixels)
@@ -152,13 +192,13 @@
     field = field.transpose(1, 2, 0, 3).reshape(-1, pixels)
     other = lax.ppermute(field, "xl", SWAP)
 
-    def image(part):
-        part = socs_image(weight, part, mine, sibling)
-        return part.reshape(LINES, ANG, depth, pixels).transpose(1, 2, 0, 3)
-
-    own, other = image(field), image(other)
-    low = lax.axis_index("xl") == 0
-    images = jnp.stack([jnp.where(low, own, other), jnp.where(low, other, own)], axis=1)
+    mine, sibling = resident(mine, sibling)
+    low = lax.axis_index("xl").astype(jnp.int32).reshape(1)
+    sources = ANG * depth
+    order = np.eye(LINES * sources).reshape(LINES, sources, -1).transpose(1, 0, 2)
+    order = jnp.asarray(order.reshape(LINES * sources, -1), BF)
+    own = socs_image(weight, low, order, field, mine, sibling)
+    images = socs_image(weight, low, order, other, mine, sibling, (own,))
     images = images.reshape(2 * ANG, depth * LINES, pixels)
     pieces = lax.all_to_all(images, ("y", "xh", "xl"), 0, 0, tiled=True)
     total = jnp.sum(pieces.astype(F32), axis=0).reshape(depth, 2, OWN, pixels)

time: 120 us -> 119 us (level)
  local copies, waits for them, and re-layouts: 10.3 us -> 7.83 us
  Pallas kernels: 26.1 us -> 27.5 us
  blocking collectives: 49.8 us -> 51 us
    ppermute x2, waiting for transfers between devices: 5.67 us -> 3.2 us  [halo(): return lax.ppermute(block[:, 0], 's', SWAP)]
    reshape x2 -> x0, local copies, waits for them, and re-layouts: 1.58 us -> none  [on_device(): images = images.reshape(2 * ANG, depth * LINES, pixels)]
    ppermute x1, waiting for transfers between devices: 7.1 us -> 8.6 us  [on_device(): other = lax.ppermute(field, 'xl', SWAP)]
    pallas_call x2 -> x3, Pallas kernels: 12.7 us -> 14 us  [the longest x2 10.5 us: socs_image(): pl.pallas_call(functools.partial(socs_kernel, 256), out_shape=out_shape,...]
    unnamed x10 -> x14, local copies, waits for them, and re-layouts: 3.35 us -> 3.26 us
  transfers between devices with their start and end apart: 5 -> 5, of which waited for: 4 -> 3; matrix products, arithmetic and copies ran while one was open for 3% -> 2% of each run, Pallas kernels for 17% -> 15%
where the time goes in v6:
time: 119 us; the launch traced here: 118 us
  blocking collectives  51 us (43%)
  Pallas kernels  27.5 us (23%)
  waiting for transfers between devices  23.8 us (20%)
  starting transfers between devices  7.88 us (7%)
  local copies, waits for them, and re-layouts  7.83 us (7%)
    all_to_all x1, blocking collectives, on_device(): field = lax.all_to_all(near, ('y', 'xh', 'z'), 0, 0, tiled=True)  37.5 us
    all_to_all x1, blocking collectives, on_device(): total = lax.all_to_all(total, ('s', 'z'), 0, 0, tiled=True)  13.6 us
    pallas_call x3, Pallas kernels, conv_stage(): pl.pallas_call(functools.partial(conv_kernel, lines, done, before, pixels...  13.5 us
    all_to_all x1, waiting for transfers between devices, on_device(): pieces = lax.all_to_all(images, ('y', 'xh', 'xl'), 0, 0, tiled=True)  12 us
    pallas_call x2, Pallas kernels, socs_image(): pl.pallas_call(functools.partial(socs_kernel, 256), out_shape=out_shape,...  10.5 us
    ppermute x1, waiting for transfers between devices, on_device(): other = lax.ppermute(field, 'xl', SWAP)  8.6 us
    all_to_all x1, starting transfers between devices, on_device(): pieces = lax.all_to_all(images, ('y', 'xh', 'xl'), 0, 0, tiled=True)  4.9 us
    pallas_call x1, Pallas kernels, resident(): pl.pallas_call(resident_kernel, out_shape=[jax.ShapeDtypeStruct(first.sha...  3.51 us
  transfers between devices with their start and end apart: 5, of which 3 were waited for; matrix products, arithmetic and copies ran while one was open for 2% of the time, Pallas kernels for 15%

profile of v6, /device:TPU:32, one launch (start us, length us, event | category | flops | bytes accessed | tf_op | source)
XLA Modules:
  0.0 118.5 jit_solution(16804363102481442825)
XLA Ops:
  0.0 1.1 dynamic-slice_bitcast_fusion
  1.1 1.9 %collective-permute-start = (bf16[2,1024,128]{2,1,0:T(8,128)(2,1)S(1)}, bf16[2,1024,128]{2,1,0:T(8,128)(2,1)S(1)}, u32[]{:S(2)}, u32[]{:S(2)}) collective-permute-start(bf16[2,1024,128]{2,1,0:T(8,128)(2,1)S(1)} %dynamic-slice_bitcast_fusion), channel_id=1, source_target_pairs={{0,128},{128,0},{1,129},{129,1},{2,130},{130,2},{3,131},{131,3},{4... | collective-permute-start | bytes 1572872 | tf_op jit(solution)/shard_map/ppermute | solution.py:174
  3.0 1.0 dynamic-slice_bitcast_fusion.1
  4.0 0.3 collective-permute-start.1
  4.3 1.4 %copy-done = bf16[1,6,1024,128]{3,2,1,0:T(8,128)(2,1)S(1)} copy-done((bf16[1,6,1024,128]{3,2,1,0:T(8,128)(2,1)S(1)}, bf16[1,6,1024,128]{3,2,1,0:T(8,128)(2,1)}, u32[]{:S(2)}) %copy-start) | copy-done | bytes 1572888
  5.7 1.1 copy-done.1
  6.8 0.7 copy-done.3
  7.5 5.3 %conv_stage.3 = (bf16[1,16,1024]{2,1,0:T(8,128)(2,1)S(1)}, f32[4,1024,128]{2,1,0:T(8,128)S(1)}) custom-call(s32[1]{0:T(128)} %bitcast.1.flip_ref, bf16[6,1024,128]{2,1,0:T(8,128)(2,1)S(1)} %bitcast.38, bf16[5,640,128]{2,1,0:T(8,128)(2,1)S(1)} %bitcast.39, bf16[16,128]{1,0:T(8,128)(2,1)S(1)} %bitcast.42), custom_call_target="tpu_custom_call" | custom-call | flops 4026531840 | bytes 4194304 | tf_op jit(solution)/shard_map/conv_stage/pallas_call | solution.py:78
  12.8 3.2 %collective-permute-done.refs_0_ = bf16[2,1024,128]{2,1,0:T(8,128)(2,1)S(1)} collective-permute-done((bf16[2,1024,128]{2,1,0:T(8,128)(2,1)S(1)}, bf16[2,1024,128]{2,1,0:T(8,128)(2,1)S(1)}, u32[]{:S(2)}, u32[]{:S(2)}) %collective-permute-start) | collective-permute-done | bytes 524320 | tf_op jit(solution)/shard_map/ppermute | solution.py:174
  16.0 4.7 %conv_stage.4 = (bf16[2,16,1024]{2,1,0:T(8,128)(2,1)S(1)}, f32[3,1024,128]{2,1,0:T(8,128)S(1)}) custom-call(s32[1]{0:T(128)} %bitcast.1.flip_ref, bf16[2,1024,128]{2,1,0:T(8,128)(2,1)S(1)} %collective-permute-done.refs_0_, bf16[5,640,128]{2,1,0:T(8,128)(2,1)S(1)} %bitcast.40, bf16[16,128]{1,0:T(8,128)(2,1)S(1)} %bitcast.43, ...), custom_call_target="tpu_custom_call" | custom-call | flops 3019898880 | bytes 4194304 | tf_op jit(solution)/shard_map/conv_stage/pallas_call | solution.py:78
  20.7 3.5 %conv_stage.5 = bf16[3,16,1024]{2,1,0:T(8,128)(2,1)S(1)} custom-call(s32[1]{0:T(128)} %bitcast.1.flip_ref, bf16[1,1024,128]{2,1,0:T(8,128)(2,1)S(1)} %collective-permute-done.1.refs_0_, bf16[5,640,128]{2,1,0:T(8,128)(2,1)S(1)} %bitcast.41, bf16[16,128]{1,0:T(8,128)(2,1)S(1)} %bitcast.44, f32[3,1024,128]{2,1,0:T(8,128)S(1)} %get-tuple-element.15.refs_3_), custom_call_target="tpu_custom_call" | custom-call | flops 1006632960 | bytes 4194304 | tf_op jit(solution)/shard_map/conv_stage/pallas_call | solution.py:78
  24.2 0.2 collective-permute-start.3
  24.4 0.1 reshape.75
  24.5 0.1 copy.25
  24.7 0.0 copy-start.6
  24.7 0.5 broadcast_in_dim.2
  25.1 37.5 %all_to_all.15 = bf16[32,2,6,1024]{3,1,2,0:T(2,128)(2,1)S(1)} all-to-all(bf16[32,2,6,1024]{3,1,2,0:T(2,128)(2,1)S(1)} %bitcast.46), channel_id=1, replica_groups=mesh['s'=2,'y'=4,'xh'=2,'xl'=2,'z'=4,'c'=2] {'y','xh','z'}, dimensions={0} | all-to-all | bytes 1572864 | tf_op jit(solution)/shard_map/all_to_all | solution.py:191
  62.6 0.2 copy.26
  62.9 0.6 collective-permute-start.2
  63.5 0.6 dynamic_slice.9.weight_ref
  64.1 0.0 collective-permute-done.3.second_ref
  64.1 3.5 %resident.1 = (bf16[1024,2048]{1,0:T(8,128)(2,1)S(1)}, bf16[1024,2048]{1,0:T(8,128)(2,1)S(1)}) custom-call(bf16[1024,2048]{1,0:T(8,128)(2,1)} %bitcast.12.first_ref, bf16[1024,2048]{1,0:T(8,128)(2,1)} %collective-permute-done.3.second_ref), custom_call_target="tpu_custom_call" | custom-call | tf_op jit(solution)/shard_map/resident/pallas_call | solution.py:152
  67.6 4.8 %socs_image.2.refs_0_ = f32[192,1024]{1,0:T(8,128)S(1)} custom-call(f32[1]{0:T(128)} %dynamic_slice.9.weight_ref, s32[1]{0:T(128)} %bitcast.low_ref, bf16[192,192]{1,0:T(8,128)(2,1)S(1)} %copy-done.5, bf16[384,1024]{1,0:T(8,128)(2,1)S(1)} %bitcast.35, bf16[1024,2048]{1,0:T(8,128)(2,1)S(1)} %get-tuple-element.17.first_ref, ...), custom_call_target="tpu_custom_call" | custom-call | flops 3221225472 | bytes 9437184 | tf_op jit(solution)/shard_map/socs_image/pallas_call | solution.py:127
  72.4 8.6 %collective-permute-done.2.left_ref = bf16[384,1024]{1,0:T(8,128)(2,1)S(1)} collective-permute-done((bf16[384,1024]{1,0:T(8,128)(2,1)S(1)}, bf16[384,1024]{1,0:T(8,128)(2,1)S(1)}, u32[]{:S(2)}, u32[]{:S(2)}) %collective-permute-start.2) | collective-permute-done | bytes 786464 | tf_op jit(solution)/shard_map/ppermute | solution.py:193
  81.0 5.7 %socs_image.3 = bf16[8,2,24,1024]{3,2,1,0:T(8,128)(2,1)} custom-call(f32[1]{0:T(128)} %dynamic_slice.9.weight_ref, s32[1]{0:T(128)} %bitcast.low_ref, bf16[192,192]{1,0:T(8,128)(2,1)S(1)} %copy-done.5, bf16[384,1024]{1,0:T(8,128)(2,1)S(1)} %collective-permute-done.2.left_ref, bf16[1024,2048]{1,0:T(8,128)(2,1)S(1)} %get-tuple-element.17.first_ref, ...), custom_call_target="tpu_custom_call" | custom-call | flops 3221225472 | bytes 9437184 | tf_op jit(solution)/shard_map/socs_image/pallas_call | solution.py:127
  86.6 4.9 %all-to-all-start.1 = ((bf16[16,24,1024]{2,1,0:T(8,128)(2,1)}), bf16[16,24,1024]{2,1,0:T(8,128)(2,1)S(1)}, u32[]{:S(2)}, u32[]{:S(2)}) async-start(bf16[16,24,1024]{2,1,0:T(8,128)(2,1)} %bitcast.13), calls=%async_computation.1 | async-start | bytes 1572864 | tf_op jit(solution)/shard_map/all_to_all | solution.py:203
  91.6 12.0 %all-to-all-done.1 = bf16[16,24,1024]{2,1,0:T(8,128)(2,1)S(1)} async-done(((bf16[16,24,1024]{2,1,0:T(8,128)(2,1)}), bf16[16,24,1024]{2,1,0:T(8,128)(2,1)S(1)}, u32[]{:S(2)}, u32[]{:S(2)}) %all-to-all-start.1) | async-done | bytes 786464 | tf_op jit(solution)/shard_map/all_to_all | solution.py:203
  103.5 0.1 convert_reduce_fusion
  103.8 0.1 reshape.80
  103.9 13.6 %all_to_all.16 = f32[8,24,128]{2,1,0:T(8,128)S(1)} all-to-all(f32[8,24,128]{2,1,0:T(8,128)S(1)} %reshape.80), channel_id=1, replica_groups=mesh['s'=2,'y'=4,'xh'=2,'xl'=2,'z'=4,'c'=2] {'s','z'}, dimensions={0} | all-to-all | bytes 196608 | tf_op jit(solution)/shard_map/all_to_all | solution.py:209
  117.5 0.2 rev.3
  117.8 0.6 reshape.82
  (22 shorter events, 0.3 us)
Async XLA Ops:
  1.1 14.9 %collective-permute-start = (bf16[2,1024,128]{2,1,0:T(8,128)(2,1)S(1)}, bf16[2,1024,128]{2,1,0:T(8,128)(2,1)S(1)}, u32[]{:S(2)}, u32[]{:S(2)}) collective-permute-start(bf16[2,1024,128]{2,1,0:T(8,128)(2,1)S(1)} %dynamic-slice_bitcast_fusion), channel_id=1, source_target_pairs={{0,128},{128,0},{1,129},{129,1},{2,130},{130,2},{3,131},{131,3},{4... | collective-permute-start | bytes 1572872 | tf_op jit(solution)/shard_map/ppermute | solution.py:174
  4.0 16.8 %collective-permute-start.1 = (bf16[1,1024,128]{2,1,0:T(8,128)(2,1)S(1)}, bf16[1,1024,128]{2,1,0:T(8,128)(2,1)S(1)}, u32[]{:S(2)}, u32[]{:S(2)}) collective-permute-start(bf16[1,1024,128]{2,1,0:T(8,128)(2,1)S(1)} %dynamic-slice_bitcast_fusion.1), channel_id=1, source_target_pairs={{0,128},{128,0},{1,129},{129,1},{2,130},{130,2},{3,131},{131,3},{4... | collective-permute-start | bytes 786440 | tf_op jit(solution)/shard_map/ppermute | solution.py:174
  4.3 1.4 %copy-start = (bf16[1,6,1024,128]{3,2,1,0:T(8,128)(2,1)S(1)}, bf16[1,6,1024,128]{3,2,1,0:T(8,128)(2,1)}, u32[]{:S(2)}) copy-start(bf16[1,6,1024,128]{3,2,1,0:T(8,128)(2,1)} %param.6) | copy-start | bytes 4718596
  5.7 1.1 copy-start.1
  6.8 0.7 copy-start.3
  7.5 8.5 %copy-start.2 = (bf16[5,5,128,128]{3,2,1,0:T(8,128)(2,1)S(1)}, bf16[5,5,128,128]{3,2,1,0:T(8,128)(2,1)}, u32[]{:S(2)}) copy-start(bf16[5,5,128,128]{3,2,1,0:T(8,128)(2,1)} %param.7) | copy-start | bytes 2457604
  7.5 8.5 %copy-start.4 = (bf16[128,16]{0,1:T(8,128)(2,1)S(1)}, bf16[128,16]{0,1:T(8,128)(2,1)}, u32[]{:S(2)}) copy-start(bf16[128,16]{0,1:T(8,128)(2,1)} %param.8) | copy-start | bytes 12292
  24.2 39.8 %collective-permute-start.3 = (bf16[1024,2048]{1,0:T(8,128)(2,1)}, bf16[1024,2048]{1,0:T(8,128)(2,1)}, u32[]{:S(2)}, u32[]{:S(2)}) collective-permute-start(bf16[1024,2048]{1,0:T(8,128)(2,1)} %bitcast.12.first_ref), channel_id=1, source_target_pairs={{0,1},{1,0},{2,3},{3,2},{4,5},{5,4},{6,7},{7,6},{8,9},{9,8},{10,11... | collective-permute-start | bytes 12582920 | tf_op jit(solution)/shard_map/ppermute | solution.py:187
  24.7 38.8 %copy-start.6 = (f32[8]{0:T(128)S(1)}, f32[8]{0:T(128)}, u32[]{:S(2)}) copy-start(f32[8]{0:T(128)} %param.10) | copy-start | bytes 100
  62.9 18.1 %collective-permute-start.2 = (bf16[384,1024]{1,0:T(8,128)(2,1)S(1)}, bf16[384,1024]{1,0:T(8,128)(2,1)S(1)}, u32[]{:S(2)}, u32[]{:S(2)}) collective-permute-start(bf16[384,1024]{1,0:T(8,128)(2,1)S(1)} %bitcast.34), channel_id=1, source_target_pairs={{0,8},{8,0},{1,9},{9,1},{2,10},{10,2},{3,11},{11,3},{4,12},{12,4},... | collective-permute-start | bytes 2359304 | tf_op jit(solution)/shard_map/ppermute | solution.py:193
  64.1 3.5 %copy-start.5 = (bf16[192,192]{1,0:T(8,128)(2,1)S(1)}, bf16[192,192]{1,0:T(8,128)(2,1)}, u32[]{:S(2)}) copy-start(bf16[192,192]{1,0:T(8,128)(2,1)} %constant.36.clone.order_ref) | copy-start | bytes 221188
  86.6 16.9 %all-to-all-start.1 = ((bf16[16,24,1024]{2,1,0:T(8,128)(2,1)}), bf16[16,24,1024]{2,1,0:T(8,128)(2,1)S(1)}, u32[]{:S(2)}, u32[]{:S(2)}) async-start(bf16[16,24,1024]{2,1,0:T(8,128)(2,1)} %bitcast.13), calls=%async_computation.1 | async-start | bytes 1572864 | tf_op jit(solution)/shard_map/all_to_all | solution.py:203

commit v7 on v6

--- a/solution.py
+++ b/solution.py
@@ -92,49 +92,59 @@
     return out[0], list(out[1:])
 
 
-def socs_kernel(block, weight_ref, low_ref, order_ref, left_ref, first_ref, second_ref, *refs):
-    o_ref = refs[-1]
-    rows, pixels = left_ref.shape[0] // 2, left_ref.shape[1]
-    step = rows // ANG
-    left = left_ref[...]
-    low = low_ref[0]
+def socs_kernel(block, fields, weight_ref, low_ref, order_ref, first_ref, second_ref, *refs):
+    field_refs, o_ref = refs[:fields], refs[-1]
+    held = refs[fields] if len(refs) > fields + 1 else None
+    count, lines, pixels = field_refs[0].shape
+    half = count * lines // 2
+    rows = fields * half
+    left = jnp.concatenate([f[z + p] for p in (0, 1) for f in field_refs for z in range(0, count, 2)], axis=0)
+    order = order_ref[...]
+    step = 2 * half // ANG
     for n in range(0, pixels, block):
+        cols = slice(n, n + block)
         total = jnp.zeros((rows, block), F32)
         for g_ref in (first_ref, second_ref):
-            by_re = jnp.dot(left, g_ref[:, n : n + block], preferred_element_type=F32)
+            by_re = jnp.dot(left, g_ref[:, cols], preferred_element_type=F32)
             by_im = jnp.dot(left, g_ref[:, pixels + n : pixels + n + block], preferred_element_type=F32)
             re = by_re[:rows] - by_im[rows:]
             im = by_im[:rows] + by_re[rows:]
             total += re * re + im * im
-        total = jnp.dot(order_ref[...], (total * weight_ref[0]).astype(BF), preferred_element_type=F32)
-        if len(refs) == 1:
-            o_ref[:, n : n + block] = total
+        total = (total * weight_ref[0]).astype(BF)
+        if held is None:
+            own = jnp.dot(order, total[: 2 * half], preferred_element_type=F32)
+            o_ref[: 2 * half, cols] = own.astype(BF)
+            o_ref[2 * half :, cols] = total[2 * half :]
         else:
+            low = low_ref[0]
+            own = held[: 2 * half, cols].astype(F32)
+            other = jnp.concatenate([held[2 * half :, cols], total], axis=0)
+            other = jnp.dot(order, other, preferred_element_type=F32)
             for g in range(ANG):
-                held = refs[0][g * step : (g + 1) * step, n : n + block]
-                o_ref[g, low, :, n : n + block] = held.astype(BF)
-                o_ref[g, 1 - low, :, n : n + block] = total[g * step : (g + 1) * step].astype(BF)
-
-
-def socs_image(weight, low, order, field, first, second, own=()):
-    rows, pixels = field.shape[0] // 2, field.shape[1]
+                o_ref[g, low, :, cols] = own[g * step : (g + 1) * step].astype(BF)
+                o_ref[g, 1 - low, :, cols] = other[g * step : (g + 1) * step].astype(BF)
+
+
+def socs_image(weight, low, order, first, second, fields, held=()):
+    count, lines, pixels = fields[0].shape
+    half = count * lines // 2
     scalar = pl.BlockSpec(memory_space=pltpu.SMEM)
     vmem = pl.BlockSpec(memory_space=pltpu.VMEM)
-    if own:
-        out_shape = jax.ShapeDtypeStruct((ANG, 2, rows // ANG, pixels), BF)
+    if held:
+        out_shape = jax.ShapeDtypeStruct((ANG, 2, 2 * half // ANG, pixels), BF)
     else:
-        out_shape = jax.ShapeDtypeStruct((rows, pixels), F32)
+        out_shape = jax.ShapeDtypeStruct((len(fields) * half, pixels), BF)
     return pl.pallas_call(
-        functools.partial(socs_kernel, 256),
+        functools.partial(socs_kernel, 256, len(fields)),
         out_shape=out_shape,
-        in_specs=[scalar, scalar] + [vmem] * (4 + len(own)),
+        in_specs=[scalar, scalar] + [vmem] * (3 + len(fields) + len(held)),
         out_specs=vmem,
-        compiler_params=pltpu.CompilerParams(vmem_limit_bytes=16 << 20),
+        compiler_params=pltpu.CompilerParams(vmem_limit_bytes=20 << 20),
         cost_estimate=pl.CostEstimate(
-            flops=16 * rows * pixels * pixels, bytes_accessed=9 << 20, transcendentals=0
+            flops=16 * len(fields) * half * pixels * pixels, bytes_accessed=9 << 20, transcendentals=0
         ),
         name="socs_image",
-    )(weight, low, order, field, first, second, *own)
+    )(weight, low, order, first, second, *fields, *held)
 
 
 def resident_kernel(first_ref, second_ref, a_ref, b_ref, sems):
@@ -156,6 +166,7 @@
         out_specs=[pl.BlockSpec(memory_space=pltpu.VMEM)] * 2,
         scratch_shapes=[pltpu.SemaphoreType.DMA((2,))],
         compiler_params=pltpu.CompilerParams(vmem_limit_bytes=12 << 20),
+        cost_estimate=pl.CostEstimate(flops=0, bytes_accessed=4 * first.size * 2, transcendentals=0),
         name="resident",
     )(first, second)
 
@@ -186,19 +197,25 @@
         if stage == 2:
             sibling = lax.ppermute(lax.optimization_barrier((mine, done))[0], "c", SWAP)
     near = jnp.concatenate(near, axis=0).reshape(LINES, ANG, 2, pixels).transpose(1, 2, 0, 3)
-    near = jnp.broadcast_to(near[:, None], (ANG, depth, 2, LINES, pixels))
-    near = near.reshape(ANG * depth, 2, LINES, pixels)
-    field = lax.all_to_all(near, ("y", "xh", "z"), 0, 0, tiled=True)
-    field = field.transpose(1, 2, 0, 3).reshape(-1, pixels)
-    other = lax.ppermute(field, "xl", SWAP)
-
+    near = lax.all_to_all(near, ("y", "xh"), 0, 0, tiled=True)
+    near = near.transpose(1, 2, 0, 3)
+    part = LINES // 2
+    own_a = lax.all_gather(near[:, :part], "z", axis=0, tiled=False)
+    other_a = lax.ppermute(own_a, "xl", SWAP)
+    rest = lax.optimization_barrier((near[:, part:], own_a))[0]
+    own_b = lax.all_gather(rest, "z", axis=0, tiled=False)
+    own_b, other_a = lax.optimization_barrier((own_b, other_a))
+    other_b = lax.ppermute(own_b, "xl", SWAP)
     mine, sibling = resident(mine, sibling)
     low = lax.axis_index("xl").astype(jnp.int32).reshape(1)
-    sources = ANG * depth
-    order = np.eye(LINES * sources).reshape(LINES, sources, -1).transpose(1, 0, 2)
-    order = jnp.asarray(order.reshape(LINES * sources, -1), BF)
-    own = socs_image(weight, low, order, field, mine, sibling)
-    images = socs_image(weight, low, order, other, mine, sibling, (own,))
+    order = np.eye(ANG * depth * LINES).reshape(2, depth, part, ANG, -1).transpose(3, 1, 0, 2, 4)
+    order = jnp.asarray(order.reshape(ANG * depth * LINES, -1), BF)
+
+    def flat(block):
+        return block.reshape(2 * depth, part * ANG, pixels)
+
+    held = socs_image(weight, low, order, mine, sibling, [flat(own_a), flat(own_b), flat(other_a)])
+    images = socs_image(weight, low, order, mine, sibling, [flat(other_b)], (held,))
     images = images.reshape(2 * ANG, depth * LINES, pixels)
     pieces = lax.all_to_all(images, ("y", "xh", "xl"), 0, 0, tiled=True)
     total = jnp.sum(pieces.astype(F32), axis=0).reshape(depth, 2, OWN, pixels)

time: 119 us -> 120 us (level)
  blocking collectives: 51 us -> 61.1 us
  waiting for transfers between devices: 23.8 us -> 14.7 us
    all_gather x0 -> x2, blocking collectives: none -> 32.9 us  [the longest x1 18 us: on_device(): own_a = lax.all_gather(near[:, :part], 'z', axis=0, tiled=False)]
    all_to_all x1, blocking collectives: 37.5 us -> 15.5 us  [on_device(): near = lax.all_to_all(near, ('y', 'xh'), 0, 0, tiled=True)]
    ppermute x1 -> x2, waiting for transfers between devices: 8.6 us -> 0.01 us  [the longest x1 0.01 us: on_device(): other_b = lax.ppermute(own_b, 'xl', SWAP)]
    ppermute x1 -> x2, starting transfers between devices: 0.6 us -> 2 us  [the longest x1 1.4 us: on_device(): other_b = lax.ppermute(own_b, 'xl', SWAP)]
    all_to_all x1, starting transfers between devices: 4.9 us -> 3.61 us  [on_device(): pieces = lax.all_to_all(images, ('y', 'xh', 'xl'), 0, 0, tiled=True)]
  transfers between devices with their start and end apart: 5 -> 6, of which waited for: 3 -> 2; matrix products, arithmetic and copies ran while one was open for 2% -> 2% of each run, Pallas kernels for 15% -> 17%
where the time goes in v7:
time: 120 us; the launch traced here: 119 us
  blocking collectives  61.1 us (51%)
  Pallas kernels  27.5 us (23%)
  waiting for transfers between devices  14.7 us (12%)
  starting transfers between devices  7.99 us (7%)
  local copies, waits for them, and re-layouts  7.31 us (6%)
    all_gather x1, blocking collectives, on_device(): own_a = lax.all_gather(near[:, :part], 'z', axis=0, tiled=False)  18 us
    all_to_all x1, blocking collectives, on_device(): near = lax.all_to_all(near, ('y', 'xh'), 0, 0, tiled=True)  15.5 us
    all_gather x1, blocking collectives, on_device(): own_b = lax.all_gather(rest, 'z', axis=0, tiled=False)  14.9 us
    pallas_call x3, Pallas kernels, conv_stage(): pl.pallas_call(functools.partial(conv_kernel, lines, done, before, pixels...  13.5 us
    all_to_all x1, blocking collectives, on_device(): total = lax.all_to_all(total, ('s', 'z'), 0, 0, tiled=True)  12.7 us
    all_to_all x1, waiting for transfers between devices, on_device(): pieces = lax.all_to_all(images, ('y', 'xh', 'xl'), 0, 0, tiled=True)  11.5 us
    pallas_call x2, Pallas kernels, socs_image(): pl.pallas_call(functools.partial(socs_kernel, 256, len(fields)), out_shap...  10.5 us
    all_to_all x1, starting transfers between devices, on_device(): pieces = lax.all_to_all(images, ('y', 'xh', 'xl'), 0, 0, tiled=True)  3.61 us
  transfers between devices with their start and end apart: 6, of which 2 were waited for; matrix products, arithmetic and copies ran while one was open for 2% of the time, Pallas kernels for 17%

profile of v7, /device:TPU:32, one launch (start us, length us, event | category | flops | bytes accessed | tf_op | source)
XLA Modules:
  0.0 119.1 jit_solution(496511336722267645)
XLA Ops:
  0.0 1.1 dynamic-slice_bitcast_fusion
  1.1 1.9 %collective-permute-start.1 = (bf16[2,1024,128]{2,1,0:T(8,128)(2,1)S(1)}, bf16[2,1024,128]{2,1,0:T(8,128)(2,1)S(1)}, u32[]{:S(2)}, u32[]{:S(2)}) collective-permute-start(bf16[2,1024,128]{2,1,0:T(8,128)(2,1)S(1)} %dynamic-slice_bitcast_fusion), channel_id=1, source_target_pairs={{0,128},{128,0},{1,129},{129,1},{2,130},{130,2},{3,131},{131,3},{4... | collective-permute-start | bytes 1572872 | tf_op jit(solution)/shard_map/ppermute | solution.py:185
  3.0 1.0 dynamic-slice_bitcast_fusion.1
  4.0 0.3 collective-permute-start
  4.3 1.4 %copy-done = bf16[1,6,1024,128]{3,2,1,0:T(8,128)(2,1)S(1)} copy-done((bf16[1,6,1024,128]{3,2,1,0:T(8,128)(2,1)S(1)}, bf16[1,6,1024,128]{3,2,1,0:T(8,128)(2,1)}, u32[]{:S(2)}) %copy-start) | copy-done | bytes 1572888
  5.7 1.1 copy-done.2
  6.8 0.7 copy-done.4
  7.5 5.3 %conv_stage.3 = (bf16[1,16,1024]{2,1,0:T(8,128)(2,1)S(1)}, f32[4,1024,128]{2,1,0:T(8,128)S(1)}) custom-call(s32[1]{0:T(128)} %bitcast.2.flip_ref, bf16[6,1024,128]{2,1,0:T(8,128)(2,1)S(1)} %bitcast.42, bf16[5,640,128]{2,1,0:T(8,128)(2,1)S(1)} %bitcast.48, bf16[16,128]{1,0:T(8,128)(2,1)S(1)} %bitcast.52), custom_call_target="tpu_custom_call" | custom-call | flops 4026531840 | bytes 4194304 | tf_op jit(solution)/shard_map/conv_stage/pallas_call | solution.py:78
  12.8 3.2 %collective-permute-done.1.refs_0_ = bf16[2,1024,128]{2,1,0:T(8,128)(2,1)S(1)} collective-permute-done((bf16[2,1024,128]{2,1,0:T(8,128)(2,1)S(1)}, bf16[2,1024,128]{2,1,0:T(8,128)(2,1)S(1)}, u32[]{:S(2)}, u32[]{:S(2)}) %collective-permute-start.1) | collective-permute-done | bytes 524320 | tf_op jit(solution)/shard_map/ppermute | solution.py:185
  16.0 4.7 %conv_stage.4 = (bf16[2,16,1024]{2,1,0:T(8,128)(2,1)S(1)}, f32[3,1024,128]{2,1,0:T(8,128)S(1)}) custom-call(s32[1]{0:T(128)} %bitcast.2.flip_ref, bf16[2,1024,128]{2,1,0:T(8,128)(2,1)S(1)} %collective-permute-done.1.refs_0_, bf16[5,640,128]{2,1,0:T(8,128)(2,1)S(1)} %bitcast.49, bf16[16,128]{1,0:T(8,128)(2,1)S(1)} %bitcast.53, ...), custom_call_target="tpu_custom_call" | custom-call | flops 3019898880 | bytes 4194304 | tf_op jit(solution)/shard_map/conv_stage/pallas_call | solution.py:78
  20.7 3.5 %conv_stage.5 = bf16[3,16,1024]{2,1,0:T(8,128)(2,1)S(1)} custom-call(s32[1]{0:T(128)} %bitcast.2.flip_ref, bf16[1,1024,128]{2,1,0:T(8,128)(2,1)S(1)} %collective-permute-done.refs_0_, bf16[5,640,128]{2,1,0:T(8,128)(2,1)S(1)} %bitcast.50, bf16[16,128]{1,0:T(8,128)(2,1)S(1)} %bitcast.54, f32[3,1024,128]{2,1,0:T(8,128)S(1)} %get-tuple-element.16.refs_3_), custom_call_target="tpu_custom_call" | custom-call | flops 1006632960 | bytes 4194304 | tf_op jit(solution)/shard_map/conv_stage/pallas_call | solution.py:78
  24.2 0.2 collective-permute-start.2
  24.4 0.1 reshape.80
  24.5 0.1 copy.36
  24.7 15.5 %all_to_all.15 = bf16[8,2,6,1024]{3,1,2,0:T(2,128)(2,1)S(1)} all-to-all(bf16[8,2,6,1024]{3,1,2,0:T(2,128)(2,1)S(1)} %bitcast.56), channel_id=1, replica_groups=mesh['s'=2,'y'=4,'xh'=2,'xl'=2,'z'=4,'c'=2] {'y','xh'}, dimensions={0} | all-to-all | bytes 393216 | tf_op jit(solution)/shard_map/all_to_all | solution.py:200
  40.2 0.1 fusion.1
  40.3 18.0 %all-gather = bf16[8,3,8,1024]{3,2,1,0:T(8,128)(2,1)S(1)} all-gather(bf16[2,3,8,1024]{3,2,1,0:T(8,128)(2,1)S(1)} %copy.27), channel_id=2, replica_groups=mesh['s'=2,'y'=4,'xh'=2,'xl'=2,'z'=4,'c'=2] {'z'}, dimensions={0}, use_global_device_ids=true | all-gather | bytes 491520 | tf_op jit(solution)/shard_map/all_gather | solution.py:203
  58.4 0.6 collective-permute-start.3
  59.0 0.6 dynamic_slice.9.weight_ref
  59.6 14.9 %all-gather.1 = bf16[8,3,8,1024]{3,2,1,0:T(8,128)(2,1)S(1)} all-gather(bf16[2,3,8,1024]{3,2,1,0:T(8,128)(2,1)S(1)} %copy.28), channel_id=3, replica_groups=mesh['s'=2,'y'=4,'xh'=2,'xl'=2,'z'=4,'c'=2] {'z'}, dimensions={0}, use_global_device_ids=true | all-gather | bytes 491520 | tf_op jit(solution)/shard_map/all_gather | solution.py:206
  74.5 1.4 %collective-permute-start.4 = (bf16[4,2,3,8,1024]{4,3,2,1,0:T(8,128)(2,1)S(1)}, bf16[4,2,3,8,1024]{4,3,2,1,0:T(8,128)(2,1)S(1)}, u32[]{:S(2)}, u32[]{:S(2)}) collective-permute-start(bf16[4,2,3,8,1024]{4,3,2,1,0:T(8,128)(2,1)S(1)} %bitcast.45), channel_id=1, source_target_pairs={{0,8},{8,0},{1,9},{9,1},{2,10},{10,2},{3,11},{11,3},{4,12},{12,4},... | collective-permute-start | bytes 1179656 | tf_op jit(solution)/shard_map/ppermute | solution.py:208
  75.9 0.0 collective-permute-done.2.second_ref
  75.9 3.5 %resident.1 = (bf16[1024,2048]{1,0:T(8,128)(2,1)S(1)}, bf16[1024,2048]{1,0:T(8,128)(2,1)S(1)}) custom-call(bf16[1024,2048]{1,0:T(8,128)(2,1)} %bitcast.1.first_ref, bf16[1024,2048]{1,0:T(8,128)(2,1)} %collective-permute-done.2.second_ref), custom_call_target="tpu_custom_call" | custom-call | bytes 16777216 | tf_op jit(solution)/shard_map/resident/pallas_call | solution.py:162
  79.4 6.4 %socs_image.2.refs_1_ = bf16[288,1024]{1,0:T(8,128)(2,1)S(1)} custom-call(f32[1]{0:T(128)} %dynamic_slice.9.weight_ref, s32[1]{0:T(128)} %bitcast.low_ref, bf16[192,192]{1,0:T(8,128)(2,1)S(1)} %copy-done.1, bf16[1024,2048]{1,0:T(8,128)(2,1)S(1)} %get-tuple-element.18.first_ref, bf16[1024,2048]{1,0:T(8,128)(2,1)S(1)} %get-tuple-element.19.second_ref, ...), custom_call_target="tpu_custom_call" | custom-call | flops 4831838208 | bytes 9437184 | tf_op jit(solution)/shard_map/socs_image/pallas_call | solution.py:137
  85.8 4.1 %socs_image.3 = bf16[8,2,24,1024]{3,2,1,0:T(8,128)(2,1)} custom-call(f32[1]{0:T(128)} %dynamic_slice.9.weight_ref, s32[1]{0:T(128)} %bitcast.low_ref, bf16[192,192]{1,0:T(8,128)(2,1)S(1)} %copy-done.1, bf16[1024,2048]{1,0:T(8,128)(2,1)S(1)} %get-tuple-element.18.first_ref, bf16[1024,2048]{1,0:T(8,128)(2,1)S(1)} %get-tuple-element.19.second_ref, ...), custom_call_target="tpu_custom_call" | custom-call | flops 1610612736 | bytes 9437184 | tf_op jit(solution)/shard_map/socs_image/pallas_call | solution.py:137
  89.9 3.6 %all-to-all-start.1 = ((bf16[16,24,1024]{2,1,0:T(8,128)(2,1)}), bf16[16,24,1024]{2,1,0:T(8,128)(2,1)S(1)}, u32[]{:S(2)}, u32[]{:S(2)}) async-start(bf16[16,24,1024]{2,1,0:T(8,128)(2,1)} %bitcast.17), calls=%async_computation.1 | async-start | bytes 1572864 | tf_op jit(solution)/shard_map/all_to_all | solution.py:220
  93.5 11.5 %all-to-all-done.1 = bf16[16,24,1024]{2,1,0:T(8,128)(2,1)S(1)} async-done(((bf16[16,24,1024]{2,1,0:T(8,128)(2,1)}), bf16[16,24,1024]{2,1,0:T(8,128)(2,1)S(1)}, u32[]{:S(2)}, u32[]{:S(2)}) %all-to-all-start.1) | async-done | bytes 786464 | tf_op jit(solution)/shard_map/all_to_all | solution.py:220
  105.0 0.1 convert_reduce_fusion
  105.3 0.1 reshape.87
  105.4 12.7 %all_to_all.16 = f32[8,24,128]{2,1,0:T(8,128)S(1)} all-to-all(f32[8,24,128]{2,1,0:T(8,128)S(1)} %reshape.87), channel_id=1, replica_groups=mesh['s'=2,'y'=4,'xh'=2,'xl'=2,'z'=4,'c'=2] {'s','z'}, dimensions={0} | all-to-all | bytes 196608 | tf_op jit(solution)/shard_map/all_to_all | solution.py:226
  118.2 0.2 rev.3
  118.5 0.6 reshape.89
  (27 shorter events, 0.3 us)
Async XLA Ops:
  1.1 14.9 %collective-permute-start.1 = (bf16[2,1024,128]{2,1,0:T(8,128)(2,1)S(1)}, bf16[2,1024,128]{2,1,0:T(8,128)(2,1)S(1)}, u32[]{:S(2)}, u32[]{:S(2)}) collective-permute-start(bf16[2,1024,128]{2,1,0:T(8,128)(2,1)S(1)} %dynamic-slice_bitcast_fusion), channel_id=1, source_target_pairs={{0,128},{128,0},{1,129},{129,1},{2,130},{130,2},{3,131},{131,3},{4... | collective-permute-start | bytes 1572872 | tf_op jit(solution)/shard_map/ppermute | solution.py:185
  4.0 16.8 %collective-permute-start = (bf16[1,1024,128]{2,1,0:T(8,128)(2,1)S(1)}, bf16[1,1024,128]{2,1,0:T(8,128)(2,1)S(1)}, u32[]{:S(2)}, u32[]{:S(2)}) collective-permute-start(bf16[1,1024,128]{2,1,0:T(8,128)(2,1)S(1)} %dynamic-slice_bitcast_fusion.1), channel_id=1, source_target_pairs={{0,128},{128,0},{1,129},{129,1},{2,130},{130,2},{3,131},{131,3},{4... | collective-permute-start | bytes 786440 | tf_op jit(solution)/shard_map/ppermute | solution.py:185
  4.3 1.4 %copy-start = (bf16[1,6,1024,128]{3,2,1,0:T(8,128)(2,1)S(1)}, bf16[1,6,1024,128]{3,2,1,0:T(8,128)(2,1)}, u32[]{:S(2)}) copy-start(bf16[1,6,1024,128]{3,2,1,0:T(8,128)(2,1)} %param.6) | copy-start | bytes 4718596
  5.7 1.1 copy-start.2
  6.8 0.7 copy-start.4
  7.5 8.5 %copy-start.3 = (bf16[5,5,128,128]{3,2,1,0:T(8,128)(2,1)S(1)}, bf16[5,5,128,128]{3,2,1,0:T(8,128)(2,1)}, u32[]{:S(2)}) copy-start(bf16[5,5,128,128]{3,2,1,0:T(8,128)(2,1)} %param.7) | copy-start | bytes 2457604
  7.5 8.5 %copy-start.5 = (bf16[128,16]{0,1:T(8,128)(2,1)S(1)}, bf16[128,16]{0,1:T(8,128)(2,1)}, u32[]{:S(2)}) copy-start(bf16[128,16]{0,1:T(8,128)(2,1)} %param.8) | copy-start | bytes 12292
  24.2 34.7 %copy-start.6 = (f32[8]{0:T(128)S(1)}, f32[8]{0:T(128)}, u32[]{:S(2)}) copy-start(f32[8]{0:T(128)} %param.10) | copy-start | bytes 100
  24.2 51.6 %collective-permute-start.2 = (bf16[1024,2048]{1,0:T(8,128)(2,1)}, bf16[1024,2048]{1,0:T(8,128)(2,1)}, u32[]{:S(2)}, u32[]{:S(2)}) collective-permute-start(bf16[1024,2048]{1,0:T(8,128)(2,1)} %bitcast.1.first_ref), channel_id=1, source_target_pairs={{0,1},{1,0},{2,3},{3,2},{4,5},{5,4},{6,7},{7,6},{8,9},{9,8},{10,11... | collective-permute-start | bytes 12582920 | tf_op jit(solution)/shard_map/ppermute | solution.py:198
  58.4 16.1 %collective-permute-start.3 = (bf16[4,2,3,8,1024]{4,3,2,1,0:T(8,128)(2,1)S(1)}, bf16[4,2,3,8,1024]{4,3,2,1,0:T(8,128)(2,1)S(1)}, u32[]{:S(2)}, u32[]{:S(2)}) collective-permute-start(bf16[4,2,3,8,1024]{4,3,2,1,0:T(8,128)(2,1)S(1)} %bitcast.43), channel_id=1, source_target_pairs={{0,8},{8,0},{1,9},{9,1},{2,10},{10,2},{3,11},{11,3},{4,12},{12,4},... | collective-permute-start | bytes 1179656 | tf_op jit(solution)/shard_map/ppermute | solution.py:204
  74.5 4.9 %copy-start.1 = (bf16[192,192]{1,0:T(8,128)(2,1)S(1)}, bf16[192,192]{1,0:T(8,128)(2,1)}, u32[]{:S(2)}) copy-start(bf16[192,192]{1,0:T(8,128)(2,1)} %constant.36.clone.order_ref) | copy-start | bytes 221188
  74.5 11.3 %collective-permute-start.4 = (bf16[4,2,3,8,1024]{4,3,2,1,0:T(8,128)(2,1)S(1)}, bf16[4,2,3,8,1024]{4,3,2,1,0:T(8,128)(2,1)S(1)}, u32[]{:S(2)}, u32[]{:S(2)}) collective-permute-start(bf16[4,2,3,8,1024]{4,3,2,1,0:T(8,128)(2,1)S(1)} %bitcast.45), channel_id=1, source_target_pairs={{0,8},{8,0},{1,9},{9,1},{2,10},{10,2},{3,11},{11,3},{4,12},{12,4},... | collective-permute-start | bytes 1179656 | tf_op jit(solution)/shard_map/ppermute | solution.py:208
  89.9 15.2 %all-to-all-start.1 = ((bf16[16,24,1024]{2,1,0:T(8,128)(2,1)}), bf16[16,24,1024]{2,1,0:T(8,128)(2,1)S(1)}, u32[]{:S(2)}, u32[]{:S(2)}) async-start(bf16[16,24,1024]{2,1,0:T(8,128)(2,1)} %bitcast.17), calls=%async_computation.1 | async-start | bytes 1572864 | tf_op jit(solution)/shard_map/all_to_all | solution.py:220

commit v8 on v7

--- a/solution.py
+++ b/solution.py
@@ -95,12 +95,13 @@
 def socs_kernel(block, fields, weight_ref, low_ref, order_ref, first_ref, second_ref, *refs):
     field_refs, o_ref = refs[:fields], refs[-1]
     held = refs[fields] if len(refs) > fields + 1 else None
-    count, lines, pixels = field_refs[0].shape
-    half = count * lines // 2
-    rows = fields * half
-    left = jnp.concatenate([f[z + p] for p in (0, 1) for f in field_refs for z in range(0, count, 2)], axis=0)
+    pixels = field_refs[0].shape[2]
+    left = [f[z + p] for p in (0, 1) for f in field_refs for z in range(0, f.shape[0], 2)]
+    left = jnp.concatenate(left, axis=0)
+    rows = left.shape[0] // 2
     order = order_ref[...]
-    step = 2 * half // ANG
+    size = order.shape[0]
+    step = size // ANG
     for n in range(0, pixels, block):
         cols = slice(n, n + block)
         total = jnp.zeros((rows, block), F32)
@@ -112,13 +113,13 @@
             total += re * re + im * im
         total = (total * weight_ref[0]).astype(BF)
         if held is None:
-            own = jnp.dot(order, total[: 2 * half], preferred_element_type=F32)
-            o_ref[: 2 * half, cols] = own.astype(BF)
-            o_ref[2 * half :, cols] = total[2 * half :]
+            own = jnp.dot(order, total[:size], preferred_element_type=F32)
+            o_ref[:size, cols] = own.astype(BF)
+            o_ref[size:, cols] = total[size:]
         else:
             low = low_ref[0]
-            own = held[: 2 * half, cols].astype(F32)
-            other = jnp.concatenate([held[2 * half :, cols], total], axis=0)
+            own = held[:size, cols].astype(F32)
+            other = jnp.concatenate([held[size:, cols], total], axis=0)
             other = jnp.dot(order, other, preferred_element_type=F32)
             for g in range(ANG):
                 o_ref[g, low, :, cols] = own[g * step : (g + 1) * step].astype(BF)
@@ -126,14 +127,14 @@
 
 
 def socs_image(weight, low, order, first, second, fields, held=()):
-    count, lines, pixels = fields[0].shape
-    half = count * lines // 2
+    pixels = fields[0].shape[2]
+    rows = sum(f.shape[0] * f.shape[1] for f in fields) // 2
     scalar = pl.BlockSpec(memory_space=pltpu.SMEM)
     vmem = pl.BlockSpec(memory_space=pltpu.VMEM)
     if held:
-        out_shape = jax.ShapeDtypeStruct((ANG, 2, 2 * half // ANG, pixels), BF)
+        out_shape = jax.ShapeDtypeStruct((ANG, 2, order.shape[0] // ANG, pixels), BF)
     else:
-        out_shape = jax.ShapeDtypeStruct((len(fields) * half, pixels), BF)
+        out_shape = jax.ShapeDtypeStruct((rows, pixels), BF)
     return pl.pallas_call(
         functools.partial(socs_kernel, 256, len(fields)),
         out_shape=out_shape,
@@ -141,7 +142,7 @@
         out_specs=vmem,
         compiler_params=pltpu.CompilerParams(vmem_limit_bytes=20 << 20),
         cost_estimate=pl.CostEstimate(
-            flops=16 * len(fields) * half * pixels * pixels, bytes_accessed=9 << 20, transcendentals=0
+            flops=16 * rows * pixels * pixels, bytes_accessed=9 << 20, transcendentals=0
         ),
         name="socs_image",
     )(weight, low, order, first, second, *fields, *held)
@@ -198,24 +199,16 @@
             sibling = lax.ppermute(lax.optimization_barrier((mine, done))[0], "c", SWAP)
     near = jnp.concatenate(near, axis=0).reshape(LINES, ANG, 2, pixels).transpose(1, 2, 0, 3)
     near = lax.all_to_all(near, ("y", "xh"), 0, 0, tiled=True)
-    near = near.transpose(1, 2, 0, 3)
-    part = LINES // 2
-    own_a = lax.all_gather(near[:, :part], "z", axis=0, tiled=False)
-    other_a = lax.ppermute(own_a, "xl", SWAP)
-    rest = lax.optimization_barrier((near[:, part:], own_a))[0]
-    own_b = lax.all_gather(rest, "z", axis=0, tiled=False)
-    own_b, other_a = lax.optimization_barrier((own_b, other_a))
-    other_b = lax.ppermute(own_b, "xl", SWAP)
+    own = lax.all_gather(near.transpose(1, 2, 0, 3), "z", axis=0, tiled=False)
+    own = own.reshape(2 * depth, LINES * ANG, pixels)
+    other_a = lax.ppermute(own[:depth], "xl", SWAP)
+    other_b = lax.ppermute(own[depth:], "xl", SWAP)
     mine, sibling = resident(mine, sibling)
     low = lax.axis_index("xl").astype(jnp.int32).reshape(1)
-    order = np.eye(ANG * depth * LINES).reshape(2, depth, part, ANG, -1).transpose(3, 1, 0, 2, 4)
+    order = np.eye(ANG * depth * LINES).reshape(depth, LINES, ANG, -1).transpose(2, 0, 1, 3)
     order = jnp.asarray(order.reshape(ANG * depth * LINES, -1), BF)
-
-    def flat(block):
-        return block.reshape(2 * depth, part * ANG, pixels)
-
-    held = socs_image(weight, low, order, mine, sibling, [flat(own_a), flat(own_b), flat(other_a)])
-    images = socs_image(weight, low, order, mine, sibling, [flat(other_b)], (held,))
+    held = socs_image(weight, low, order, mine, sibling, [own, other_a])
+    images = socs_image(weight, low, order, mine, sibling, [other_b], (held,))
     images = images.reshape(2 * ANG, depth * LINES, pixels)
     pieces = lax.all_to_all(images, ("y", "xh", "xl"), 0, 0, tiled=True)
     total = jnp.sum(pieces.astype(F32), axis=0).reshape(depth, 2, OWN, pixels)

time: 120 us -> 114 us (0.950)
  blocking collectives: 61.1 us -> 49.7 us
  waiting for transfers between devices: 14.7 us -> 19.9 us
    all_gather x2 -> x1, blocking collectives: 32.9 us -> 21.8 us  [on_device(): own = lax.all_gather(near.transpose(1, 2, 0, 3), 'z', axis=0, tiled=False)]
    ppermute x2, waiting for transfers between devices: 0.01 us -> 5.14 us  [the longest x1 5.14 us: on_device(): other_a = lax.ppermute(own[:depth], 'xl', SWAP)]
  transfers between devices with their start and end apart: 6 -> 6, of which waited for: 2 -> 3; matrix products, arithmetic and copies ran while one was open for 2% -> 2% of each run, Pallas kernels for 17% -> 18%
where the time goes in v8:
time: 114 us; the launch traced here: 113 us
  blocking collectives  49.7 us (44%)
  Pallas kernels  27.4 us (24%)
  waiting for transfers between devices  19.9 us (17%)
  starting transfers between devices  8.3 us (7%)
  local copies, waits for them, and re-layouts  7.25 us (6%)
    all_gather x1, blocking collectives, on_device(): own = lax.all_gather(near.transpose(1, 2, 0, 3), 'z', axis=0, tiled=False)  21.8 us
    all_to_all x1, blocking collectives, on_device(): near = lax.all_to_all(near, ('y', 'xh'), 0, 0, tiled=True)  15.5 us
    pallas_call x3, Pallas kernels, conv_stage(): pl.pallas_call(functools.partial(conv_kernel, lines, done, before, pixels...  13.5 us
    all_to_all x1, blocking collectives, on_device(): total = lax.all_to_all(total, ('s', 'z'), 0, 0, tiled=True)  12.4 us
    all_to_all x1, waiting for transfers between devices, on_device(): pieces = lax.all_to_all(images, ('y', 'xh', 'xl'), 0, 0, tiled=True)  11.6 us
    pallas_call x2, Pallas kernels, socs_image(): pl.pallas_call(functools.partial(socs_kernel, 256, len(fields)), out_shap...  10.5 us
    ppermute x1, waiting for transfers between devices, on_device(): other_a = lax.ppermute(own[:depth], 'xl', SWAP)  5.14 us
    all_to_all x1, starting transfers between devices, on_device(): pieces = lax.all_to_all(images, ('y', 'xh', 'xl'), 0, 0, tiled=True)  3.81 us
  transfers between devices with their start and end apart: 6, of which 3 were waited for; matrix products, arithmetic and copies ran while one was open for 2% of the time, Pallas kernels for 18%

profile of v8, /device:TPU:32, one launch (start us, length us, event | category | flops | bytes accessed | tf_op | source)
XLA Modules:
  0.0 113.1 jit_solution(3797160496226624969)
XLA Ops:
  0.0 1.1 dynamic-slice_bitcast_fusion
  1.1 1.9 %collective-permute-start.1 = (bf16[2,1024,128]{2,1,0:T(8,128)(2,1)S(1)}, bf16[2,1024,128]{2,1,0:T(8,128)(2,1)S(1)}, u32[]{:S(2)}, u32[]{:S(2)}) collective-permute-start(bf16[2,1024,128]{2,1,0:T(8,128)(2,1)S(1)} %dynamic-slice_bitcast_fusion), channel_id=1, source_target_pairs={{0,128},{128,0},{1,129},{129,1},{2,130},{130,2},{3,131},{131,3},{4... | collective-permute-start | bytes 1572872 | tf_op jit(solution)/shard_map/ppermute | solution.py:186
  3.0 1.0 dynamic-slice_bitcast_fusion.1
  4.0 0.3 collective-permute-start
  4.3 1.4 %copy-done = bf16[1,6,1024,128]{3,2,1,0:T(8,128)(2,1)S(1)} copy-done((bf16[1,6,1024,128]{3,2,1,0:T(8,128)(2,1)S(1)}, bf16[1,6,1024,128]{3,2,1,0:T(8,128)(2,1)}, u32[]{:S(2)}) %copy-start) | copy-done | bytes 1572888
  5.7 1.1 %copy-done.2 = bf16[5,5,128,128]{3,2,1,0:T(8,128)(2,1)S(1)} copy-done((bf16[5,5,128,128]{3,2,1,0:T(8,128)(2,1)S(1)}, bf16[5,5,128,128]{3,2,1,0:T(8,128)(2,1)}, u32[]{:S(2)}) %copy-start.2) | copy-done | bytes 819224
  6.8 0.7 copy-done.4
  7.5 5.3 %conv_stage.3 = (bf16[1,16,1024]{2,1,0:T(8,128)(2,1)S(1)}, f32[4,1024,128]{2,1,0:T(8,128)S(1)}) custom-call(s32[1]{0:T(128)} %bitcast.2.flip_ref, bf16[6,1024,128]{2,1,0:T(8,128)(2,1)S(1)} %bitcast.42, bf16[5,640,128]{2,1,0:T(8,128)(2,1)S(1)} %bitcast.43, bf16[16,128]{1,0:T(8,128)(2,1)S(1)} %bitcast.46), custom_call_target="tpu_custom_call" | custom-call | flops 4026531840 | bytes 4194304 | tf_op jit(solution)/shard_map/conv_stage/pallas_call | solution.py:78
  12.8 3.2 %collective-permute-done.1.refs_0_ = bf16[2,1024,128]{2,1,0:T(8,128)(2,1)S(1)} collective-permute-done((bf16[2,1024,128]{2,1,0:T(8,128)(2,1)S(1)}, bf16[2,1024,128]{2,1,0:T(8,128)(2,1)S(1)}, u32[]{:S(2)}, u32[]{:S(2)}) %collective-permute-start.1) | collective-permute-done | bytes 524320 | tf_op jit(solution)/shard_map/ppermute | solution.py:186
  16.0 4.7 %conv_stage.4 = (bf16[2,16,1024]{2,1,0:T(8,128)(2,1)S(1)}, f32[3,1024,128]{2,1,0:T(8,128)S(1)}) custom-call(s32[1]{0:T(128)} %bitcast.2.flip_ref, bf16[2,1024,128]{2,1,0:T(8,128)(2,1)S(1)} %collective-permute-done.1.refs_0_, bf16[5,640,128]{2,1,0:T(8,128)(2,1)S(1)} %bitcast.44, bf16[16,128]{1,0:T(8,128)(2,1)S(1)} %bitcast.47, ...), custom_call_target="tpu_custom_call" | custom-call | flops 3019898880 | bytes 4194304 | tf_op jit(solution)/shard_map/conv_stage/pallas_call | solution.py:78
  20.7 3.5 %conv_stage.5 = bf16[3,16,1024]{2,1,0:T(8,128)(2,1)S(1)} custom-call(s32[1]{0:T(128)} %bitcast.2.flip_ref, bf16[1,1024,128]{2,1,0:T(8,128)(2,1)S(1)} %collective-permute-done.refs_0_, bf16[5,640,128]{2,1,0:T(8,128)(2,1)S(1)} %bitcast.45, bf16[16,128]{1,0:T(8,128)(2,1)S(1)} %bitcast.48, f32[3,1024,128]{2,1,0:T(8,128)S(1)} %get-tuple-element.13.refs_3_), custom_call_target="tpu_custom_call" | custom-call | flops 1006632960 | bytes 4194304 | tf_op jit(solution)/shard_map/conv_stage/pallas_call | solution.py:78
  24.2 0.2 collective-permute-start.2
  24.4 0.1 reshape.73
  24.5 0.1 copy.34
  24.7 15.5 %all_to_all.15 = bf16[8,2,6,1024]{3,1,2,0:T(2,128)(2,1)S(1)} all-to-all(bf16[8,2,6,1024]{3,1,2,0:T(2,128)(2,1)S(1)} %bitcast.49), channel_id=1, replica_groups=mesh['s'=2,'y'=4,'xh'=2,'xl'=2,'z'=4,'c'=2] {'y','xh'}, dimensions={0} | all-to-all | bytes 393216 | tf_op jit(solution)/shard_map/all_to_all | solution.py:201
  40.2 0.1 copy.26
  40.2 21.8 %all-gather = bf16[8,6,8,1024]{3,2,1,0:T(8,128)(2,1)S(1)} all-gather(bf16[2,6,8,1024]{3,2,1,0:T(8,128)(2,1)S(1)} %copy.26), channel_id=2, replica_groups=mesh['s'=2,'y'=4,'xh'=2,'xl'=2,'z'=4,'c'=2] {'z'}, dimensions={0}, use_global_device_ids=true | all-gather | bytes 983040 | tf_op jit(solution)/shard_map/all_gather | solution.py:202
  62.0 0.1 slice_bitcast_fusion
  62.1 0.7 collective-permute-start.4
  62.7 0.6 dynamic_slice.9.weight_ref
  63.3 1.5 %collective-permute-start.3 = (bf16[4,48,1024]{2,1,0:T(8,128)(2,1)S(1)}, bf16[4,48,1024]{2,1,0:T(8,128)(2,1)S(1)}, u32[]{:S(2)}, u32[]{:S(2)}) collective-permute-start(bf16[4,48,1024]{2,1,0:T(8,128)(2,1)S(1)} %get-tuple-element.20), channel_id=1, source_target_pairs={{0,8},{8,0},{1,9},{9,1},{2,10},{10,2},{3,11},{11,3},{4,12},{12,4},... | collective-permute-start | bytes 1179656 | tf_op jit(solution)/shard_map/ppermute | solution.py:205
  64.8 3.5 %resident.1 = (bf16[1024,2048]{1,0:T(8,128)(2,1)S(1)}, bf16[1024,2048]{1,0:T(8,128)(2,1)S(1)}) custom-call(bf16[1024,2048]{1,0:T(8,128)(2,1)} %bitcast.1.first_ref, bf16[1024,2048]{1,0:T(8,128)(2,1)} %collective-permute-done.2.second_ref), custom_call_target="tpu_custom_call" | custom-call | bytes 16777216 | tf_op jit(solution)/shard_map/resident/pallas_call | solution.py:163
  68.3 5.1 %collective-permute-done.4.refs_1_ = bf16[4,48,1024]{2,1,0:T(8,128)(2,1)S(1)} collective-permute-done((bf16[4,48,1024]{2,1,0:T(8,128)(2,1)S(1)}, bf16[4,48,1024]{2,1,0:T(8,128)(2,1)S(1)}, u32[]{:S(2)}, u32[]{:S(2)}) %collective-permute-start.4) | collective-permute-done | bytes 393248 | tf_op jit(solution)/shard_map/ppermute | solution.py:204
  73.4 6.4 %socs_image.2.refs_1_ = bf16[288,1024]{1,0:T(8,128)(2,1)S(1)} custom-call(f32[1]{0:T(128)} %dynamic_slice.9.weight_ref, s32[1]{0:T(128)} %bitcast.low_ref, bf16[192,192]{1,0:T(8,128)(2,1)S(1)} %copy-done.1, bf16[1024,2048]{1,0:T(8,128)(2,1)S(1)} %get-tuple-element.15.first_ref, bf16[1024,2048]{1,0:T(8,128)(2,1)S(1)} %get-tuple-element.16.second_ref, ...), custom_call_target="tpu_custom_call" | custom-call | flops 4831838208 | bytes 9437184 | tf_op jit(solution)/shard_map/socs_image/pallas_call | solution.py:138
  79.8 4.1 %socs_image.3 = bf16[8,2,24,1024]{3,2,1,0:T(8,128)(2,1)} custom-call(f32[1]{0:T(128)} %dynamic_slice.9.weight_ref, s32[1]{0:T(128)} %bitcast.low_ref, bf16[192,192]{1,0:T(8,128)(2,1)S(1)} %copy-done.1, bf16[1024,2048]{1,0:T(8,128)(2,1)S(1)} %get-tuple-element.15.first_ref, bf16[1024,2048]{1,0:T(8,128)(2,1)S(1)} %get-tuple-element.16.second_ref, ...), custom_call_target="tpu_custom_call" | custom-call | flops 1610612736 | bytes 9437184 | tf_op jit(solution)/shard_map/socs_image/pallas_call | solution.py:138
  83.9 3.8 %all-to-all-start.1 = ((bf16[16,24,1024]{2,1,0:T(8,128)(2,1)}), bf16[16,24,1024]{2,1,0:T(8,128)(2,1)S(1)}, u32[]{:S(2)}, u32[]{:S(2)}) async-start(bf16[16,24,1024]{2,1,0:T(8,128)(2,1)} %bitcast.14), calls=%async_computation.1 | async-start | bytes 1572864 | tf_op jit(solution)/shard_map/all_to_all | solution.py:213
  87.7 11.6 %all-to-all-done.1 = bf16[16,24,1024]{2,1,0:T(8,128)(2,1)S(1)} async-done(((bf16[16,24,1024]{2,1,0:T(8,128)(2,1)}), bf16[16,24,1024]{2,1,0:T(8,128)(2,1)S(1)}, u32[]{:S(2)}, u32[]{:S(2)}) %all-to-all-start.1) | async-done | bytes 786464 | tf_op jit(solution)/shard_map/all_to_all | solution.py:213
  99.3 0.1 convert_reduce_fusion
  99.6 0.1 reshape.77
  99.7 12.4 %all_to_all.16 = f32[8,24,128]{2,1,0:T(8,128)S(1)} all-to-all(f32[8,24,128]{2,1,0:T(8,128)S(1)} %reshape.77), channel_id=1, replica_groups=mesh['s'=2,'y'=4,'xh'=2,'xl'=2,'z'=4,'c'=2] {'s','z'}, dimensions={0} | all-to-all | bytes 196608 | tf_op jit(solution)/shard_map/all_to_all | solution.py:219
  112.1 0.2 rev.3
  112.4 0.6 reshape.79
  (25 shorter events, 0.3 us)
Async XLA Ops:
  1.1 14.9 %collective-permute-start.1 = (bf16[2,1024,128]{2,1,0:T(8,128)(2,1)S(1)}, bf16[2,1024,128]{2,1,0:T(8,128)(2,1)S(1)}, u32[]{:S(2)}, u32[]{:S(2)}) collective-permute-start(bf16[2,1024,128]{2,1,0:T(8,128)(2,1)S(1)} %dynamic-slice_bitcast_fusion), channel_id=1, source_target_pairs={{0,128},{128,0},{1,129},{129,1},{2,130},{130,2},{3,131},{131,3},{4... | collective-permute-start | bytes 1572872 | tf_op jit(solution)/shard_map/ppermute | solution.py:186
  4.0 16.8 %collective-permute-start = (bf16[1,1024,128]{2,1,0:T(8,128)(2,1)S(1)}, bf16[1,1024,128]{2,1,0:T(8,128)(2,1)S(1)}, u32[]{:S(2)}, u32[]{:S(2)}) collective-permute-start(bf16[1,1024,128]{2,1,0:T(8,128)(2,1)S(1)} %dynamic-slice_bitcast_fusion.1), channel_id=1, source_target_pairs={{0,128},{128,0},{1,129},{129,1},{2,130},{130,2},{3,131},{131,3},{4... | collective-permute-start | bytes 786440 | tf_op jit(solution)/shard_map/ppermute | solution.py:186
  4.3 1.4 %copy-start = (bf16[1,6,1024,128]{3,2,1,0:T(8,128)(2,1)S(1)}, bf16[1,6,1024,128]{3,2,1,0:T(8,128)(2,1)}, u32[]{:S(2)}) copy-start(bf16[1,6,1024,128]{3,2,1,0:T(8,128)(2,1)} %param.6) | copy-start | bytes 4718596
  5.7 1.1 %copy-start.2 = (bf16[5,5,128,128]{3,2,1,0:T(8,128)(2,1)S(1)}, bf16[5,5,128,128]{3,2,1,0:T(8,128)(2,1)}, u32[]{:S(2)}) copy-start(bf16[5,5,128,128]{3,2,1,0:T(8,128)(2,1)} %param.7) | copy-start | bytes 2457604
  6.8 0.7 copy-start.4
  7.5 8.5 %copy-start.3 = (bf16[5,5,128,128]{3,2,1,0:T(8,128)(2,1)S(1)}, bf16[5,5,128,128]{3,2,1,0:T(8,128)(2,1)}, u32[]{:S(2)}) copy-start(bf16[5,5,128,128]{3,2,1,0:T(8,128)(2,1)} %param.7) | copy-start | bytes 2457604
  7.5 8.5 %copy-start.5 = (bf16[128,16]{0,1:T(8,128)(2,1)S(1)}, bf16[128,16]{0,1:T(8,128)(2,1)}, u32[]{:S(2)}) copy-start(bf16[128,16]{0,1:T(8,128)(2,1)} %param.8) | copy-start | bytes 12292
  24.2 40.6 %collective-permute-start.2 = (bf16[1024,2048]{1,0:T(8,128)(2,1)}, bf16[1024,2048]{1,0:T(8,128)(2,1)}, u32[]{:S(2)}, u32[]{:S(2)}) collective-permute-start(bf16[1024,2048]{1,0:T(8,128)(2,1)} %bitcast.1.first_ref), channel_id=1, source_target_pairs={{0,1},{1,0},{2,3},{3,2},{4,5},{5,4},{6,7},{7,6},{8,9},{9,8},{10,11... | collective-permute-start | bytes 12582920 | tf_op jit(solution)/shard_map/ppermute | solution.py:199
  24.4 38.3 %copy-start.6 = (f32[8]{0:T(128)S(1)}, f32[8]{0:T(128)}, u32[]{:S(2)}) copy-start(f32[8]{0:T(128)} %param.10) | copy-start | bytes 100
  62.1 11.3 %collective-permute-start.4 = (bf16[4,48,1024]{2,1,0:T(8,128)(2,1)S(1)}, bf16[4,48,1024]{2,1,0:T(8,128)(2,1)S(1)}, u32[]{:S(2)}, u32[]{:S(2)}) collective-permute-start(bf16[4,48,1024]{2,1,0:T(8,128)(2,1)S(1)} %get-tuple-element.19), channel_id=1, source_target_pairs={{0,8},{8,0},{1,9},{9,1},{2,10},{10,2},{3,11},{11,3},{4,12},{12,4},... | collective-permute-start | bytes 1179656 | tf_op jit(solution)/shard_map/ppermute | solution.py:204
  63.3 10.1 %copy-start.1 = (bf16[192,192]{1,0:T(8,128)(2,1)S(1)}, bf16[192,192]{1,0:T(8,128)(2,1)}, u32[]{:S(2)}) copy-start(bf16[192,192]{1,0:T(8,128)(2,1)} %constant.36.clone.order_ref) | copy-start | bytes 221188
  63.3 16.5 %collective-permute-start.3 = (bf16[4,48,1024]{2,1,0:T(8,128)(2,1)S(1)}, bf16[4,48,1024]{2,1,0:T(8,128)(2,1)S(1)}, u32[]{:S(2)}, u32[]{:S(2)}) collective-permute-start(bf16[4,48,1024]{2,1,0:T(8,128)(2,1)S(1)} %get-tuple-element.20), channel_id=1, source_target_pairs={{0,8},{8,0},{1,9},{9,1},{2,10},{10,2},{3,11},{11,3},{4,12},{12,4},... | collective-permute-start | bytes 1179656 | tf_op jit(solution)/shard_map/ppermute | solution.py:205
  83.9 15.4 %all-to-all-start.1 = ((bf16[16,24,1024]{2,1,0:T(8,128)(2,1)}), bf16[16,24,1024]{2,1,0:T(8,128)(2,1)S(1)}, u32[]{:S(2)}, u32[]{:S(2)}) async-start(bf16[16,24,1024]{2,1,0:T(8,128)(2,1)} %bitcast.14), calls=%async_computation.1 | async-start | bytes 1572864 | tf_op jit(solution)/shard_map/all_to_all | solution.py:213

commit v9 on v8

--- a/solution.py
+++ b/solution.py
@@ -92,9 +92,9 @@
     return out[0], list(out[1:])
 
 
-def socs_kernel(block, fields, weight_ref, low_ref, order_ref, first_ref, second_ref, *refs):
+def socs_kernel(block, fields, last, weight_ref, low_ref, order_ref, first_ref, second_ref, *refs):
     field_refs, o_ref = refs[:fields], refs[-1]
-    held = refs[fields] if len(refs) > fields + 1 else None
+    held = refs[fields:-1]
     pixels = field_refs[0].shape[2]
     left = [f[z + p] for p in (0, 1) for f in field_refs for z in range(0, f.shape[0], 2)]
     left = jnp.concatenate(left, axis=0)
@@ -112,14 +112,17 @@
             im = by_im[:rows] + by_re[rows:]
             total += re * re + im * im
         total = (total * weight_ref[0]).astype(BF)
-        if held is None:
-            own = jnp.dot(order, total[:size], preferred_element_type=F32)
-            o_ref[:size, cols] = own.astype(BF)
-            o_ref[size:, cols] = total[size:]
+        if not last:
+            if rows >= size:
+                own = jnp.dot(order, total[:size], preferred_element_type=F32)
+                o_ref[:size, cols] = own.astype(BF)
+                o_ref[size:, cols] = total[size:]
+            else:
+                o_ref[:, cols] = total
         else:
             low = low_ref[0]
-            own = held[:size, cols].astype(F32)
-            other = jnp.concatenate([held[size:, cols], total], axis=0)
+            own = held[0][:size, cols].astype(F32)
+            other = jnp.concatenate([held[0][size:, cols], held[1][:, cols], total], axis=0)
             other = jnp.dot(order, other, preferred_element_type=F32)
             for g in range(ANG):
                 o_ref[g, low, :, cols] = own[g * step : (g + 1) * step].astype(BF)
@@ -136,7 +139,7 @@
     else:
         out_shape = jax.ShapeDtypeStruct((rows, pixels), BF)
     return pl.pallas_call(
-        functools.partial(socs_kernel, 256, len(fields)),
+        functools.partial(socs_kernel, 256, len(fields), bool(held)),
         out_shape=out_shape,
         in_specs=[scalar, scalar] + [vmem] * (3 + len(fields) + len(held)),
         out_specs=vmem,
@@ -199,16 +202,28 @@
             sibling = lax.ppermute(lax.optimization_barrier((mine, done))[0], "c", SWAP)
     near = jnp.concatenate(near, axis=0).reshape(LINES, ANG, 2, pixels).transpose(1, 2, 0, 3)
     near = lax.all_to_all(near, ("y", "xh"), 0, 0, tiled=True)
-    own = lax.all_gather(near.transpose(1, 2, 0, 3), "z", axis=0, tiled=False)
-    own = own.reshape(2 * depth, LINES * ANG, pixels)
-    other_a = lax.ppermute(own[:depth], "xl", SWAP)
-    other_b = lax.ppermute(own[depth:], "xl", SWAP)
+    near = near.transpose(1, 2, 0, 3).reshape(2, LINES * ANG, pixels)
+    early = lax.ppermute(near, "xl", SWAP)
+    own = lax.all_gather(near, "z", axis=0, tiled=True)
+    own, early = lax.optimization_barrier((own, early))
+    at = lax.axis_index("z")
+
+    def ahead(k):
+        return lax.dynamic_slice_in_dim(own, 2 * lax.rem(at + k, depth), 2, 0)
+
+    other_a = lax.ppermute(jnp.concatenate([ahead(1), ahead(2)], axis=0), "xl", SWAP)
+    other_b = lax.ppermute(ahead(3), "xl", SWAP)
     mine, sibling = resident(mine, sibling)
     low = lax.axis_index("xl").astype(jnp.int32).reshape(1)
     order = np.eye(ANG * depth * LINES).reshape(depth, LINES, ANG, -1).transpose(2, 0, 1, 3)
-    order = jnp.asarray(order.reshape(ANG * depth * LINES, -1), BF)
-    held = socs_image(weight, low, order, mine, sibling, [own, other_a])
-    images = socs_image(weight, low, order, mine, sibling, [other_b], (held,))
+    order = order.reshape(ANG * depth * LINES, -1)
+    width = LINES * ANG
+    shifted = jnp.asarray(np.concatenate([order, order], axis=1).reshape(-1, 2 * depth, width).transpose(1, 0, 2), BF)
+    shifted = lax.dynamic_slice_in_dim(shifted, at, depth, 0).transpose(1, 0, 2).reshape(order.shape)
+    order = jnp.asarray(order, BF)
+    held_a = socs_image(weight, low, order, mine, sibling, [own, early])
+    held_b = socs_image(weight, low, order, mine, sibling, [other_a])
+    images = socs_image(weight, low, shifted, mine, sibling, [other_b], (held_a, held_b))
     images = images.reshape(2 * ANG, depth * LINES, pixels)
     pieces = lax.all_to_all(images, ("y", "xh", "xl"), 0, 0, tiled=True)
     total = jnp.sum(pieces.astype(F32), axis=0).reshape(depth, 2, OWN, pixels)

time: 114 us -> 111 us (0.974)
  blocking collectives: 49.7 us -> 33.4 us
  starting transfers between devices: 8.3 us -> 16.6 us
  waiting for transfers between devices: 19.9 us -> 23.5 us
  Pallas kernels: 27.4 us -> 28.7 us
    all_to_all x1 -> x0, blocking collectives: 15.5 us -> none  [on_device(): near = lax.all_to_all(near, ('y', 'xh'), 0, 0, tiled=True)]
    all_to_all x0 -> x1, waiting for transfers between devices: none -> 8.76 us  [on_device(): near = lax.all_to_all(near, ('y', 'xh'), 0, 0, tiled=True)]
    all_to_all x0 -> x1, starting transfers between devices: none -> 7.06 us  [on_device(): near = lax.all_to_all(near, ('y', 'xh'), 0, 0, tiled=True)]
    ppermute x2 -> x3, waiting for transfers between devices: 5.14 us -> 0.01 us  [the longest x1 0.01 us: on_device(): early = lax.ppermute(near, 'xl', SWAP)]
    pallas_call x2 -> x3, Pallas kernels: 10.5 us -> 11.7 us  [socs_image(): pl.pallas_call(functools.partial(socs_kernel, 256, len(fields), bool(held...]
    ppermute x2 -> x3, starting transfers between devices: 2.11 us -> 2.8 us  [the longest x1 1.45 us: on_device(): lax.ppermute(jnp.concatenate([ahead(1), ahead(2)], axis=0), 'xl', SWAP)]
    unnamed x14 -> x16, local copies, waits for them, and re-layouts: 3.26 us -> 3.26 us
  transfers between devices with their start and end apart: 6 -> 8, of which waited for: 3 -> 3; matrix products, arithmetic and copies ran while one was open for 2% -> 2% of each run, Pallas kernels for 18% -> 19%
where the time goes in v9:
time: 111 us
  blocking collectives  33.4 us (30%)
  Pallas kernels  28.7 us (26%)
  waiting for transfers between devices  23.5 us (21%)
  starting transfers between devices  16.6 us (15%)
  local copies, waits for them, and re-layouts  8.03 us (7%)
    all_gather x1, blocking collectives, on_device(): own = lax.all_gather(near, 'z', axis=0, tiled=True)  21.2 us
    pallas_call x3, Pallas kernels, conv_stage(): pl.pallas_call(functools.partial(conv_kernel, lines, done, before, pixels...  13.5 us
    all_to_all x1, blocking collectives, on_device(): total = lax.all_to_all(total, ('s', 'z'), 0, 0, tiled=True)  12.2 us
    pallas_call x3, Pallas kernels, socs_image(): pl.pallas_call(functools.partial(socs_kernel, 256, len(fields), bool(held...  11.7 us
    all_to_all x1, waiting for transfers between devices, on_device(): pieces = lax.all_to_all(images, ('y', 'xh', 'xl'), 0, 0, tiled=True)  11.6 us
    all_to_all x1, waiting for transfers between devices, on_device(): near = lax.all_to_all(near, ('y', 'xh'), 0, 0, tiled=True)  8.76 us
    all_to_all x1, starting transfers between devices, on_device(): near = lax.all_to_all(near, ('y', 'xh'), 0, 0, tiled=True)  7.06 us
    all_to_all x1, starting transfers between devices, on_device(): pieces = lax.all_to_all(images, ('y', 'xh', 'xl'), 0, 0, tiled=True)  4.37 us
  transfers between devices with their start and end apart: 8, of which 3 were waited for; matrix products, arithmetic and copies ran while one was open for 2% of the time, Pallas kernels for 19%

profile of v9, /device:TPU:32, one launch (start us, length us, event | category | flops | bytes accessed | tf_op | source)
XLA Modules:
  0.0 110.8 jit_solution(8934320381361214063)
XLA Ops:
  0.0 1.1 dynamic-slice_bitcast_fusion
  1.1 1.9 %collective-permute-start.1 = (bf16[2,1024,128]{2,1,0:T(8,128)(2,1)S(1)}, bf16[2,1024,128]{2,1,0:T(8,128)(2,1)S(1)}, u32[]{:S(2)}, u32[]{:S(2)}) collective-permute-start(bf16[2,1024,128]{2,1,0:T(8,128)(2,1)S(1)} %dynamic-slice_bitcast_fusion), channel_id=1, source_target_pairs={{0,128},{128,0},{1,129},{129,1},{2,130},{130,2},{3,131},{131,3},{4... | collective-permute-start | bytes 1572872 | tf_op jit(solution)/shard_map/ppermute | solution.py:189
  3.0 1.0 dynamic-slice_bitcast_fusion.1
  4.0 0.3 collective-permute-start
  4.3 1.4 %copy-done = bf16[1,6,1024,128]{3,2,1,0:T(8,128)(2,1)S(1)} copy-done((bf16[1,6,1024,128]{3,2,1,0:T(8,128)(2,1)S(1)}, bf16[1,6,1024,128]{3,2,1,0:T(8,128)(2,1)}, u32[]{:S(2)}) %copy-start) | copy-done | bytes 1572888
  5.7 1.1 %copy-done.2 = bf16[5,5,128,128]{3,2,1,0:T(8,128)(2,1)S(1)} copy-done((bf16[5,5,128,128]{3,2,1,0:T(8,128)(2,1)S(1)}, bf16[5,5,128,128]{3,2,1,0:T(8,128)(2,1)}, u32[]{:S(2)}) %copy-start.2) | copy-done | bytes 819224
  6.8 0.7 copy-done.4
  7.5 5.3 %conv_stage.3 = (bf16[1,16,1024]{2,1,0:T(8,128)(2,1)S(1)}, f32[4,1024,128]{2,1,0:T(8,128)S(1)}) custom-call(s32[1]{0:T(128)} %bitcast.4.flip_ref, bf16[6,1024,128]{2,1,0:T(8,128)(2,1)S(1)} %bitcast.42, bf16[5,640,128]{2,1,0:T(8,128)(2,1)S(1)} %bitcast.43, bf16[16,128]{1,0:T(8,128)(2,1)S(1)} %bitcast.46), custom_call_target="tpu_custom_call" | custom-call | flops 4026531840 | bytes 4194304 | tf_op jit(solution)/shard_map/conv_stage/pallas_call | solution.py:78
  12.8 3.2 %collective-permute-done.1.refs_0_ = bf16[2,1024,128]{2,1,0:T(8,128)(2,1)S(1)} collective-permute-done((bf16[2,1024,128]{2,1,0:T(8,128)(2,1)S(1)}, bf16[2,1024,128]{2,1,0:T(8,128)(2,1)S(1)}, u32[]{:S(2)}, u32[]{:S(2)}) %collective-permute-start.1) | collective-permute-done | bytes 524320 | tf_op jit(solution)/shard_map/ppermute | solution.py:189
  16.0 4.7 %conv_stage.4 = (bf16[2,16,1024]{2,1,0:T(8,128)(2,1)S(1)}, f32[3,1024,128]{2,1,0:T(8,128)S(1)}) custom-call(s32[1]{0:T(128)} %bitcast.4.flip_ref, bf16[2,1024,128]{2,1,0:T(8,128)(2,1)S(1)} %collective-permute-done.1.refs_0_, bf16[5,640,128]{2,1,0:T(8,128)(2,1)S(1)} %bitcast.44, bf16[16,128]{1,0:T(8,128)(2,1)S(1)} %bitcast.47, ...), custom_call_target="tpu_custom_call" | custom-call | flops 3019898880 | bytes 4194304 | tf_op jit(solution)/shard_map/conv_stage/pallas_call | solution.py:78
  20.7 3.5 %conv_stage.5 = bf16[3,16,1024]{2,1,0:T(8,128)(2,1)S(1)} custom-call(s32[1]{0:T(128)} %bitcast.4.flip_ref, bf16[1,1024,128]{2,1,0:T(8,128)(2,1)S(1)} %collective-permute-done.refs_0_, bf16[5,640,128]{2,1,0:T(8,128)(2,1)S(1)} %bitcast.45, bf16[16,128]{1,0:T(8,128)(2,1)S(1)} %bitcast.48, f32[3,1024,128]{2,1,0:T(8,128)S(1)} %get-tuple-element.15.refs_3_), custom_call_target="tpu_custom_call" | custom-call | flops 1006632960 | bytes 4194304 | tf_op jit(solution)/shard_map/conv_stage/pallas_call | solution.py:78
  24.2 0.2 collective-permute-start.2
  24.4 0.1 reshape.75
  24.5 0.8 copy.40
  25.3 7.1 %all-to-all-start = ((bf16[8,2,6,1024]{3,1,2,0:T(2,128)(2,1)}), bf16[8,2,6,1024]{3,1,2,0:T(2,128)(2,1)S(1)}, u32[]{:S(2)}, u32[]{:S(2)}) async-start(bf16[8,2,6,1024]{3,1,2,0:T(2,128)(2,1)} %bitcast.39), calls=%async_computation | async-start | bytes 393216 | tf_op jit(solution)/shard_map/all_to_all | solution.py:204
  32.4 8.8 %all-to-all-done = bf16[8,2,6,1024]{3,1,2,0:T(2,128)(2,1)S(1)} async-done(((bf16[8,2,6,1024]{3,1,2,0:T(2,128)(2,1)}), bf16[8,2,6,1024]{3,1,2,0:T(2,128)(2,1)S(1)}, u32[]{:S(2)}, u32[]{:S(2)}) %all-to-all-start) | async-done | bytes 196640 | tf_op jit(solution)/shard_map/all_to_all | solution.py:204
  41.2 0.7 collective-permute-start.3
  41.9 21.2 %all_gather.3.refs_0_ = bf16[8,48,1024]{2,1,0:T(8,128)(2,1)S(1)} all-gather(bf16[2,48,1024]{2,1,0:T(8,128)(2,1)S(1)} %bitcast.51), channel_id=1, replica_groups=mesh['s'=2,'y'=4,'xh'=2,'xl'=2,'z'=4,'c'=2] {'z'}, dimensions={0}, use_global_device_ids=true | all-gather | bytes 983040 | tf_op jit(solution)/shard_map/all_gather | solution.py:207
  63.2 1.4 %collective-permute-start.5 = (bf16[4,48,1024]{2,1,0:T(8,128)(2,1)S(1)}, bf16[4,48,1024]{2,1,0:T(8,128)(2,1)S(1)}, u32[]{:S(2)}, u32[]{:S(2)}) collective-permute-start(bf16[4,48,1024]{2,1,0:T(8,128)(2,1)S(1)} %pad_maximum_fusion), channel_id=1, source_target_pairs={{0,8},{8,0},{1,9},{9,1},{2,10},{10,2},{3,11},{11,3},{4,12},{12,4},... | collective-permute-start | bytes 1179656 | tf_op jit(solution)/shard_map/ppermute | solution.py:214
  64.7 0.1 copy.30.order_ref
  64.8 0.6 dynamic_slice.21.weight_ref
  65.4 0.7 collective-permute-start.4
  66.1 3.5 %resident.1 = (bf16[1024,2048]{1,0:T(8,128)(2,1)S(1)}, bf16[1024,2048]{1,0:T(8,128)(2,1)S(1)}) custom-call(bf16[1024,2048]{1,0:T(8,128)(2,1)} %bitcast.3.first_ref, bf16[1024,2048]{1,0:T(8,128)(2,1)} %collective-permute-done.2.second_ref), custom_call_target="tpu_custom_call" | custom-call | bytes 16777216 | tf_op jit(solution)/shard_map/resident/pallas_call | solution.py:166
  69.6 5.6 %socs_image.3.refs_1_ = bf16[240,1024]{1,0:T(8,128)(2,1)S(1)} custom-call(f32[1]{0:T(128)} %dynamic_slice.21.weight_ref, s32[1]{0:T(128)} %bitcast.low_ref, bf16[192,192]{1,0:T(8,128)(2,1)S(1)} %copy-done.1, bf16[1024,2048]{1,0:T(8,128)(2,1)S(1)} %get-tuple-element.17.first_ref, bf16[1024,2048]{1,0:T(8,128)(2,1)S(1)} %get-tuple-element.18.second_ref, ...), custom_call_target="tpu_custom_call" | custom-call | flops 4026531840 | bytes 9437184 | tf_op jit(solution)/shard_map/socs_image/pallas_call | solution.py:141
  75.2 2.5 %socs_image.4.refs_2_ = bf16[96,1024]{1,0:T(8,128)(2,1)S(1)} custom-call(f32[1]{0:T(128)} %dynamic_slice.21.weight_ref, s32[1]{0:T(128)} %bitcast.low_ref, bf16[192,192]{1,0:T(8,128)(2,1)S(1)} %copy-done.1, bf16[1024,2048]{1,0:T(8,128)(2,1)S(1)} %get-tuple-element.17.first_ref, bf16[1024,2048]{1,0:T(8,128)(2,1)S(1)} %get-tuple-element.18.second_ref, ...), custom_call_target="tpu_custom_call" | custom-call | flops 1610612736 | bytes 9437184 | tf_op jit(solution)/shard_map/socs_image/pallas_call | solution.py:141
  77.7 3.6 %socs_image.5 = bf16[8,2,24,1024]{3,2,1,0:T(8,128)(2,1)} custom-call(f32[1]{0:T(128)} %dynamic_slice.21.weight_ref, s32[1]{0:T(128)} %bitcast.low_ref, bf16[192,192]{1,0:T(8,128)(2,1)S(1)} %copy.30.order_ref, bf16[1024,2048]{1,0:T(8,128)(2,1)S(1)} %get-tuple-element.17.first_ref, bf16[1024,2048]{1,0:T(8,128)(2,1)S(1)} %get-tuple-element.18.second_ref, ...), custom_call_target="tpu_custom_call" | custom-call | flops 805306368 | bytes 9437184 | tf_op jit(solution)/shard_map/socs_image/pallas_call | solution.py:141
  81.3 4.4 %all-to-all-start.1 = ((bf16[16,24,1024]{2,1,0:T(8,128)(2,1)}), bf16[16,24,1024]{2,1,0:T(8,128)(2,1)S(1)}, u32[]{:S(2)}, u32[]{:S(2)}) async-start(bf16[16,24,1024]{2,1,0:T(8,128)(2,1)} %bitcast.14), calls=%async_computation.1 | async-start | bytes 1572864 | tf_op jit(solution)/shard_map/all_to_all | solution.py:228
  85.7 11.6 %all-to-all-done.1 = bf16[16,24,1024]{2,1,0:T(8,128)(2,1)S(1)} async-done(((bf16[16,24,1024]{2,1,0:T(8,128)(2,1)}), bf16[16,24,1024]{2,1,0:T(8,128)(2,1)S(1)}, u32[]{:S(2)}, u32[]{:S(2)}) %all-to-all-start.1) | async-done | bytes 786464 | tf_op jit(solution)/shard_map/all_to_all | solution.py:228
  97.2 0.1 convert_reduce_fusion
  97.6 12.2 %all_to_all.15 = f32[8,24,128]{2,1,0:T(8,128)S(1)} all-to-all(f32[8,24,128]{2,1,0:T(8,128)S(1)} %reshape.79), channel_id=1, replica_groups=mesh['s'=2,'y'=4,'xh'=2,'xl'=2,'z'=4,'c'=2] {'s','z'}, dimensions={0} | all-to-all | bytes 196608 | tf_op jit(solution)/shard_map/all_to_all | solution.py:234
  109.9 0.2 rev.3
  110.2 0.6 reshape.81
  (34 shorter events, 0.5 us)
Async XLA Ops:
  1.1 14.9 %collective-permute-start.1 = (bf16[2,1024,128]{2,1,0:T(8,128)(2,1)S(1)}, bf16[2,1024,128]{2,1,0:T(8,128)(2,1)S(1)}, u32[]{:S(2)}, u32[]{:S(2)}) collective-permute-start(bf16[2,1024,128]{2,1,0:T(8,128)(2,1)S(1)} %dynamic-slice_bitcast_fusion), channel_id=1, source_target_pairs={{0,128},{128,0},{1,129},{129,1},{2,130},{130,2},{3,131},{131,3},{4... | collective-permute-start | bytes 1572872 | tf_op jit(solution)/shard_map/ppermute | solution.py:189
  4.0 16.8 %collective-permute-start = (bf16[1,1024,128]{2,1,0:T(8,128)(2,1)S(1)}, bf16[1,1024,128]{2,1,0:T(8,128)(2,1)S(1)}, u32[]{:S(2)}, u32[]{:S(2)}) collective-permute-start(bf16[1,1024,128]{2,1,0:T(8,128)(2,1)S(1)} %dynamic-slice_bitcast_fusion.1), channel_id=1, source_target_pairs={{0,128},{128,0},{1,129},{129,1},{2,130},{130,2},{3,131},{131,3},{4... | collective-permute-start | bytes 786440 | tf_op jit(solution)/shard_map/ppermute | solution.py:189
  4.3 1.4 %copy-start = (bf16[1,6,1024,128]{3,2,1,0:T(8,128)(2,1)S(1)}, bf16[1,6,1024,128]{3,2,1,0:T(8,128)(2,1)}, u32[]{:S(2)}) copy-start(bf16[1,6,1024,128]{3,2,1,0:T(8,128)(2,1)} %param.7) | copy-start | bytes 4718596
  5.7 1.1 %copy-start.2 = (bf16[5,5,128,128]{3,2,1,0:T(8,128)(2,1)S(1)}, bf16[5,5,128,128]{3,2,1,0:T(8,128)(2,1)}, u32[]{:S(2)}) copy-start(bf16[5,5,128,128]{3,2,1,0:T(8,128)(2,1)} %param.8) | copy-start | bytes 2457604
  6.8 0.7 copy-start.4
  7.5 8.5 %copy-start.3 = (bf16[5,5,128,128]{3,2,1,0:T(8,128)(2,1)S(1)}, bf16[5,5,128,128]{3,2,1,0:T(8,128)(2,1)}, u32[]{:S(2)}) copy-start(bf16[5,5,128,128]{3,2,1,0:T(8,128)(2,1)} %param.8) | copy-start | bytes 2457604
  7.5 8.5 %copy-start.5 = (bf16[128,16]{0,1:T(8,128)(2,1)S(1)}, bf16[128,16]{0,1:T(8,128)(2,1)}, u32[]{:S(2)}) copy-start(bf16[128,16]{0,1:T(8,128)(2,1)} %param.9) | copy-start | bytes 12292
  24.2 41.8 %collective-permute-start.2 = (bf16[1024,2048]{1,0:T(8,128)(2,1)}, bf16[1024,2048]{1,0:T(8,128)(2,1)}, u32[]{:S(2)}, u32[]{:S(2)}) collective-permute-start(bf16[1024,2048]{1,0:T(8,128)(2,1)} %bitcast.3.first_ref), channel_id=1, source_target_pairs={{0,1},{1,0},{2,3},{3,2},{4,5},{5,4},{6,7},{7,6},{8,9},{9,8},{10,11... | collective-permute-start | bytes 12582920 | tf_op jit(solution)/shard_map/ppermute | solution.py:202
  24.5 40.1 %copy-start.6 = (bf16[8,192,48]{1,2,0:T(8,128)(2,1)S(1)}, bf16[8,192,48]{1,2,0:T(8,128)(2,1)}, u32[]{:S(2)}) copy-start(bf16[8,192,48]{1,2,0:T(8,128)(2,1)} %constant.47.clone) | copy-start | bytes 442372
  25.3 39.5 %copy-start.7 = (f32[8]{0:T(128)S(1)}, f32[8]{0:T(128)}, u32[]{:S(2)}) copy-start(f32[8]{0:T(128)} %param.11) | copy-start | bytes 100
  25.3 15.8 %all-to-all-start = ((bf16[8,2,6,1024]{3,1,2,0:T(2,128)(2,1)}), bf16[8,2,6,1024]{3,1,2,0:T(2,128)(2,1)S(1)}, u32[]{:S(2)}, u32[]{:S(2)}) async-start(bf16[8,2,6,1024]{3,1,2,0:T(2,128)(2,1)} %bitcast.39), calls=%async_computation | async-start | bytes 393216 | tf_op jit(solution)/shard_map/all_to_all | solution.py:204
  41.2 21.9 %collective-permute-start.3 = (bf16[2,48,1024]{2,1,0:T(8,128)(2,1)S(1)}, bf16[2,48,1024]{2,1,0:T(8,128)(2,1)S(1)}, u32[]{:S(2)}, u32[]{:S(2)}) collective-permute-start(bf16[2,48,1024]{2,1,0:T(8,128)(2,1)S(1)} %bitcast.50), channel_id=1, source_target_pairs={{0,8},{8,0},{1,9},{9,1},{2,10},{10,2},{3,11},{11,3},{4,12},{12,4},... | collective-permute-start | bytes 589832 | tf_op jit(solution)/shard_map/ppermute | solution.py:206
  63.2 11.9 %collective-permute-start.5 = (bf16[4,48,1024]{2,1,0:T(8,128)(2,1)S(1)}, bf16[4,48,1024]{2,1,0:T(8,128)(2,1)S(1)}, u32[]{:S(2)}, u32[]{:S(2)}) collective-permute-start(bf16[4,48,1024]{2,1,0:T(8,128)(2,1)S(1)} %pad_maximum_fusion), channel_id=1, source_target_pairs={{0,8},{8,0},{1,9},{9,1},{2,10},{10,2},{3,11},{11,3},{4,12},{12,4},... | collective-permute-start | bytes 1179656 | tf_op jit(solution)/shard_map/ppermute | solution.py:214
  65.4 4.2 %copy-start.1 = (bf16[192,192]{1,0:T(8,128)(2,1)S(1)}, bf16[192,192]{1,0:T(8,128)(2,1)}, u32[]{:S(2)}) copy-start(bf16[192,192]{1,0:T(8,128)(2,1)} %constant.48.clone.order_ref) | copy-start | bytes 221188
  65.4 12.3 %collective-permute-start.4 = (bf16[2,48,1024]{2,1,0:T(8,128)(2,1)S(1)}, bf16[2,48,1024]{2,1,0:T(8,128)(2,1)S(1)}, u32[]{:S(2)}, u32[]{:S(2)}) collective-permute-start(bf16[2,48,1024]{2,1,0:T(8,128)(2,1)S(1)} %get-tuple-element.25), channel_id=1, source_target_pairs={{0,8},{8,0},{1,9},{9,1},{2,10},{10,2},{3,11},{11,3},{4,12},{12,4},... | collective-permute-start | bytes 589832 | tf_op jit(solution)/shard_map/ppermute | solution.py:215
  81.3 16.0 %all-to-all-start.1 = ((bf16[16,24,1024]{2,1,0:T(8,128)(2,1)}), bf16[16,24,1024]{2,1,0:T(8,128)(2,1)S(1)}, u32[]{:S(2)}, u32[]{:S(2)}) async-start(bf16[16,24,1024]{2,1,0:T(8,128)(2,1)} %bitcast.14), calls=%async_computation.1 | async-start | bytes 1572864 | tf_op jit(solution)/shard_map/all_to_all | solution.py:228

commit v10 on v9

--- a/solution.py
+++ b/solution.py
@@ -92,7 +92,7 @@
     return out[0], list(out[1:])
 
 
-def socs_kernel(block, fields, last, weight_ref, low_ref, order_ref, first_ref, second_ref, *refs):
+def socs_kernel(block, fields, last, weight_ref, place_ref, order_ref, first_ref, second_ref, *refs):
     field_refs, o_ref = refs[:fields], refs[-1]
     held = refs[fields:-1]
     pixels = field_refs[0].shape[2]
@@ -111,7 +111,7 @@
             re = by_re[:rows] - by_im[rows:]
             im = by_im[:rows] + by_re[rows:]
             total += re * re + im * im
-        total = (total * weight_ref[0]).astype(BF)
+        total = (total * weight_ref[place_ref[0]]).astype(BF)
         if not last:
             if rows >= size:
                 own = jnp.dot(order, total[:size], preferred_element_type=F32)
@@ -120,7 +120,7 @@
             else:
                 o_ref[:, cols] = total
         else:
-            low = low_ref[0]
+            low = place_ref[1]
             own = held[0][:size, cols].astype(F32)
             other = jnp.concatenate([held[0][size:, cols], held[1][:, cols], total], axis=0)
             other = jnp.dot(order, other, preferred_element_type=F32)
@@ -129,7 +129,7 @@
                 o_ref[g, 1 - low, :, cols] = other[g * step : (g + 1) * step].astype(BF)
 
 
-def socs_image(weight, low, order, first, second, fields, held=()):
+def socs_image(weights, place, order, first, second, fields, held=()):
     pixels = fields[0].shape[2]
     rows = sum(f.shape[0] * f.shape[1] for f in fields) // 2
     scalar = pl.BlockSpec(memory_space=pltpu.SMEM)
@@ -148,13 +148,18 @@
             flops=16 * rows * pixels * pixels, bytes_accessed=9 << 20, transcendentals=0
         ),
         name="socs_image",
-    )(weight, low, order, first, second, *fields, *held)
+    )(weights, place, order, first, second, *fields, *held)
 
 
 def resident_kernel(first_ref, second_ref, a_ref, b_ref, sems):
+    parts = sems.shape[1]
+    rows = a_ref.shape[0] // parts
     copies = [
-        pltpu.make_async_copy(first_ref, a_ref, sems.at[0]),
-        pltpu.make_async_copy(second_ref, b_ref, sems.at[1]),
+        pltpu.make_async_copy(
+            source.at[i * rows : (i + 1) * rows], target.at[i * rows : (i + 1) * rows], sems.at[k, i]
+        )
+        for i in range(parts)
+        for k, (source, target) in enumerate(((first_ref, a_ref), (second_ref, b_ref)))
     ]
     for copy in copies:
         copy.start()
@@ -168,7 +173,7 @@
         out_shape=[jax.ShapeDtypeStruct(first.shape, first.dtype)] * 2,
         in_specs=[pl.BlockSpec(memory_space=pl.ANY)] * 2,
         out_specs=[pl.BlockSpec(memory_space=pltpu.VMEM)] * 2,
-        scratch_shapes=[pltpu.SemaphoreType.DMA((2,))],
+        scratch_shapes=[pltpu.SemaphoreType.DMA((2, 8))],
         compiler_params=pltpu.CompilerParams(vmem_limit_bytes=12 << 20),
         cost_estimate=pl.CostEstimate(flops=0, bytes_accessed=4 * first.size * 2, transcendentals=0),
         name="resident",
@@ -180,7 +185,6 @@
     angle = lax.axis_index(("y", "xh"))
     section = lax.axis_index("s")
     depth = lax.axis_size("z")
-    weight = lax.dynamic_slice_in_dim(source_weights, angle, 1, 0)
     window = features[0]
     pairs = window.reshape(rows // 2, 2, pixels, channels)
 
@@ -214,16 +218,16 @@
     other_a = lax.ppermute(jnp.concatenate([ahead(1), ahead(2)], axis=0), "xl", SWAP)
     other_b = lax.ppermute(ahead(3), "xl", SWAP)
     mine, sibling = resident(mine, sibling)
-    low = lax.axis_index("xl").astype(jnp.int32).reshape(1)
+    place = jnp.stack([angle, lax.axis_index("xl")]).astype(jnp.int32)
     order = np.eye(ANG * depth * LINES).reshape(depth, LINES, ANG, -1).transpose(2, 0, 1, 3)
     order = order.reshape(ANG * depth * LINES, -1)
     width = LINES * ANG
     shifted = jnp.asarray(np.concatenate([order, order], axis=1).reshape(-1, 2 * depth, width).transpose(1, 0, 2), BF)
     shifted = lax.dynamic_slice_in_dim(shifted, at, depth, 0).transpose(1, 0, 2).reshape(order.shape)
     order = jnp.asarray(order, BF)
-    held_a = socs_image(weight, low, order, mine, sibling, [own, early])
-    held_b = socs_image(weight, low, order, mine, sibling, [other_a])
-    images = socs_image(weight, low, shifted, mine, sibling, [other_b], (held_a, held_b))
+    held_a = socs_image(source_weights, place, order, mine, sibling, [own, early])
+    held_b = socs_image(source_weights, place, order, mine, sibling, [other_a])
+    images = socs_image(source_weights, place, shifted, mine, sibling, [other_b], (held_a, held_b))
     images = images.reshape(2 * ANG, depth * LINES, pixels)
     pieces = lax.all_to_all(images, ("y", "xh", "xl"), 0, 0, tiled=True)
     total = jnp.sum(pieces.astype(F32), axis=0).reshape(depth, 2, OWN, pixels)
@@ -232,7 +236,7 @@
     total = jnp.stack([jnp.where(stays, kept, given), jnp.where(stays, given, kept)])
     total = total.reshape(2 * depth, OWN * pixels // 128, 128)
     total = lax.all_to_all(total, ("s", "z"), 0, 0, tiled=True)
-    even, odd = jnp.sum(total.reshape(2, depth, OWN, pixels), axis=1)
+    even, odd = jnp.sum(total.reshape(2, depth, OWN, pixels // 128, 128), axis=1)
     return jnp.stack([even, odd[::-1]], axis=1).reshape(1, LINES, pixels)
 
 

time: 111 us -> 110 us (level)
  local copies, waits for them, and re-layouts: 8.03 us -> 6.52 us
  transfers between devices with their start and end apart: 8 -> 8, of which waited for: 3 -> 3; matrix products, arithmetic and copies ran while one was open for 2% -> 2% of each run, Pallas kernels for 19% -> 20%
where the time goes in v10:
time: 110 us
  blocking collectives  33.7 us (31%)
  Pallas kernels  28.4 us (26%)
  waiting for transfers between devices  23.5 us (21%)
  starting transfers between devices  16.3 us (15%)
  local copies, waits for them, and re-layouts  6.52 us (6%)
    all_gather x1, blocking collectives, on_device(): own = lax.all_gather(near, 'z', axis=0, tiled=True)  21.4 us
    pallas_call x3, Pallas kernels, conv_stage(): pl.pallas_call(functools.partial(conv_kernel, lines, done, before, pixels...  13.5 us
    all_to_all x1, blocking collectives, on_device(): total = lax.all_to_all(total, ('s', 'z'), 0, 0, tiled=True)  12.3 us
    all_to_all x1, waiting for transfers between devices, on_device(): pieces = lax.all_to_all(images, ('y', 'xh', 'xl'), 0, 0, tiled=True)  11.6 us
    pallas_call x3, Pallas kernels, socs_image(): pl.pallas_call(functools.partial(socs_kernel, 256, len(fields), bool(held...  11.4 us
    all_to_all x1, waiting for transfers between devices, on_device(): near = lax.all_to_all(near, ('y', 'xh'), 0, 0, tiled=True)  8.73 us
    all_to_all x1, starting transfers between devices, on_device(): near = lax.all_to_all(near, ('y', 'xh'), 0, 0, tiled=True)  6.93 us
    all_to_all x1, starting transfers between devices, on_device(): pieces = lax.all_to_all(images, ('y', 'xh', 'xl'), 0, 0, tiled=True)  4.13 us
  transfers between devices with their start and end apart: 8, of which 3 were waited for; matrix products, arithmetic and copies ran while one was open for 2% of the time, Pallas kernels for 20%

profile of v10, /device:TPU:32, one launch (start us, length us, event | category | flops | bytes accessed | tf_op | source)
XLA Modules:
  0.0 109.6 jit_solution(10119540123319595497)
XLA Ops:
  0.0 1.1 dynamic-slice_bitcast_fusion
  1.1 1.9 %collective-permute-start.1 = (bf16[2,1024,128]{2,1,0:T(8,128)(2,1)S(1)}, bf16[2,1024,128]{2,1,0:T(8,128)(2,1)S(1)}, u32[]{:S(2)}, u32[]{:S(2)}) collective-permute-start(bf16[2,1024,128]{2,1,0:T(8,128)(2,1)S(1)} %dynamic-slice_bitcast_fusion), channel_id=1, source_target_pairs={{0,128},{128,0},{1,129},{129,1},{2,130},{130,2},{3,131},{131,3},{4... | collective-permute-start | bytes 1572872 | tf_op jit(solution)/shard_map/ppermute | solution.py:193
  3.0 1.0 dynamic-slice_bitcast_fusion.1
  4.0 0.3 collective-permute-start
  4.3 1.4 %copy-done = bf16[1,6,1024,128]{3,2,1,0:T(8,128)(2,1)S(1)} copy-done((bf16[1,6,1024,128]{3,2,1,0:T(8,128)(2,1)S(1)}, bf16[1,6,1024,128]{3,2,1,0:T(8,128)(2,1)}, u32[]{:S(2)}) %copy-start) | copy-done | bytes 1572888
  5.7 1.1 %copy-done.3 = bf16[5,5,128,128]{3,2,1,0:T(8,128)(2,1)S(1)} copy-done((bf16[5,5,128,128]{3,2,1,0:T(8,128)(2,1)S(1)}, bf16[5,5,128,128]{3,2,1,0:T(8,128)(2,1)}, u32[]{:S(2)}) %copy-start.3) | copy-done | bytes 819224
  6.8 0.7 copy-done.5
  7.5 5.3 %conv_stage.3 = (bf16[1,16,1024]{2,1,0:T(8,128)(2,1)S(1)}, f32[4,1024,128]{2,1,0:T(8,128)S(1)}) custom-call(s32[1]{0:T(128)} %bitcast.5.flip_ref, bf16[6,1024,128]{2,1,0:T(8,128)(2,1)S(1)} %bitcast.49, bf16[5,640,128]{2,1,0:T(8,128)(2,1)S(1)} %bitcast.50, bf16[16,128]{1,0:T(8,128)(2,1)S(1)} %bitcast.53), custom_call_target="tpu_custom_call" | custom-call | flops 4026531840 | bytes 4194304 | tf_op jit(solution)/shard_map/conv_stage/pallas_call | solution.py:78
  12.8 3.2 %collective-permute-done.1.refs_0_ = bf16[2,1024,128]{2,1,0:T(8,128)(2,1)S(1)} collective-permute-done((bf16[2,1024,128]{2,1,0:T(8,128)(2,1)S(1)}, bf16[2,1024,128]{2,1,0:T(8,128)(2,1)S(1)}, u32[]{:S(2)}, u32[]{:S(2)}) %collective-permute-start.1) | collective-permute-done | bytes 524320 | tf_op jit(solution)/shard_map/ppermute | solution.py:193
  16.0 4.7 %conv_stage.4 = (bf16[2,16,1024]{2,1,0:T(8,128)(2,1)S(1)}, f32[3,1024,128]{2,1,0:T(8,128)S(1)}) custom-call(s32[1]{0:T(128)} %bitcast.5.flip_ref, bf16[2,1024,128]{2,1,0:T(8,128)(2,1)S(1)} %collective-permute-done.1.refs_0_, bf16[5,640,128]{2,1,0:T(8,128)(2,1)S(1)} %bitcast.51, bf16[16,128]{1,0:T(8,128)(2,1)S(1)} %bitcast.54, ...), custom_call_target="tpu_custom_call" | custom-call | flops 3019898880 | bytes 4194304 | tf_op jit(solution)/shard_map/conv_stage/pallas_call | solution.py:78
  20.8 3.5 %conv_stage.5 = bf16[3,16,1024]{2,1,0:T(8,128)(2,1)S(1)} custom-call(s32[1]{0:T(128)} %bitcast.5.flip_ref, bf16[1,1024,128]{2,1,0:T(8,128)(2,1)S(1)} %collective-permute-done.refs_0_, bf16[5,640,128]{2,1,0:T(8,128)(2,1)S(1)} %bitcast.52, bf16[16,128]{1,0:T(8,128)(2,1)S(1)} %bitcast.55, f32[3,1024,128]{2,1,0:T(8,128)S(1)} %get-tuple-element.15.refs_3_), custom_call_target="tpu_custom_call" | custom-call | flops 1006632960 | bytes 4194304 | tf_op jit(solution)/shard_map/conv_stage/pallas_call | solution.py:78
  24.2 0.2 collective-permute-start.2
  24.4 0.1 reshape.71
  24.5 0.8 copy.40
  25.3 6.9 %all-to-all-start = ((bf16[8,2,6,1024]{3,1,2,0:T(2,128)(2,1)}), bf16[8,2,6,1024]{3,1,2,0:T(2,128)(2,1)S(1)}, u32[]{:S(2)}, u32[]{:S(2)}) async-start(bf16[8,2,6,1024]{3,1,2,0:T(2,128)(2,1)} %bitcast.46), calls=%async_computation | async-start | bytes 393216 | tf_op jit(solution)/shard_map/all_to_all | solution.py:208
  32.3 8.7 %all-to-all-done = bf16[8,2,6,1024]{3,1,2,0:T(2,128)(2,1)S(1)} async-done(((bf16[8,2,6,1024]{3,1,2,0:T(2,128)(2,1)}), bf16[8,2,6,1024]{3,1,2,0:T(2,128)(2,1)S(1)}, u32[]{:S(2)}, u32[]{:S(2)}) %all-to-all-start) | async-done | bytes 196640 | tf_op jit(solution)/shard_map/all_to_all | solution.py:208
  41.0 0.1 copy.39
  41.1 0.7 collective-permute-start.3
  41.8 21.4 %all_gather.3.refs_0_ = bf16[8,48,1024]{2,1,0:T(8,128)(2,1)S(1)} all-gather(bf16[2,48,1024]{2,1,0:T(8,128)(2,1)S(1)} %bitcast.58), channel_id=1, replica_groups=mesh['s'=2,'y'=4,'xh'=2,'xl'=2,'z'=4,'c'=2] {'z'}, dimensions={0}, use_global_device_ids=true | all-gather | bytes 983040 | tf_op jit(solution)/shard_map/all_gather | solution.py:211
  63.3 1.2 %collective-permute-start.5 = (bf16[4,48,1024]{2,1,0:T(8,128)(2,1)S(1)}, bf16[4,48,1024]{2,1,0:T(8,128)(2,1)S(1)}, u32[]{:S(2)}, u32[]{:S(2)}) collective-permute-start(bf16[4,48,1024]{2,1,0:T(8,128)(2,1)S(1)} %pad_maximum_fusion), channel_id=1, source_target_pairs={{0,8},{8,0},{1,9},{9,1},{2,10},{10,2},{3,11},{11,3},{4,12},{12,4},... | collective-permute-start | bytes 1179656 | tf_op jit(solution)/shard_map/ppermute | solution.py:218
  64.5 0.1 pad_add_fusion.place_ref
  64.5 0.1 copy.30.order_ref
  64.7 1.0 collective-permute-start.4
  65.7 3.5 %resident.1 = (bf16[1024,2048]{1,0:T(8,128)(2,1)S(1)}, bf16[1024,2048]{1,0:T(8,128)(2,1)S(1)}) custom-call(bf16[1024,2048]{1,0:T(8,128)(2,1)} %bitcast.4.first_ref, bf16[1024,2048]{1,0:T(8,128)(2,1)} %collective-permute-done.2.second_ref), custom_call_target="tpu_custom_call" | custom-call | bytes 16777216 | tf_op jit(solution)/shard_map/resident/pallas_call | solution.py:171
  69.2 5.5 %socs_image.3.refs_1_ = bf16[240,1024]{1,0:T(8,128)(2,1)S(1)} custom-call(f32[8]{0:T(128)S(1)} %copy-done.2, s32[2]{0:T(128)S(1)} %pad_add_fusion.place_ref, bf16[192,192]{1,0:T(8,128)(2,1)S(1)} %copy-done.1, bf16[1024,2048]{1,0:T(8,128)(2,1)S(1)} %get-tuple-element.17.first_ref, bf16[1024,2048]{1,0:T(8,128)(2,1)S(1)} %get-tuple-element.18.second_ref, ...), custom_call_target="tpu_custom_call" | custom-call | flops 4026531840 | bytes 9437184 | tf_op jit(solution)/shard_map/socs_image/pallas_call | solution.py:141
  74.7 2.4 %socs_image.4.refs_2_ = bf16[96,1024]{1,0:T(8,128)(2,1)S(1)} custom-call(f32[8]{0:T(128)S(1)} %copy-done.2, s32[2]{0:T(128)S(1)} %pad_add_fusion.place_ref, bf16[192,192]{1,0:T(8,128)(2,1)S(1)} %copy-done.1, bf16[1024,2048]{1,0:T(8,128)(2,1)S(1)} %get-tuple-element.17.first_ref, bf16[1024,2048]{1,0:T(8,128)(2,1)S(1)} %get-tuple-element.18.second_ref, ...), custom_call_target="tpu_custom_call" | custom-call | flops 1610612736 | bytes 9437184 | tf_op jit(solution)/shard_map/socs_image/pallas_call | solution.py:141
  77.2 3.5 %socs_image.5 = bf16[8,2,24,1024]{3,2,1,0:T(8,128)(2,1)} custom-call(f32[8]{0:T(128)S(1)} %copy-done.2, s32[2]{0:T(128)S(1)} %pad_add_fusion.place_ref, bf16[192,192]{1,0:T(8,128)(2,1)S(1)} %copy.30.order_ref, bf16[1024,2048]{1,0:T(8,128)(2,1)S(1)} %get-tuple-element.17.first_ref, bf16[1024,2048]{1,0:T(8,128)(2,1)S(1)} %get-tuple-element.18.second_ref, ...), custom_call_target="tpu_custom_call" | custom-call | flops 805306368 | bytes 9437184 | tf_op jit(solution)/shard_map/socs_image/pallas_call | solution.py:141
  80.6 4.1 %all-to-all-start.1 = ((bf16[16,24,1024]{2,1,0:T(8,128)(2,1)}), bf16[16,24,1024]{2,1,0:T(8,128)(2,1)S(1)}, u32[]{:S(2)}, u32[]{:S(2)}) async-start(bf16[16,24,1024]{2,1,0:T(8,128)(2,1)} %bitcast.15), calls=%async_computation.1 | async-start | bytes 1572864 | tf_op jit(solution)/shard_map/all_to_all | solution.py:232
  84.8 11.6 %all-to-all-done.1 = bf16[16,24,1024]{2,1,0:T(8,128)(2,1)S(1)} async-done(((bf16[16,24,1024]{2,1,0:T(8,128)(2,1)}), bf16[16,24,1024]{2,1,0:T(8,128)(2,1)S(1)}, u32[]{:S(2)}, u32[]{:S(2)}) %all-to-all-start.1) | async-done | bytes 786464 | tf_op jit(solution)/shard_map/all_to_all | solution.py:232
  96.4 0.1 convert_reduce_fusion
  96.7 12.3 %all_to_all.15 = f32[8,24,128]{2,1,0:T(8,128)S(1)} all-to-all(f32[8,24,128]{2,1,0:T(8,128)S(1)} %reshape.75), channel_id=1, replica_groups=mesh['s'=2,'y'=4,'xh'=2,'xl'=2,'z'=4,'c'=2] {'s','z'}, dimensions={0} | all-to-all | bytes 196608 | tf_op jit(solution)/shard_map/all_to_all | solution.py:238
  109.0 0.6 pad_maximum_fusion.3
  (30 shorter events, 0.4 us)
Async XLA Ops:
  1.1 14.9 %collective-permute-start.1 = (bf16[2,1024,128]{2,1,0:T(8,128)(2,1)S(1)}, bf16[2,1024,128]{2,1,0:T(8,128)(2,1)S(1)}, u32[]{:S(2)}, u32[]{:S(2)}) collective-permute-start(bf16[2,1024,128]{2,1,0:T(8,128)(2,1)S(1)} %dynamic-slice_bitcast_fusion), channel_id=1, source_target_pairs={{0,128},{128,0},{1,129},{129,1},{2,130},{130,2},{3,131},{131,3},{4... | collective-permute-start | bytes 1572872 | tf_op jit(solution)/shard_map/ppermute | solution.py:193
  4.0 16.8 %collective-permute-start = (bf16[1,1024,128]{2,1,0:T(8,128)(2,1)S(1)}, bf16[1,1024,128]{2,1,0:T(8,128)(2,1)S(1)}, u32[]{:S(2)}, u32[]{:S(2)}) collective-permute-start(bf16[1,1024,128]{2,1,0:T(8,128)(2,1)S(1)} %dynamic-slice_bitcast_fusion.1), channel_id=1, source_target_pairs={{0,128},{128,0},{1,129},{129,1},{2,130},{130,2},{3,131},{131,3},{4... | collective-permute-start | bytes 786440 | tf_op jit(solution)/shard_map/ppermute | solution.py:193
  4.3 1.4 %copy-start = (bf16[1,6,1024,128]{3,2,1,0:T(8,128)(2,1)S(1)}, bf16[1,6,1024,128]{3,2,1,0:T(8,128)(2,1)}, u32[]{:S(2)}) copy-start(bf16[1,6,1024,128]{3,2,1,0:T(8,128)(2,1)} %param.7) | copy-start | bytes 4718596
  5.7 1.1 %copy-start.3 = (bf16[5,5,128,128]{3,2,1,0:T(8,128)(2,1)S(1)}, bf16[5,5,128,128]{3,2,1,0:T(8,128)(2,1)}, u32[]{:S(2)}) copy-start(bf16[5,5,128,128]{3,2,1,0:T(8,128)(2,1)} %param.8) | copy-start | bytes 2457604
  6.8 0.7 copy-start.5
  7.5 8.5 %copy-start.4 = (bf16[5,5,128,128]{3,2,1,0:T(8,128)(2,1)S(1)}, bf16[5,5,128,128]{3,2,1,0:T(8,128)(2,1)}, u32[]{:S(2)}) copy-start(bf16[5,5,128,128]{3,2,1,0:T(8,128)(2,1)} %param.8) | copy-start | bytes 2457604
  7.5 8.5 %copy-start.6 = (bf16[128,16]{0,1:T(8,128)(2,1)S(1)}, bf16[128,16]{0,1:T(8,128)(2,1)}, u32[]{:S(2)}) copy-start(bf16[128,16]{0,1:T(8,128)(2,1)} %param.9) | copy-start | bytes 12292
  20.7 11.5 %copy-start.7 = (bf16[8,192,48]{1,2,0:T(8,128)(2,1)S(1)}, bf16[8,192,48]{1,2,0:T(8,128)(2,1)}, u32[]{:S(2)}) copy-start(bf16[8,192,48]{1,2,0:T(8,128)(2,1)} %constant.47.clone) | copy-start | bytes 442372
  24.2 41.5 %collective-permute-start.2 = (bf16[1024,2048]{1,0:T(8,128)(2,1)}, bf16[1024,2048]{1,0:T(8,128)(2,1)}, u32[]{:S(2)}, u32[]{:S(2)}) collective-permute-start(bf16[1024,2048]{1,0:T(8,128)(2,1)} %bitcast.4.first_ref), channel_id=1, source_target_pairs={{0,1},{1,0},{2,3},{3,2},{4,5},{5,4},{6,7},{7,6},{8,9},{9,8},{10,11... | collective-permute-start | bytes 12582920 | tf_op jit(solution)/shard_map/ppermute | solution.py:206
  25.3 15.7 %all-to-all-start = ((bf16[8,2,6,1024]{3,1,2,0:T(2,128)(2,1)}), bf16[8,2,6,1024]{3,1,2,0:T(2,128)(2,1)S(1)}, u32[]{:S(2)}, u32[]{:S(2)}) async-start(bf16[8,2,6,1024]{3,1,2,0:T(2,128)(2,1)} %bitcast.46), calls=%async_computation | async-start | bytes 393216 | tf_op jit(solution)/shard_map/all_to_all | solution.py:208
  41.1 22.1 %collective-permute-start.3 = (bf16[2,48,1024]{2,1,0:T(8,128)(2,1)S(1)}, bf16[2,48,1024]{2,1,0:T(8,128)(2,1)S(1)}, u32[]{:S(2)}, u32[]{:S(2)}) collective-permute-start(bf16[2,48,1024]{2,1,0:T(8,128)(2,1)S(1)} %bitcast.57), channel_id=1, source_target_pairs={{0,8},{8,0},{1,9},{9,1},{2,10},{10,2},{3,11},{11,3},{4,12},{12,4},... | collective-permute-start | bytes 589832 | tf_op jit(solution)/shard_map/ppermute | solution.py:210
  63.3 11.4 %collective-permute-start.5 = (bf16[4,48,1024]{2,1,0:T(8,128)(2,1)S(1)}, bf16[4,48,1024]{2,1,0:T(8,128)(2,1)S(1)}, u32[]{:S(2)}, u32[]{:S(2)}) collective-permute-start(bf16[4,48,1024]{2,1,0:T(8,128)(2,1)S(1)} %pad_maximum_fusion), channel_id=1, source_target_pairs={{0,8},{8,0},{1,9},{9,1},{2,10},{10,2},{3,11},{11,3},{4,12},{12,4},... | collective-permute-start | bytes 1179656 | tf_op jit(solution)/shard_map/ppermute | solution.py:218
  64.6 4.6 %copy-start.1 = (bf16[192,192]{1,0:T(8,128)(2,1)S(1)}, bf16[192,192]{1,0:T(8,128)(2,1)}, u32[]{:S(2)}) copy-start(bf16[192,192]{1,0:T(8,128)(2,1)} %constant.48.clone.order_ref) | copy-start | bytes 221188
  64.6 4.6 %copy-start.2 = (f32[8]{0:T(128)S(1)}, f32[8]{0:T(128)}, u32[]{:S(2)}) copy-start(f32[8]{0:T(128)} %weight_ref.5) | copy-start | bytes 100
  64.7 12.5 %collective-permute-start.4 = (bf16[2,48,1024]{2,1,0:T(8,128)(2,1)S(1)}, bf16[2,48,1024]{2,1,0:T(8,128)(2,1)S(1)}, u32[]{:S(2)}, u32[]{:S(2)}) collective-permute-start(bf16[2,48,1024]{2,1,0:T(8,128)(2,1)S(1)} %get-tuple-element.25), channel_id=1, source_target_pairs={{0,8},{8,0},{1,9},{9,1},{2,10},{10,2},{3,11},{11,3},{4,12},{12,4},... | collective-permute-start | bytes 589832 | tf_op jit(solution)/shard_map/ppermute | solution.py:219
  80.6 15.7 %all-to-all-start.1 = ((bf16[16,24,1024]{2,1,0:T(8,128)(2,1)}), bf16[16,24,1024]{2,1,0:T(8,128)(2,1)S(1)}, u32[]{:S(2)}, u32[]{:S(2)}) async-start(bf16[16,24,1024]{2,1,0:T(8,128)(2,1)} %bitcast.15), calls=%async_computation.1 | async-start | bytes 1572864 | tf_op jit(solution)/shard_map/all_to_all | solution.py:232

commit v11 on v10

--- a/solution.py
+++ b/solution.py
@@ -205,26 +205,26 @@
         if stage == 2:
             sibling = lax.ppermute(lax.optimization_barrier((mine, done))[0], "c", SWAP)
     near = jnp.concatenate(near, axis=0).reshape(LINES, ANG, 2, pixels).transpose(1, 2, 0, 3)
-    near = lax.all_to_all(near, ("y", "xh"), 0, 0, tiled=True)
-    near = near.transpose(1, 2, 0, 3).reshape(2, LINES * ANG, pixels)
-    early = lax.ppermute(near, "xl", SWAP)
-    own = lax.all_gather(near, "z", axis=0, tiled=True)
-    own, early = lax.optimization_barrier((own, early))
-    at = lax.axis_index("z")
-
-    def ahead(k):
-        return lax.dynamic_slice_in_dim(own, 2 * lax.rem(at + k, depth), 2, 0)
-
-    other_a = lax.ppermute(jnp.concatenate([ahead(1), ahead(2)], axis=0), "xl", SWAP)
-    other_b = lax.ppermute(ahead(3), "xl", SWAP)
-    mine, sibling = resident(mine, sibling)
-    place = jnp.stack([angle, lax.axis_index("xl")]).astype(jnp.int32)
+    at = lax.axis_index("z").astype(jnp.uint32)
+    starts = [2 * ((at + k) % depth) for k in range(1, depth)]
     order = np.eye(ANG * depth * LINES).reshape(depth, LINES, ANG, -1).transpose(2, 0, 1, 3)
     order = order.reshape(ANG * depth * LINES, -1)
     width = LINES * ANG
     shifted = jnp.asarray(np.concatenate([order, order], axis=1).reshape(-1, 2 * depth, width).transpose(1, 0, 2), BF)
     shifted = lax.dynamic_slice_in_dim(shifted, at, depth, 0).transpose(1, 0, 2).reshape(order.shape)
     order = jnp.asarray(order, BF)
+    place = jnp.stack([angle, lax.axis_index("xl")]).astype(jnp.int32)
+    stays = section == 0
+    near, starts, shifted, place, stays = lax.optimization_barrier((near, starts, shifted, place, stays))
+    near = lax.all_to_all(near, ("y", "xh"), 0, 0, tiled=True)
+    near = near.transpose(1, 2, 0, 3).reshape(2, LINES * ANG, pixels)
+    early = lax.ppermute(near, "xl", SWAP)
+    own = lax.all_gather(near, "z", axis=0, tiled=True)
+    own, early = lax.optimization_barrier((own, early))
+    ahead = [lax.dynamic_slice_in_dim(own, start, 2, 0) for start in starts]
+    other_a = lax.ppermute(jnp.concatenate(ahead[:2], axis=0), "xl", SWAP)
+    other_b = lax.ppermute(ahead[2], "xl", SWAP)
+    mine, sibling = resident(mine, sibling)
     held_a = socs_image(source_weights, place, order, mine, sibling, [own, early])
     held_b = socs_image(source_weights, place, order, mine, sibling, [other_a])
     images = socs_image(source_weights, place, shifted, mine, sibling, [other_b], (held_a, held_b))
@@ -232,7 +232,6 @@
     pieces = lax.all_to_all(images, ("y", "xh", "xl"), 0, 0, tiled=True)
     total = jnp.sum(pieces.astype(F32), axis=0).reshape(depth, 2, OWN, pixels)
     kept, given = total[:, 0], total[:, 1]
-    stays = section == 0
     total = jnp.stack([jnp.where(stays, kept, given), jnp.where(stays, given, kept)])
     total = total.reshape(2 * depth, OWN * pixels // 128, 128)
     total = lax.all_to_all(total, ("s", "z"), 0, 0, tiled=True)

time: 110 us -> 108 us (0.982)
  blocking collectives: 33.7 us -> 64.6 us
  waiting for transfers between devices: 23.5 us -> 3.21 us
  starting transfers between devices: 16.3 us -> 5.25 us
    all_to_all x0 -> x2, blocking collectives: none -> 31.3 us  [the longest x1 15.8 us: on_device(): pieces = lax.all_to_all(images, ('y', 'xh', 'xl'), 0, 0, tiled=True)]
    all_to_all x2 -> x0, waiting for transfers between devices: 20.3 us -> none  [the longest x1 11.6 us: on_device(): pieces = lax.all_to_all(images, ('y', 'xh', 'xl'), 0, 0, tiled=True)]
    all_to_all x2 -> x0, starting transfers between devices: 11.1 us -> none  [the longest x1 6.93 us: on_device(): near = lax.all_to_all(near, ('y', 'xh'), 0, 0, tiled=True)]
  transfers between devices with their start and end apart: 8 -> 6, of which waited for: 3 -> 1; matrix products, arithmetic and copies ran while one was open for 2% -> 1% of each run, Pallas kernels for 20% -> 20%
where the time goes in v11:
time: 108 us
  blocking collectives  64.6 us (60%)
  Pallas kernels  27.5 us (25%)
  local copies, waits for them, and re-layouts  5.84 us (5%)
  starting transfers between devices  5.25 us (5%)
  waiting for transfers between devices  3.21 us (3%)
    all_gather x1, blocking collectives, on_device(): own = lax.all_gather(near, 'z', axis=0, tiled=True)  21.1 us
    all_to_all x1, blocking collectives, on_device(): pieces = lax.all_to_all(images, ('y', 'xh', 'xl'), 0, 0, tiled=True)  15.8 us
    all_to_all x1, blocking collectives, on_device(): near = lax.all_to_all(near, ('y', 'xh'), 0, 0, tiled=True)  15.5 us
    pallas_call x3, Pallas kernels, conv_stage(): pl.pallas_call(functools.partial(conv_kernel, lines, done, before, pixels...  13.5 us
    all_to_all x1, blocking collectives, on_device(): total = lax.all_to_all(total, ('s', 'z'), 0, 0, tiled=True)  12.2 us
    pallas_call x3, Pallas kernels, socs_image(): pl.pallas_call(functools.partial(socs_kernel, 256, len(fields), bool(held...  10.5 us
    pallas_call x1, Pallas kernels, resident(): pl.pallas_call(resident_kernel, out_shape=[jax.ShapeDtypeStruct(first.sha...  3.51 us
    unnamed x16, local copies, waits for them, and re-layouts  3.27 us
  transfers between devices with their start and end apart: 6, of which 1 were waited for; matrix products, arithmetic and copies ran while one was open for 1% of the time, Pallas kernels for 20%

profile of v11, /device:TPU:32, one launch (start us, length us, event | category | flops | bytes accessed | tf_op | source)
XLA Modules:
  0.0 107.6 jit_solution(3044295535910276815)
XLA Ops:
  0.0 1.1 %dynamic-slice_bitcast_fusion = bf16[2,1024,128]{2,1,0:T(8,128)(2,1)S(1)} fusion(bf16[3,2,1024,128]{3,2,1,0:T(8,128)(2,1)} %bitcast.48, s32[]{:T(128)S(6)} %select_n.51, s32[]{:T(128)S(6)} %select_n.52), kind=kLoop, calls=%fused_computation.1 | loop fusion | bytes 1048584 | tf_op jit(solution)/shard_map/squeeze | solution.py:193
  1.1 1.9 %collective-permute-start = (bf16[2,1024,128]{2,1,0:T(8,128)(2,1)S(1)}, bf16[2,1024,128]{2,1,0:T(8,128)(2,1)S(1)}, u32[]{:S(2)}, u32[]{:S(2)}) collective-permute-start(bf16[2,1024,128]{2,1,0:T(8,128)(2,1)S(1)} %dynamic-slice_bitcast_fusion), channel_id=1, source_target_pairs={{0,128},{128,0},{1,129},{129,1},{2,130},{130,2},{3,131},{131,3},{4... | collective-permute-start | bytes 1572872 | tf_op jit(solution)/shard_map/ppermute | solution.py:193
  3.0 1.0 dynamic-slice_bitcast_fusion.1
  4.0 0.3 collective-permute-start.1
  4.3 1.4 %copy-done = bf16[1,6,1024,128]{3,2,1,0:T(8,128)(2,1)S(1)} copy-done((bf16[1,6,1024,128]{3,2,1,0:T(8,128)(2,1)S(1)}, bf16[1,6,1024,128]{3,2,1,0:T(8,128)(2,1)}, u32[]{:S(2)}) %copy-start) | copy-done | bytes 1572888
  5.7 1.1 %copy-done.3 = bf16[5,5,128,128]{3,2,1,0:T(8,128)(2,1)S(1)} copy-done((bf16[5,5,128,128]{3,2,1,0:T(8,128)(2,1)S(1)}, bf16[5,5,128,128]{3,2,1,0:T(8,128)(2,1)}, u32[]{:S(2)}) %copy-start.3) | copy-done | bytes 819224
  6.8 0.7 copy-done.5
  7.5 5.3 %conv_stage.3 = (bf16[1,16,1024]{2,1,0:T(8,128)(2,1)S(1)}, f32[4,1024,128]{2,1,0:T(8,128)S(1)}) custom-call(s32[1]{0:T(128)} %bitcast.flip_ref, bf16[6,1024,128]{2,1,0:T(8,128)(2,1)S(1)} %bitcast.50, bf16[5,640,128]{2,1,0:T(8,128)(2,1)S(1)} %bitcast.51, bf16[16,128]{1,0:T(8,128)(2,1)S(1)} %bitcast.54), custom_call_target="tpu_custom_call" | custom-call | flops 4026531840 | bytes 4194304 | tf_op jit(solution)/shard_map/conv_stage/pallas_call | solution.py:78
  12.8 3.2 %collective-permute-done.refs_0_ = bf16[2,1024,128]{2,1,0:T(8,128)(2,1)S(1)} collective-permute-done((bf16[2,1024,128]{2,1,0:T(8,128)(2,1)S(1)}, bf16[2,1024,128]{2,1,0:T(8,128)(2,1)S(1)}, u32[]{:S(2)}, u32[]{:S(2)}) %collective-permute-start) | collective-permute-done | bytes 524320 | tf_op jit(solution)/shard_map/ppermute | solution.py:193
  16.0 4.7 %conv_stage.4 = (bf16[2,16,1024]{2,1,0:T(8,128)(2,1)S(1)}, f32[3,1024,128]{2,1,0:T(8,128)S(1)}) custom-call(s32[1]{0:T(128)} %bitcast.flip_ref, bf16[2,1024,128]{2,1,0:T(8,128)(2,1)S(1)} %collective-permute-done.refs_0_, bf16[5,640,128]{2,1,0:T(8,128)(2,1)S(1)} %bitcast.52, bf16[16,128]{1,0:T(8,128)(2,1)S(1)} %bitcast.55, ...), custom_call_target="tpu_custom_call" | custom-call | flops 3019898880 | bytes 4194304 | tf_op jit(solution)/shard_map/conv_stage/pallas_call | solution.py:78
  20.7 0.0 copy-start.7
  20.8 3.5 %conv_stage.5 = bf16[3,16,1024]{2,1,0:T(8,128)(2,1)S(1)} custom-call(s32[1]{0:T(128)} %bitcast.flip_ref, bf16[1,1024,128]{2,1,0:T(8,128)(2,1)S(1)} %collective-permute-done.1.refs_0_, bf16[5,640,128]{2,1,0:T(8,128)(2,1)S(1)} %bitcast.53, bf16[16,128]{1,0:T(8,128)(2,1)S(1)} %bitcast.56, f32[3,1024,128]{2,1,0:T(8,128)S(1)} %get-tuple-element.24.refs_3_), custom_call_target="tpu_custom_call" | custom-call | flops 1006632960 | bytes 4194304 | tf_op jit(solution)/shard_map/conv_stage/pallas_call | solution.py:78
  24.2 0.2 collective-permute-start.2
  24.4 0.1 pad_add_fusion.place_ref
  24.6 0.1 reshape.70
  24.6 0.1 copy.40
  24.8 15.5 %all_to_all.15 = bf16[8,2,6,1024]{3,1,2,0:T(2,128)(2,1)S(1)} all-to-all(bf16[8,2,6,1024]{3,1,2,0:T(2,128)(2,1)S(1)} %bitcast.57), channel_id=1, replica_groups=mesh['s'=2,'y'=4,'xh'=2,'xl'=2,'z'=4,'c'=2] {'y','xh'}, dimensions={0} | all-to-all | bytes 393216 | tf_op jit(solution)/shard_map/all_to_all | solution.py:219
  40.3 0.1 copy.39
  40.3 0.7 collective-permute-start.3
  41.0 21.1 %all_gather.3.refs_0_ = bf16[8,48,1024]{2,1,0:T(8,128)(2,1)S(1)} all-gather(bf16[2,48,1024]{2,1,0:T(8,128)(2,1)S(1)} %bitcast.60), channel_id=1, replica_groups=mesh['s'=2,'y'=4,'xh'=2,'xl'=2,'z'=4,'c'=2] {'z'}, dimensions={0}, use_global_device_ids=true | all-gather | bytes 983040 | tf_op jit(solution)/shard_map/all_gather | solution.py:222
  62.2 1.5 %collective-permute-start.5 = (bf16[4,48,1024]{2,1,0:T(8,128)(2,1)S(1)}, bf16[4,48,1024]{2,1,0:T(8,128)(2,1)S(1)}, u32[]{:S(2)}, u32[]{:S(2)}) collective-permute-start(bf16[4,48,1024]{2,1,0:T(8,128)(2,1)S(1)} %pad_maximum_fusion), channel_id=1, source_target_pairs={{0,8},{8,0},{1,9},{9,1},{2,10},{10,2},{3,11},{11,3},{4,12},{12,4},... | collective-permute-start | bytes 1179656 | tf_op jit(solution)/shard_map/ppermute | solution.py:225
  63.6 0.1 copy.30.order_ref
  63.8 0.7 collective-permute-start.4
  64.5 3.5 %resident.1 = (bf16[1024,2048]{1,0:T(8,128)(2,1)S(1)}, bf16[1024,2048]{1,0:T(8,128)(2,1)S(1)}) custom-call(bf16[1024,2048]{1,0:T(8,128)(2,1)} %bitcast.12.first_ref, bf16[1024,2048]{1,0:T(8,128)(2,1)} %collective-permute-done.2.second_ref), custom_call_target="tpu_custom_call" | custom-call | bytes 16777216 | tf_op jit(solution)/shard_map/resident/pallas_call | solution.py:171
  68.0 5.5 %socs_image.3.refs_1_ = bf16[240,1024]{1,0:T(8,128)(2,1)S(1)} custom-call(f32[8]{0:T(128)S(1)} %copy-done.2, s32[2]{0:T(128)S(1)} %pad_add_fusion.place_ref, bf16[192,192]{1,0:T(8,128)(2,1)S(1)} %copy-done.1, bf16[1024,2048]{1,0:T(8,128)(2,1)S(1)} %get-tuple-element.29.first_ref, bf16[1024,2048]{1,0:T(8,128)(2,1)S(1)} %get-tuple-element.30.second_ref, ...), custom_call_target="tpu_custom_call" | custom-call | flops 4026531840 | bytes 9437184 | tf_op jit(solution)/shard_map/socs_image/pallas_call | solution.py:141
  73.5 2.4 %socs_image.4.refs_2_ = bf16[96,1024]{1,0:T(8,128)(2,1)S(1)} custom-call(f32[8]{0:T(128)S(1)} %copy-done.2, s32[2]{0:T(128)S(1)} %pad_add_fusion.place_ref, bf16[192,192]{1,0:T(8,128)(2,1)S(1)} %copy-done.1, bf16[1024,2048]{1,0:T(8,128)(2,1)S(1)} %get-tuple-element.29.first_ref, bf16[1024,2048]{1,0:T(8,128)(2,1)S(1)} %get-tuple-element.30.second_ref, ...), custom_call_target="tpu_custom_call" | custom-call | flops 1610612736 | bytes 9437184 | tf_op jit(solution)/shard_map/socs_image/pallas_call | solution.py:141
  76.0 2.6 %socs_image.5 = bf16[8,2,24,1024]{3,2,1,0:T(8,128)(2,1)S(1)} custom-call(f32[8]{0:T(128)S(1)} %copy-done.2, s32[2]{0:T(128)S(1)} %pad_add_fusion.place_ref, bf16[192,192]{1,0:T(8,128)(2,1)S(1)} %copy.30.order_ref, bf16[1024,2048]{1,0:T(8,128)(2,1)S(1)} %get-tuple-element.29.first_ref, bf16[1024,2048]{1,0:T(8,128)(2,1)S(1)} %get-tuple-element.30.second_ref, ...), custom_call_target="tpu_custom_call" | custom-call | flops 805306368 | bytes 9437184 | tf_op jit(solution)/shard_map/socs_image/pallas_call | solution.py:141
  78.6 15.8 %all_to_all.16 = bf16[16,24,1024]{2,1,0:T(8,128)(2,1)S(1)} all-to-all(bf16[16,24,1024]{2,1,0:T(8,128)(2,1)S(1)} %bitcast.47), channel_id=1, replica_groups=mesh['s'=2,'y'=4,'xh'=2,'xl'=2,'z'=4,'c'=2] {'y','xh','xl'}, dimensions={0} | all-to-all | bytes 1572864 | tf_op jit(solution)/shard_map/all_to_all | solution.py:232
  94.4 0.1 convert_reduce_fusion
  94.7 0.1 reshape.75
  94.7 12.2 %all_to_all.17 = f32[8,24,128]{2,1,0:T(8,128)S(1)} all-to-all(f32[8,24,128]{2,1,0:T(8,128)S(1)} %reshape.75), channel_id=1, replica_groups=mesh['s'=2,'y'=4,'xh'=2,'xl'=2,'z'=4,'c'=2] {'s','z'}, dimensions={0} | all-to-all | bytes 196608 | tf_op jit(solution)/shard_map/all_to_all | solution.py:237
  107.0 0.6 pad_maximum_fusion.3
  (28 shorter events, 0.3 us)
Async XLA Ops:
  1.1 14.9 %collective-permute-start = (bf16[2,1024,128]{2,1,0:T(8,128)(2,1)S(1)}, bf16[2,1024,128]{2,1,0:T(8,128)(2,1)S(1)}, u32[]{:S(2)}, u32[]{:S(2)}) collective-permute-start(bf16[2,1024,128]{2,1,0:T(8,128)(2,1)S(1)} %dynamic-slice_bitcast_fusion), channel_id=1, source_target_pairs={{0,128},{128,0},{1,129},{129,1},{2,130},{130,2},{3,131},{131,3},{4... | collective-permute-start | bytes 1572872 | tf_op jit(solution)/shard_map/ppermute | solution.py:193
  4.0 16.8 %collective-permute-start.1 = (bf16[1,1024,128]{2,1,0:T(8,128)(2,1)S(1)}, bf16[1,1024,128]{2,1,0:T(8,128)(2,1)S(1)}, u32[]{:S(2)}, u32[]{:S(2)}) collective-permute-start(bf16[1,1024,128]{2,1,0:T(8,128)(2,1)S(1)} %dynamic-slice_bitcast_fusion.1), channel_id=1, source_target_pairs={{0,128},{128,0},{1,129},{129,1},{2,130},{130,2},{3,131},{131,3},{4... | collective-permute-start | bytes 786440 | tf_op jit(solution)/shard_map/ppermute | solution.py:193
  4.3 1.4 %copy-start = (bf16[1,6,1024,128]{3,2,1,0:T(8,128)(2,1)S(1)}, bf16[1,6,1024,128]{3,2,1,0:T(8,128)(2,1)}, u32[]{:S(2)}) copy-start(bf16[1,6,1024,128]{3,2,1,0:T(8,128)(2,1)} %param.7) | copy-start | bytes 4718596
  5.7 1.1 %copy-start.3 = (bf16[5,5,128,128]{3,2,1,0:T(8,128)(2,1)S(1)}, bf16[5,5,128,128]{3,2,1,0:T(8,128)(2,1)}, u32[]{:S(2)}) copy-start(bf16[5,5,128,128]{3,2,1,0:T(8,128)(2,1)} %param.8) | copy-start | bytes 2457604
  6.8 0.7 copy-start.5
  7.5 8.5 %copy-start.4 = (bf16[5,5,128,128]{3,2,1,0:T(8,128)(2,1)S(1)}, bf16[5,5,128,128]{3,2,1,0:T(8,128)(2,1)}, u32[]{:S(2)}) copy-start(bf16[5,5,128,128]{3,2,1,0:T(8,128)(2,1)} %param.8) | copy-start | bytes 2457604
  7.5 8.5 %copy-start.6 = (bf16[128,16]{0,1:T(8,128)(2,1)S(1)}, bf16[128,16]{0,1:T(8,128)(2,1)}, u32[]{:S(2)}) copy-start(bf16[128,16]{0,1:T(8,128)(2,1)} %param.9) | copy-start | bytes 12292
  20.7 3.8 %copy-start.7 = (bf16[8,192,48]{1,2,0:T(8,128)(2,1)S(1)}, bf16[8,192,48]{1,2,0:T(8,128)(2,1)}, u32[]{:S(2)}) copy-start(bf16[8,192,48]{1,2,0:T(8,128)(2,1)} %constant.62.clone) | copy-start | bytes 442372
  24.2 40.3 %collective-permute-start.2 = (bf16[1024,2048]{1,0:T(8,128)(2,1)}, bf16[1024,2048]{1,0:T(8,128)(2,1)}, u32[]{:S(2)}, u32[]{:S(2)}) collective-permute-start(bf16[1024,2048]{1,0:T(8,128)(2,1)} %bitcast.12.first_ref), channel_id=1, source_target_pairs={{0,1},{1,0},{2,3},{3,2},{4,5},{5,4},{6,7},{7,6},{8,9},{9,8},{10,11... | collective-permute-start | bytes 12582920 | tf_op jit(solution)/shard_map/ppermute | solution.py:206
  40.3 21.7 %collective-permute-start.3 = (bf16[2,48,1024]{2,1,0:T(8,128)(2,1)S(1)}, bf16[2,48,1024]{2,1,0:T(8,128)(2,1)S(1)}, u32[]{:S(2)}, u32[]{:S(2)}) collective-permute-start(bf16[2,48,1024]{2,1,0:T(8,128)(2,1)S(1)} %bitcast.59), channel_id=1, source_target_pairs={{0,8},{8,0},{1,9},{9,1},{2,10},{10,2},{3,11},{11,3},{4,12},{12,4},... | collective-permute-start | bytes 589832 | tf_op jit(solution)/shard_map/ppermute | solution.py:221
  62.2 11.4 %collective-permute-start.5 = (bf16[4,48,1024]{2,1,0:T(8,128)(2,1)S(1)}, bf16[4,48,1024]{2,1,0:T(8,128)(2,1)S(1)}, u32[]{:S(2)}, u32[]{:S(2)}) collective-permute-start(bf16[4,48,1024]{2,1,0:T(8,128)(2,1)S(1)} %pad_maximum_fusion), channel_id=1, source_target_pairs={{0,8},{8,0},{1,9},{9,1},{2,10},{10,2},{3,11},{11,3},{4,12},{12,4},... | collective-permute-start | bytes 1179656 | tf_op jit(solution)/shard_map/ppermute | solution.py:225
  63.7 4.3 %copy-start.1 = (bf16[192,192]{1,0:T(8,128)(2,1)S(1)}, bf16[192,192]{1,0:T(8,128)(2,1)}, u32[]{:S(2)}) copy-start(bf16[192,192]{1,0:T(8,128)(2,1)} %constant.63.clone.order_ref) | copy-start | bytes 221188
  63.7 4.3 %copy-start.2 = (f32[8]{0:T(128)S(1)}, f32[8]{0:T(128)}, u32[]{:S(2)}) copy-start(f32[8]{0:T(128)} %weight_ref.5) | copy-start | bytes 100
  63.8 12.2 %collective-permute-start.4 = (bf16[2,48,1024]{2,1,0:T(8,128)(2,1)S(1)}, bf16[2,48,1024]{2,1,0:T(8,128)(2,1)S(1)}, u32[]{:S(2)}, u32[]{:S(2)}) collective-permute-start(bf16[2,48,1024]{2,1,0:T(8,128)(2,1)S(1)} %get-tuple-element.39), channel_id=1, source_target_pairs={{0,8},{8,0},{1,9},{9,1},{2,10},{10,2},{3,11},{11,3},{4,12},{12,4},... | collective-permute-start | bytes 589832 | tf_op jit(solution)/shard_map/ppermute | solution.py:226

commit v12 on v11

--- a/solution.py
+++ b/solution.py
@@ -1,4 +1,5 @@
 import functools
+import math
 
 import jax
 import jax.numpy as jnp
@@ -56,7 +57,9 @@
                     )
                     acc = part if acc is None else acc + part
             if o in done:
-                hidden = jax.nn.gelu(acc, approximate=True).astype(BF)
+                scale = math.sqrt(2 / math.pi)
+                curve = jnp.tanh(acc * (scale + (0.044715 * scale) * (acc * acc)))
+                hidden = (0.5 * acc + 0.5 * acc * curve).astype(BF)
                 near = lax.dot_general(
                     h_ref[...], hidden, (((1,), (1,)), ((), ())), preferred_element_type=F32
                 )
@@ -232,10 +235,10 @@
     pieces = lax.all_to_all(images, ("y", "xh", "xl"), 0, 0, tiled=True)
     total = jnp.sum(pieces.astype(F32), axis=0).reshape(depth, 2, OWN, pixels)
     kept, given = total[:, 0], total[:, 1]
-    total = jnp.stack([jnp.where(stays, kept, given), jnp.where(stays, given, kept)])
+    total = jnp.stack([jnp.where(stays, kept, given), jnp.where(stays, given, kept)], axis=1)
     total = total.reshape(2 * depth, OWN * pixels // 128, 128)
-    total = lax.all_to_all(total, ("s", "z"), 0, 0, tiled=True)
-    even, odd = jnp.sum(total.reshape(2, depth, OWN, pixels // 128, 128), axis=1)
+    total = lax.all_to_all(total, ("z", "s"), 0, 0, tiled=True)
+    even, odd = jnp.sum(total.reshape(depth, 2, OWN, pixels // 128, 128), axis=0)
     return jnp.stack([even, odd[::-1]], axis=1).reshape(1, LINES, pixels)
 
 

time: 108 us -> 108 us (level)
  no operation moved by 1% of the time
where the time goes in v12:
time: 108 us
  blocking collectives  64.8 us (60%)
  Pallas kernels  27.4 us (25%)
  local copies, waits for them, and re-layouts  5.84 us (5%)
  starting transfers between devices  5.25 us (5%)
  waiting for transfers between devices  3.23 us (3%)
    all_gather x1, blocking collectives, on_device(): own = lax.all_gather(near, 'z', axis=0, tiled=True)  21.1 us
    all_to_all x1, blocking collectives, on_device(): near = lax.all_to_all(near, ('y', 'xh'), 0, 0, tiled=True)  15.5 us
    all_to_all x1, blocking collectives, on_device(): pieces = lax.all_to_all(images, ('y', 'xh', 'xl'), 0, 0, tiled=True)  15.4 us
    pallas_call x3, Pallas kernels, conv_stage(): pl.pallas_call(functools.partial(conv_kernel, lines, done, before, pixels...  13.4 us
    all_to_all x1, blocking collectives, on_device(): total = lax.all_to_all(total, ('z', 's'), 0, 0, tiled=True)  12.8 us
    pallas_call x3, Pallas kernels, socs_image(): pl.pallas_call(functools.partial(socs_kernel, 256, len(fields), bool(held...  10.5 us
    pallas_call x1, Pallas kernels, resident(): pl.pallas_call(resident_kernel, out_shape=[jax.ShapeDtypeStruct(first.sha...  3.51 us
    unnamed x16, local copies, waits for them, and re-layouts  3.27 us
  transfers between devices with their start and end apart: 6, of which 1 were waited for; matrix products, arithmetic and copies ran while one was open for 1% of the time, Pallas kernels for 20%

profile of v12, /device:TPU:32, one launch (start us, length us, event | category | flops | bytes accessed | tf_op | source)
XLA Modules:
  0.0 107.7 jit_solution(510853698799995502)
XLA Ops:
  0.0 1.1 dynamic-slice_bitcast_fusion
  1.1 1.9 %collective-permute-start = (bf16[2,1024,128]{2,1,0:T(8,128)(2,1)S(1)}, bf16[2,1024,128]{2,1,0:T(8,128)(2,1)S(1)}, u32[]{:S(2)}, u32[]{:S(2)}) collective-permute-start(bf16[2,1024,128]{2,1,0:T(8,128)(2,1)S(1)} %dynamic-slice_bitcast_fusion), channel_id=1, source_target_pairs={{0,128},{128,0},{1,129},{129,1},{2,130},{130,2},{3,131},{131,3},{4... | collective-permute-start | bytes 1572872 | tf_op jit(solution)/shard_map/ppermute | solution.py:196
  3.0 1.0 dynamic-slice_bitcast_fusion.1
  4.0 0.3 collective-permute-start.1
  4.3 1.4 %copy-done = bf16[1,6,1024,128]{3,2,1,0:T(8,128)(2,1)S(1)} copy-done((bf16[1,6,1024,128]{3,2,1,0:T(8,128)(2,1)S(1)}, bf16[1,6,1024,128]{3,2,1,0:T(8,128)(2,1)}, u32[]{:S(2)}) %copy-start) | copy-done | bytes 1572888
  5.7 1.1 %copy-done.3 = bf16[5,5,128,128]{3,2,1,0:T(8,128)(2,1)S(1)} copy-done((bf16[5,5,128,128]{3,2,1,0:T(8,128)(2,1)S(1)}, bf16[5,5,128,128]{3,2,1,0:T(8,128)(2,1)}, u32[]{:S(2)}) %copy-start.3) | copy-done | bytes 819224
  6.8 0.7 copy-done.5
  7.5 5.3 %conv_stage.3 = (bf16[1,16,1024]{2,1,0:T(8,128)(2,1)S(1)}, f32[4,1024,128]{2,1,0:T(8,128)S(1)}) custom-call(s32[1]{0:T(128)} %bitcast.flip_ref, bf16[6,1024,128]{2,1,0:T(8,128)(2,1)S(1)} %bitcast.36, bf16[5,640,128]{2,1,0:T(8,128)(2,1)S(1)} %bitcast.37, bf16[16,128]{1,0:T(8,128)(2,1)S(1)} %bitcast.40), custom_call_target="tpu_custom_call" | custom-call | flops 4026531840 | bytes 4194304 | tf_op jit(solution)/shard_map/conv_stage/pallas_call | solution.py:81
  12.8 3.2 %collective-permute-done.refs_0_ = bf16[2,1024,128]{2,1,0:T(8,128)(2,1)S(1)} collective-permute-done((bf16[2,1024,128]{2,1,0:T(8,128)(2,1)S(1)}, bf16[2,1024,128]{2,1,0:T(8,128)(2,1)S(1)}, u32[]{:S(2)}, u32[]{:S(2)}) %collective-permute-start) | collective-permute-done | bytes 524320 | tf_op jit(solution)/shard_map/ppermute | solution.py:196
  16.0 4.7 %conv_stage.4 = (bf16[2,16,1024]{2,1,0:T(8,128)(2,1)S(1)}, f32[3,1024,128]{2,1,0:T(8,128)S(1)}) custom-call(s32[1]{0:T(128)} %bitcast.flip_ref, bf16[2,1024,128]{2,1,0:T(8,128)(2,1)S(1)} %collective-permute-done.refs_0_, bf16[5,640,128]{2,1,0:T(8,128)(2,1)S(1)} %bitcast.38, bf16[16,128]{1,0:T(8,128)(2,1)S(1)} %bitcast.41, ...), custom_call_target="tpu_custom_call" | custom-call | flops 3019898880 | bytes 4194304 | tf_op jit(solution)/shard_map/conv_stage/pallas_call | solution.py:81
  20.7 0.0 copy-start.7
  20.7 3.5 %conv_stage.5 = bf16[3,16,1024]{2,1,0:T(8,128)(2,1)S(1)} custom-call(s32[1]{0:T(128)} %bitcast.flip_ref, bf16[1,1024,128]{2,1,0:T(8,128)(2,1)S(1)} %collective-permute-done.1.refs_0_, bf16[5,640,128]{2,1,0:T(8,128)(2,1)S(1)} %bitcast.39, bf16[16,128]{1,0:T(8,128)(2,1)S(1)} %bitcast.42, f32[3,1024,128]{2,1,0:T(8,128)S(1)} %get-tuple-element.24.refs_3_), custom_call_target="tpu_custom_call" | custom-call | flops 1006632960 | bytes 4194304 | tf_op jit(solution)/shard_map/conv_stage/pallas_call | solution.py:81
  24.2 0.2 collective-permute-start.2
  24.4 0.1 pad_add_fusion.place_ref
  24.5 0.1 reshape.32
  24.6 0.1 copy.24
  24.7 15.5 %all_to_all.15 = bf16[8,2,6,1024]{3,1,2,0:T(2,128)(2,1)S(1)} all-to-all(bf16[8,2,6,1024]{3,1,2,0:T(2,128)(2,1)S(1)} %bitcast.43), channel_id=1, replica_groups=mesh['s'=2,'y'=4,'xh'=2,'xl'=2,'z'=4,'c'=2] {'y','xh'}, dimensions={0} | all-to-all | bytes 393216 | tf_op jit(solution)/shard_map/all_to_all | solution.py:222
  40.2 0.1 copy.23
  40.3 0.7 collective-permute-start.3
  40.9 21.1 %all_gather.3.refs_0_ = bf16[8,48,1024]{2,1,0:T(8,128)(2,1)S(1)} all-gather(bf16[2,48,1024]{2,1,0:T(8,128)(2,1)S(1)} %bitcast.46), channel_id=1, replica_groups=mesh['s'=2,'y'=4,'xh'=2,'xl'=2,'z'=4,'c'=2] {'z'}, dimensions={0}, use_global_device_ids=true | all-gather | bytes 983040 | tf_op jit(solution)/shard_map/all_gather | solution.py:225
  62.1 1.5 %collective-permute-start.5 = (bf16[4,48,1024]{2,1,0:T(8,128)(2,1)S(1)}, bf16[4,48,1024]{2,1,0:T(8,128)(2,1)S(1)}, u32[]{:S(2)}, u32[]{:S(2)}) collective-permute-start(bf16[4,48,1024]{2,1,0:T(8,128)(2,1)S(1)} %pad_maximum_fusion), channel_id=1, source_target_pairs={{0,8},{8,0},{1,9},{9,1},{2,10},{10,2},{3,11},{11,3},{4,12},{12,4},... | collective-permute-start | bytes 1179656 | tf_op jit(solution)/shard_map/ppermute | solution.py:228
  63.7 0.1 copy.19.order_ref
  63.8 0.7 collective-permute-start.4
  64.4 3.5 %resident.1 = (bf16[1024,2048]{1,0:T(8,128)(2,1)S(1)}, bf16[1024,2048]{1,0:T(8,128)(2,1)S(1)}) custom-call(bf16[1024,2048]{1,0:T(8,128)(2,1)} %bitcast.12.first_ref, bf16[1024,2048]{1,0:T(8,128)(2,1)} %collective-permute-done.2.second_ref), custom_call_target="tpu_custom_call" | custom-call | bytes 16777216 | tf_op jit(solution)/shard_map/resident/pallas_call | solution.py:174
  68.0 5.5 %socs_image.3.refs_1_ = bf16[240,1024]{1,0:T(8,128)(2,1)S(1)} custom-call(f32[8]{0:T(128)S(1)} %copy-done.2, s32[2]{0:T(128)S(1)} %pad_add_fusion.place_ref, bf16[192,192]{1,0:T(8,128)(2,1)S(1)} %copy-done.1, bf16[1024,2048]{1,0:T(8,128)(2,1)S(1)} %get-tuple-element.29.first_ref, bf16[1024,2048]{1,0:T(8,128)(2,1)S(1)} %get-tuple-element.30.second_ref, ...), custom_call_target="tpu_custom_call" | custom-call | flops 4026531840 | bytes 9437184 | tf_op jit(solution)/shard_map/socs_image/pallas_call | solution.py:144
  73.5 2.4 %socs_image.4.refs_2_ = bf16[96,1024]{1,0:T(8,128)(2,1)S(1)} custom-call(f32[8]{0:T(128)S(1)} %copy-done.2, s32[2]{0:T(128)S(1)} %pad_add_fusion.place_ref, bf16[192,192]{1,0:T(8,128)(2,1)S(1)} %copy-done.1, bf16[1024,2048]{1,0:T(8,128)(2,1)S(1)} %get-tuple-element.29.first_ref, bf16[1024,2048]{1,0:T(8,128)(2,1)S(1)} %get-tuple-element.30.second_ref, ...), custom_call_target="tpu_custom_call" | custom-call | flops 1610612736 | bytes 9437184 | tf_op jit(solution)/shard_map/socs_image/pallas_call | solution.py:144
  75.9 2.6 %socs_image.5 = bf16[8,2,24,1024]{3,2,1,0:T(8,128)(2,1)S(1)} custom-call(f32[8]{0:T(128)S(1)} %copy-done.2, s32[2]{0:T(128)S(1)} %pad_add_fusion.place_ref, bf16[192,192]{1,0:T(8,128)(2,1)S(1)} %copy.19.order_ref, bf16[1024,2048]{1,0:T(8,128)(2,1)S(1)} %get-tuple-element.29.first_ref, bf16[1024,2048]{1,0:T(8,128)(2,1)S(1)} %get-tuple-element.30.second_ref, ...), custom_call_target="tpu_custom_call" | custom-call | flops 805306368 | bytes 9437184 | tf_op jit(solution)/shard_map/socs_image/pallas_call | solution.py:144
  78.5 15.4 %all_to_all.16 = bf16[16,24,1024]{2,1,0:T(8,128)(2,1)S(1)} all-to-all(bf16[16,24,1024]{2,1,0:T(8,128)(2,1)S(1)} %bitcast.33), channel_id=1, replica_groups=mesh['s'=2,'y'=4,'xh'=2,'xl'=2,'z'=4,'c'=2] {'y','xh','xl'}, dimensions={0} | all-to-all | bytes 1572864 | tf_op jit(solution)/shard_map/all_to_all | solution.py:235
  93.9 0.1 convert_reduce_fusion
  94.1 0.1 reshape.37
  94.2 12.8 %all_to_all.17 = f32[8,24,128]{2,1,0:T(8,128)S(1)} all-to-all(f32[8,24,128]{2,1,0:T(8,128)S(1)} %reshape.37), channel_id=1, replica_groups=mesh['s'=2,'y'=4,'xh'=2,'xl'=2,'z'=4,'c'=2] {'z','s'}, dimensions={0} | all-to-all | bytes 196608 | tf_op jit(solution)/shard_map/all_to_all | solution.py:240
  107.1 0.6 pad_maximum_fusion.3
  (27 shorter events, 0.3 us)
Async XLA Ops:
  1.1 14.9 %collective-permute-start = (bf16[2,1024,128]{2,1,0:T(8,128)(2,1)S(1)}, bf16[2,1024,128]{2,1,0:T(8,128)(2,1)S(1)}, u32[]{:S(2)}, u32[]{:S(2)}) collective-permute-start(bf16[2,1024,128]{2,1,0:T(8,128)(2,1)S(1)} %dynamic-slice_bitcast_fusion), channel_id=1, source_target_pairs={{0,128},{128,0},{1,129},{129,1},{2,130},{130,2},{3,131},{131,3},{4... | collective-permute-start | bytes 1572872 | tf_op jit(solution)/shard_map/ppermute | solution.py:196
  4.0 16.7 %collective-permute-start.1 = (bf16[1,1024,128]{2,1,0:T(8,128)(2,1)S(1)}, bf16[1,1024,128]{2,1,0:T(8,128)(2,1)S(1)}, u32[]{:S(2)}, u32[]{:S(2)}) collective-permute-start(bf16[1,1024,128]{2,1,0:T(8,128)(2,1)S(1)} %dynamic-slice_bitcast_fusion.1), channel_id=1, source_target_pairs={{0,128},{128,0},{1,129},{129,1},{2,130},{130,2},{3,131},{131,3},{4... | collective-permute-start | bytes 786440 | tf_op jit(solution)/shard_map/ppermute | solution.py:196
  4.3 1.4 %copy-start = (bf16[1,6,1024,128]{3,2,1,0:T(8,128)(2,1)S(1)}, bf16[1,6,1024,128]{3,2,1,0:T(8,128)(2,1)}, u32[]{:S(2)}) copy-start(bf16[1,6,1024,128]{3,2,1,0:T(8,128)(2,1)} %param.7) | copy-start | bytes 4718596
  5.7 1.1 %copy-start.3 = (bf16[5,5,128,128]{3,2,1,0:T(8,128)(2,1)S(1)}, bf16[5,5,128,128]{3,2,1,0:T(8,128)(2,1)}, u32[]{:S(2)}) copy-start(bf16[5,5,128,128]{3,2,1,0:T(8,128)(2,1)} %param.8) | copy-start | bytes 2457604
  6.8 0.7 copy-start.5
  7.5 8.5 %copy-start.4 = (bf16[5,5,128,128]{3,2,1,0:T(8,128)(2,1)S(1)}, bf16[5,5,128,128]{3,2,1,0:T(8,128)(2,1)}, u32[]{:S(2)}) copy-start(bf16[5,5,128,128]{3,2,1,0:T(8,128)(2,1)} %param.8) | copy-start | bytes 2457604
  7.5 8.5 %copy-start.6 = (bf16[128,16]{0,1:T(8,128)(2,1)S(1)}, bf16[128,16]{0,1:T(8,128)(2,1)}, u32[]{:S(2)}) copy-start(bf16[128,16]{0,1:T(8,128)(2,1)} %param.9) | copy-start | bytes 12292
  20.7 3.8 %copy-start.7 = (bf16[8,192,48]{1,2,0:T(8,128)(2,1)S(1)}, bf16[8,192,48]{1,2,0:T(8,128)(2,1)}, u32[]{:S(2)}) copy-start(bf16[8,192,48]{1,2,0:T(8,128)(2,1)} %constant.62.clone) | copy-start | bytes 442372
  24.2 40.3 %collective-permute-start.2 = (bf16[1024,2048]{1,0:T(8,128)(2,1)}, bf16[1024,2048]{1,0:T(8,128)(2,1)}, u32[]{:S(2)}, u32[]{:S(2)}) collective-permute-start(bf16[1024,2048]{1,0:T(8,128)(2,1)} %bitcast.12.first_ref), channel_id=1, source_target_pairs={{0,1},{1,0},{2,3},{3,2},{4,5},{5,4},{6,7},{7,6},{8,9},{9,8},{10,11... | collective-permute-start | bytes 12582920 | tf_op jit(solution)/shard_map/ppermute | solution.py:209
  40.3 21.7 %collective-permute-start.3 = (bf16[2,48,1024]{2,1,0:T(8,128)(2,1)S(1)}, bf16[2,48,1024]{2,1,0:T(8,128)(2,1)S(1)}, u32[]{:S(2)}, u32[]{:S(2)}) collective-permute-start(bf16[2,48,1024]{2,1,0:T(8,128)(2,1)S(1)} %bitcast.45), channel_id=1, source_target_pairs={{0,8},{8,0},{1,9},{9,1},{2,10},{10,2},{3,11},{11,3},{4,12},{12,4},... | collective-permute-start | bytes 589832 | tf_op jit(solution)/shard_map/ppermute | solution.py:224
  62.1 11.4 %collective-permute-start.5 = (bf16[4,48,1024]{2,1,0:T(8,128)(2,1)S(1)}, bf16[4,48,1024]{2,1,0:T(8,128)(2,1)S(1)}, u32[]{:S(2)}, u32[]{:S(2)}) collective-permute-start(bf16[4,48,1024]{2,1,0:T(8,128)(2,1)S(1)} %pad_maximum_fusion), channel_id=1, source_target_pairs={{0,8},{8,0},{1,9},{9,1},{2,10},{10,2},{3,11},{11,3},{4,12},{12,4},... | collective-permute-start | bytes 1179656 | tf_op jit(solution)/shard_map/ppermute | solution.py:228
  63.8 4.2 %copy-start.1 = (bf16[192,192]{1,0:T(8,128)(2,1)S(1)}, bf16[192,192]{1,0:T(8,128)(2,1)}, u32[]{:S(2)}) copy-start(bf16[192,192]{1,0:T(8,128)(2,1)} %constant.63.clone.order_ref) | copy-start | bytes 221188
  63.8 4.2 %copy-start.2 = (f32[8]{0:T(128)S(1)}, f32[8]{0:T(128)}, u32[]{:S(2)}) copy-start(f32[8]{0:T(128)} %weight_ref.5) | copy-start | bytes 100
  63.8 12.1 %collective-permute-start.4 = (bf16[2,48,1024]{2,1,0:T(8,128)(2,1)S(1)}, bf16[2,48,1024]{2,1,0:T(8,128)(2,1)S(1)}, u32[]{:S(2)}, u32[]{:S(2)}) collective-permute-start(bf16[2,48,1024]{2,1,0:T(8,128)(2,1)S(1)} %get-tuple-element.39), channel_id=1, source_target_pairs={{0,8},{8,0},{1,9},{9,1},{2,10},{10,2},{3,11},{11,3},{4,12},{12,4},... | collective-permute-start | bytes 589832 | tf_op jit(solution)/shard_map/ppermute | solution.py:229

commit v13 on v11

--- a/solution.py
+++ b/solution.py
@@ -76,7 +76,7 @@
     terms = sum(abs(i - o) <= 2 for i in lines for o in range(LINES))
     vmem = pl.BlockSpec(memory_space=pltpu.VMEM)
     out = pl.pallas_call(
-        functools.partial(conv_kernel, lines, done, before, pixels, 256),
+        functools.partial(conv_kernel, lines, done, before, pixels, pixels),
         out_shape=out_shape,
         in_specs=[pl.BlockSpec(memory_space=pltpu.SMEM)] + [vmem] * (3 + len(held)),
         out_specs=[vmem] * len(out_shape),

time: 108 us -> 106 us (0.981)
  Pallas kernels: 27.5 us -> 25 us
    pallas_call x3, Pallas kernels: 13.5 us -> 11 us  [conv_stage(): pl.pallas_call(functools.partial(conv_kernel, lines, done, before, pixels...]
  transfers between devices with their start and end apart: 6 -> 6, of which waited for: 1 -> 2; matrix products, arithmetic and copies ran while one was open for 1% -> 1% of each run, Pallas kernels for 20% -> 19%
where the time goes in v13:
time: 106 us
  blocking collectives  64.8 us (61%)
  Pallas kernels  25 us (24%)
  local copies, waits for them, and re-layouts  5.84 us (6%)
  starting transfers between devices  5.26 us (5%)
  waiting for transfers between devices  3.93 us (4%)
    all_gather x1, blocking collectives, on_device(): own = lax.all_gather(near, 'z', axis=0, tiled=True)  21.4 us
    all_to_all x1, blocking collectives, on_device(): pieces = lax.all_to_all(images, ('y', 'xh', 'xl'), 0, 0, tiled=True)  15.5 us
    all_to_all x1, blocking collectives, on_device(): near = lax.all_to_all(near, ('y', 'xh'), 0, 0, tiled=True)  15.5 us
    all_to_all x1, blocking collectives, on_device(): total = lax.all_to_all(total, ('s', 'z'), 0, 0, tiled=True)  12.3 us
    pallas_call x3, Pallas kernels, conv_stage(): pl.pallas_call(functools.partial(conv_kernel, lines, done, before, pixels...  11 us
    pallas_call x3, Pallas kernels, socs_image(): pl.pallas_call(functools.partial(socs_kernel, 256, len(fields), bool(held...  10.5 us
    ppermute x2, waiting for transfers between devices, halo(): return lax.ppermute(block[:, 0], 's', SWAP)  3.92 us
    pallas_call x1, Pallas kernels, resident(): pl.pallas_call(resident_kernel, out_shape=[jax.ShapeDtypeStruct(first.sha...  3.51 us
  transfers between devices with their start and end apart: 6, of which 2 were waited for; matrix products, arithmetic and copies ran while one was open for 1% of the time, Pallas kernels for 19%

profile of v13, /device:TPU:32, one launch (start us, length us, event | category | flops | bytes accessed | tf_op | source)
XLA Modules:
  0.0 106.0 jit_solution(13909388350617475093)
XLA Ops:
  0.0 1.1 %dynamic-slice_bitcast_fusion = bf16[2,1024,128]{2,1,0:T(8,128)(2,1)S(1)} fusion(bf16[3,2,1024,128]{3,2,1,0:T(8,128)(2,1)} %bitcast.48, s32[]{:T(128)S(6)} %select_n.51, s32[]{:T(128)S(6)} %select_n.52), kind=kLoop, calls=%fused_computation.1 | loop fusion | bytes 1048584 | tf_op jit(solution)/shard_map/squeeze | solution.py:193
  1.1 1.9 %collective-permute-start = (bf16[2,1024,128]{2,1,0:T(8,128)(2,1)S(1)}, bf16[2,1024,128]{2,1,0:T(8,128)(2,1)S(1)}, u32[]{:S(2)}, u32[]{:S(2)}) collective-permute-start(bf16[2,1024,128]{2,1,0:T(8,128)(2,1)S(1)} %dynamic-slice_bitcast_fusion), channel_id=1, source_target_pairs={{0,128},{128,0},{1,129},{129,1},{2,130},{130,2},{3,131},{131,3},{4... | collective-permute-start | bytes 1572872 | tf_op jit(solution)/shard_map/ppermute | solution.py:193
  3.0 1.0 dynamic-slice_bitcast_fusion.1
  4.0 0.3 collective-permute-start.1
  4.3 1.4 %copy-done = bf16[1,6,1024,128]{3,2,1,0:T(8,128)(2,1)S(1)} copy-done((bf16[1,6,1024,128]{3,2,1,0:T(8,128)(2,1)S(1)}, bf16[1,6,1024,128]{3,2,1,0:T(8,128)(2,1)}, u32[]{:S(2)}) %copy-start) | copy-done | bytes 1572888
  5.7 1.1 %copy-done.3 = bf16[5,5,128,128]{3,2,1,0:T(8,128)(2,1)S(1)} copy-done((bf16[5,5,128,128]{3,2,1,0:T(8,128)(2,1)S(1)}, bf16[5,5,128,128]{3,2,1,0:T(8,128)(2,1)}, u32[]{:S(2)}) %copy-start.3) | copy-done | bytes 819224
  6.8 0.7 copy-done.5
  7.5 5.0 %conv_stage.3 = (bf16[1,16,1024]{2,1,0:T(8,128)(2,1)S(1)}, f32[4,1024,128]{2,1,0:T(8,128)S(1)}) custom-call(s32[1]{0:T(128)} %bitcast.flip_ref, bf16[6,1024,128]{2,1,0:T(8,128)(2,1)S(1)} %bitcast.50, bf16[5,640,128]{2,1,0:T(8,128)(2,1)S(1)} %bitcast.51, bf16[16,128]{1,0:T(8,128)(2,1)S(1)} %bitcast.54), custom_call_target="tpu_custom_call" | custom-call | flops 4026531840 | bytes 4194304 | tf_op jit(solution)/shard_map/conv_stage/pallas_call | solution.py:78
  12.5 3.5 %collective-permute-done.refs_0_ = bf16[2,1024,128]{2,1,0:T(8,128)(2,1)S(1)} collective-permute-done((bf16[2,1024,128]{2,1,0:T(8,128)(2,1)S(1)}, bf16[2,1024,128]{2,1,0:T(8,128)(2,1)S(1)}, u32[]{:S(2)}, u32[]{:S(2)}) %collective-permute-start) | collective-permute-done | bytes 524320 | tf_op jit(solution)/shard_map/ppermute | solution.py:193
  16.0 4.0 %conv_stage.4 = (bf16[2,16,1024]{2,1,0:T(8,128)(2,1)S(1)}, f32[3,1024,128]{2,1,0:T(8,128)S(1)}) custom-call(s32[1]{0:T(128)} %bitcast.flip_ref, bf16[2,1024,128]{2,1,0:T(8,128)(2,1)S(1)} %collective-permute-done.refs_0_, bf16[5,640,128]{2,1,0:T(8,128)(2,1)S(1)} %bitcast.52, bf16[16,128]{1,0:T(8,128)(2,1)S(1)} %bitcast.55, ...), custom_call_target="tpu_custom_call" | custom-call | flops 3019898880 | bytes 4194304 | tf_op jit(solution)/shard_map/conv_stage/pallas_call | solution.py:78
  20.0 0.0 copy-start.7
  20.0 0.4 collective-permute-done.1.refs_0_
  20.4 2.0 %conv_stage.5 = bf16[3,16,1024]{2,1,0:T(8,128)(2,1)S(1)} custom-call(s32[1]{0:T(128)} %bitcast.flip_ref, bf16[1,1024,128]{2,1,0:T(8,128)(2,1)S(1)} %collective-permute-done.1.refs_0_, bf16[5,640,128]{2,1,0:T(8,128)(2,1)S(1)} %bitcast.53, bf16[16,128]{1,0:T(8,128)(2,1)S(1)} %bitcast.56, f32[3,1024,128]{2,1,0:T(8,128)S(1)} %get-tuple-element.24.refs_3_), custom_call_target="tpu_custom_call" | custom-call | flops 1006632960 | bytes 4194304 | tf_op jit(solution)/shard_map/conv_stage/pallas_call | solution.py:78
  22.4 0.1 pad_add_fusion.place_ref
  22.6 0.1 reshape.70
  22.6 0.1 copy.40
  22.8 15.5 %all_to_all.15 = bf16[8,2,6,1024]{3,1,2,0:T(2,128)(2,1)S(1)} all-to-all(bf16[8,2,6,1024]{3,1,2,0:T(2,128)(2,1)S(1)} %bitcast.57), channel_id=1, replica_groups=mesh['s'=2,'y'=4,'xh'=2,'xl'=2,'z'=4,'c'=2] {'y','xh'}, dimensions={0} | all-to-all | bytes 393216 | tf_op jit(solution)/shard_map/all_to_all | solution.py:219
  38.3 0.1 copy.39
  38.3 0.9 collective-permute-start.3
  39.2 21.4 %all_gather.3.refs_0_ = bf16[8,48,1024]{2,1,0:T(8,128)(2,1)S(1)} all-gather(bf16[2,48,1024]{2,1,0:T(8,128)(2,1)S(1)} %bitcast.60), channel_id=1, replica_groups=mesh['s'=2,'y'=4,'xh'=2,'xl'=2,'z'=4,'c'=2] {'z'}, dimensions={0}, use_global_device_ids=true | all-gather | bytes 983040 | tf_op jit(solution)/shard_map/all_gather | solution.py:222
  60.7 1.6 %collective-permute-start.5 = (bf16[4,48,1024]{2,1,0:T(8,128)(2,1)S(1)}, bf16[4,48,1024]{2,1,0:T(8,128)(2,1)S(1)}, u32[]{:S(2)}, u32[]{:S(2)}) collective-permute-start(bf16[4,48,1024]{2,1,0:T(8,128)(2,1)S(1)} %pad_maximum_fusion), channel_id=1, source_target_pairs={{0,8},{8,0},{1,9},{9,1},{2,10},{10,2},{3,11},{11,3},{4,12},{12,4},... | collective-permute-start | bytes 1179656 | tf_op jit(solution)/shard_map/ppermute | solution.py:225
  62.3 0.1 copy.30.order_ref
  62.5 0.6 collective-permute-start.4
  63.1 3.5 %resident.1 = (bf16[1024,2048]{1,0:T(8,128)(2,1)S(1)}, bf16[1024,2048]{1,0:T(8,128)(2,1)S(1)}) custom-call(bf16[1024,2048]{1,0:T(8,128)(2,1)} %bitcast.12.first_ref, bf16[1024,2048]{1,0:T(8,128)(2,1)} %collective-permute-done.2.second_ref), custom_call_target="tpu_custom_call" | custom-call | bytes 16777216 | tf_op jit(solution)/shard_map/resident/pallas_call | solution.py:171
  66.6 5.5 %socs_image.3.refs_1_ = bf16[240,1024]{1,0:T(8,128)(2,1)S(1)} custom-call(f32[8]{0:T(128)S(1)} %copy-done.2, s32[2]{0:T(128)S(1)} %pad_add_fusion.place_ref, bf16[192,192]{1,0:T(8,128)(2,1)S(1)} %copy-done.1, bf16[1024,2048]{1,0:T(8,128)(2,1)S(1)} %get-tuple-element.29.first_ref, bf16[1024,2048]{1,0:T(8,128)(2,1)S(1)} %get-tuple-element.30.second_ref, ...), custom_call_target="tpu_custom_call" | custom-call | flops 4026531840 | bytes 9437184 | tf_op jit(solution)/shard_map/socs_image/pallas_call | solution.py:141
  72.1 2.4 %socs_image.4.refs_2_ = bf16[96,1024]{1,0:T(8,128)(2,1)S(1)} custom-call(f32[8]{0:T(128)S(1)} %copy-done.2, s32[2]{0:T(128)S(1)} %pad_add_fusion.place_ref, bf16[192,192]{1,0:T(8,128)(2,1)S(1)} %copy-done.1, bf16[1024,2048]{1,0:T(8,128)(2,1)S(1)} %get-tuple-element.29.first_ref, bf16[1024,2048]{1,0:T(8,128)(2,1)S(1)} %get-tuple-element.30.second_ref, ...), custom_call_target="tpu_custom_call" | custom-call | flops 1610612736 | bytes 9437184 | tf_op jit(solution)/shard_map/socs_image/pallas_call | solution.py:141
  74.5 2.6 %socs_image.5 = bf16[8,2,24,1024]{3,2,1,0:T(8,128)(2,1)S(1)} custom-call(f32[8]{0:T(128)S(1)} %copy-done.2, s32[2]{0:T(128)S(1)} %pad_add_fusion.place_ref, bf16[192,192]{1,0:T(8,128)(2,1)S(1)} %copy.30.order_ref, bf16[1024,2048]{1,0:T(8,128)(2,1)S(1)} %get-tuple-element.29.first_ref, bf16[1024,2048]{1,0:T(8,128)(2,1)S(1)} %get-tuple-element.30.second_ref, ...), custom_call_target="tpu_custom_call" | custom-call | flops 805306368 | bytes 9437184 | tf_op jit(solution)/shard_map/socs_image/pallas_call | solution.py:141
  77.1 15.5 %all_to_all.16 = bf16[16,24,1024]{2,1,0:T(8,128)(2,1)S(1)} all-to-all(bf16[16,24,1024]{2,1,0:T(8,128)(2,1)S(1)} %bitcast.47), channel_id=1, replica_groups=mesh['s'=2,'y'=4,'xh'=2,'xl'=2,'z'=4,'c'=2] {'y','xh','xl'}, dimensions={0} | all-to-all | bytes 1572864 | tf_op jit(solution)/shard_map/all_to_all | solution.py:232
  92.7 0.1 convert_reduce_fusion
  92.9 0.1 reshape.75
  93.0 12.3 %all_to_all.17 = f32[8,24,128]{2,1,0:T(8,128)S(1)} all-to-all(f32[8,24,128]{2,1,0:T(8,128)S(1)} %reshape.75), channel_id=1, replica_groups=mesh['s'=2,'y'=4,'xh'=2,'xl'=2,'z'=4,'c'=2] {'s','z'}, dimensions={0} | all-to-all | bytes 196608 | tf_op jit(solution)/shard_map/all_to_all | solution.py:237
  105.4 0.6 pad_maximum_fusion.3
  (28 shorter events, 0.3 us)
Async XLA Ops:
  1.1 14.9 %collective-permute-start = (bf16[2,1024,128]{2,1,0:T(8,128)(2,1)S(1)}, bf16[2,1024,128]{2,1,0:T(8,128)(2,1)S(1)}, u32[]{:S(2)}, u32[]{:S(2)}) collective-permute-start(bf16[2,1024,128]{2,1,0:T(8,128)(2,1)S(1)} %dynamic-slice_bitcast_fusion), channel_id=1, source_target_pairs={{0,128},{128,0},{1,129},{129,1},{2,130},{130,2},{3,131},{131,3},{4... | collective-permute-start | bytes 1572872 | tf_op jit(solution)/shard_map/ppermute | solution.py:193
  4.0 16.5 %collective-permute-start.1 = (bf16[1,1024,128]{2,1,0:T(8,128)(2,1)S(1)}, bf16[1,1024,128]{2,1,0:T(8,128)(2,1)S(1)}, u32[]{:S(2)}, u32[]{:S(2)}) collective-permute-start(bf16[1,1024,128]{2,1,0:T(8,128)(2,1)S(1)} %dynamic-slice_bitcast_fusion.1), channel_id=1, source_target_pairs={{0,128},{128,0},{1,129},{129,1},{2,130},{130,2},{3,131},{131,3},{4... | collective-permute-start | bytes 786440 | tf_op jit(solution)/shard_map/ppermute | solution.py:193
  4.3 1.4 %copy-start = (bf16[1,6,1024,128]{3,2,1,0:T(8,128)(2,1)S(1)}, bf16[1,6,1024,128]{3,2,1,0:T(8,128)(2,1)}, u32[]{:S(2)}) copy-start(bf16[1,6,1024,128]{3,2,1,0:T(8,128)(2,1)} %param.7) | copy-start | bytes 4718596
  5.7 1.1 %copy-start.3 = (bf16[5,5,128,128]{3,2,1,0:T(8,128)(2,1)S(1)}, bf16[5,5,128,128]{3,2,1,0:T(8,128)(2,1)}, u32[]{:S(2)}) copy-start(bf16[5,5,128,128]{3,2,1,0:T(8,128)(2,1)} %param.8) | copy-start | bytes 2457604
  6.8 0.7 copy-start.5
  7.5 8.5 %copy-start.4 = (bf16[5,5,128,128]{3,2,1,0:T(8,128)(2,1)S(1)}, bf16[5,5,128,128]{3,2,1,0:T(8,128)(2,1)}, u32[]{:S(2)}) copy-start(bf16[5,5,128,128]{3,2,1,0:T(8,128)(2,1)} %param.8) | copy-start | bytes 2457604
  7.5 8.5 %copy-start.6 = (bf16[128,16]{0,1:T(8,128)(2,1)S(1)}, bf16[128,16]{0,1:T(8,128)(2,1)}, u32[]{:S(2)}) copy-start(bf16[128,16]{0,1:T(8,128)(2,1)} %param.9) | copy-start | bytes 12292
  20.0 2.5 %copy-start.7 = (bf16[8,192,48]{1,2,0:T(8,128)(2,1)S(1)}, bf16[8,192,48]{1,2,0:T(8,128)(2,1)}, u32[]{:S(2)}) copy-start(bf16[8,192,48]{1,2,0:T(8,128)(2,1)} %constant.62.clone) | copy-start | bytes 442372
  22.4 40.7 %collective-permute-start.2 = (bf16[1024,2048]{1,0:T(8,128)(2,1)}, bf16[1024,2048]{1,0:T(8,128)(2,1)}, u32[]{:S(2)}, u32[]{:S(2)}) collective-permute-start(bf16[1024,2048]{1,0:T(8,128)(2,1)} %bitcast.12.first_ref), channel_id=1, source_target_pairs={{0,1},{1,0},{2,3},{3,2},{4,5},{5,4},{6,7},{7,6},{8,9},{9,8},{10,11... | collective-permute-start | bytes 12582920 | tf_op jit(solution)/shard_map/ppermute | solution.py:206
  38.3 22.3 %collective-permute-start.3 = (bf16[2,48,1024]{2,1,0:T(8,128)(2,1)S(1)}, bf16[2,48,1024]{2,1,0:T(8,128)(2,1)S(1)}, u32[]{:S(2)}, u32[]{:S(2)}) collective-permute-start(bf16[2,48,1024]{2,1,0:T(8,128)(2,1)S(1)} %bitcast.59), channel_id=1, source_target_pairs={{0,8},{8,0},{1,9},{9,1},{2,10},{10,2},{3,11},{11,3},{4,12},{12,4},... | collective-permute-start | bytes 589832 | tf_op jit(solution)/shard_map/ppermute | solution.py:221
  60.7 11.4 %collective-permute-start.5 = (bf16[4,48,1024]{2,1,0:T(8,128)(2,1)S(1)}, bf16[4,48,1024]{2,1,0:T(8,128)(2,1)S(1)}, u32[]{:S(2)}, u32[]{:S(2)}) collective-permute-start(bf16[4,48,1024]{2,1,0:T(8,128)(2,1)S(1)} %pad_maximum_fusion), channel_id=1, source_target_pairs={{0,8},{8,0},{1,9},{9,1},{2,10},{10,2},{3,11},{11,3},{4,12},{12,4},... | collective-permute-start | bytes 1179656 | tf_op jit(solution)/shard_map/ppermute | solution.py:225
  62.4 4.2 %copy-start.1 = (bf16[192,192]{1,0:T(8,128)(2,1)S(1)}, bf16[192,192]{1,0:T(8,128)(2,1)}, u32[]{:S(2)}) copy-start(bf16[192,192]{1,0:T(8,128)(2,1)} %constant.63.clone.order_ref) | copy-start | bytes 221188
  62.5 4.2 %copy-start.2 = (f32[8]{0:T(128)S(1)}, f32[8]{0:T(128)}, u32[]{:S(2)}) copy-start(f32[8]{0:T(128)} %weight_ref.5) | copy-start | bytes 100
  62.5 12.1 %collective-permute-start.4 = (bf16[2,48,1024]{2,1,0:T(8,128)(2,1)S(1)}, bf16[2,48,1024]{2,1,0:T(8,128)(2,1)S(1)}, u32[]{:S(2)}, u32[]{:S(2)}) collective-permute-start(bf16[2,48,1024]{2,1,0:T(8,128)(2,1)S(1)} %get-tuple-element.39), channel_id=1, source_target_pairs={{0,8},{8,0},{1,9},{9,1},{2,10},{10,2},{3,11},{11,3},{4,12},{12,4},... | collective-permute-start | bytes 589832 | tf_op jit(solution)/shard_map/ppermute | solution.py:226

commit v14 on v13

--- a/solution.py
+++ b/solution.py
@@ -139,7 +139,7 @@
     else:
         out_shape = jax.ShapeDtypeStruct((rows, pixels), BF)
     return pl.pallas_call(
-        functools.partial(socs_kernel, 256, len(fields), bool(held)),
+        functools.partial(socs_kernel, 512, len(fields), bool(held)),
         out_shape=out_shape,
         in_specs=[scalar, scalar] + [vmem] * (3 + len(fields) + len(held)),
         out_specs=vmem,

time: 106 us -> 106 us (level)
  no operation moved by 1% of the time
where the time goes in v14:
time: 106 us
  blocking collectives  64.8 us (61%)
  Pallas kernels  24.5 us (23%)
  local copies, waits for them, and re-layouts  5.84 us (6%)
  starting transfers between devices  5.26 us (5%)
  waiting for transfers between devices  3.93 us (4%)
    all_gather x1, blocking collectives, on_device(): own = lax.all_gather(near, 'z', axis=0, tiled=True)  21.4 us
    all_to_all x1, blocking collectives, on_device(): pieces = lax.all_to_all(images, ('y', 'xh', 'xl'), 0, 0, tiled=True)  15.6 us
    all_to_all x1, blocking collectives, on_device(): near = lax.all_to_all(near, ('y', 'xh'), 0, 0, tiled=True)  15.5 us
    all_to_all x1, blocking collectives, on_device(): total = lax.all_to_all(total, ('s', 'z'), 0, 0, tiled=True)  12.3 us
    pallas_call x3, Pallas kernels, conv_stage(): pl.pallas_call(functools.partial(conv_kernel, lines, done, before, pixels...  11 us
    pallas_call x3, Pallas kernels, socs_image(): pl.pallas_call(functools.partial(socs_kernel, 512, len(fields), bool(held...  10 us
    ppermute x2, waiting for transfers between devices, halo(): return lax.ppermute(block[:, 0], 's', SWAP)  3.92 us
    pallas_call x1, Pallas kernels, resident(): pl.pallas_call(resident_kernel, out_shape=[jax.ShapeDtypeStruct(first.sha...  3.51 us
  transfers between devices with their start and end apart: 6, of which 2 were waited for; matrix products, arithmetic and copies ran while one was open for 1% of the time, Pallas kernels for 19%

profile of v14, /device:TPU:32, one launch (start us, length us, event | category | flops | bytes accessed | tf_op | source)
XLA Modules:
  0.0 105.5 jit_solution(323509443351816920)
XLA Ops:
  0.0 1.1 %dynamic-slice_bitcast_fusion = bf16[2,1024,128]{2,1,0:T(8,128)(2,1)S(1)} fusion(bf16[3,2,1024,128]{3,2,1,0:T(8,128)(2,1)} %bitcast.48, s32[]{:T(128)S(6)} %select_n.51, s32[]{:T(128)S(6)} %select_n.52), kind=kLoop, calls=%fused_computation.1 | loop fusion | bytes 1048584 | tf_op jit(solution)/shard_map/squeeze | solution.py:193
  1.1 1.9 %collective-permute-start = (bf16[2,1024,128]{2,1,0:T(8,128)(2,1)S(1)}, bf16[2,1024,128]{2,1,0:T(8,128)(2,1)S(1)}, u32[]{:S(2)}, u32[]{:S(2)}) collective-permute-start(bf16[2,1024,128]{2,1,0:T(8,128)(2,1)S(1)} %dynamic-slice_bitcast_fusion), channel_id=1, source_target_pairs={{0,128},{128,0},{1,129},{129,1},{2,130},{130,2},{3,131},{131,3},{4... | collective-permute-start | bytes 1572872 | tf_op jit(solution)/shard_map/ppermute | solution.py:193
  3.0 1.0 dynamic-slice_bitcast_fusion.1
  4.0 0.3 collective-permute-start.1
  4.3 1.4 %copy-done = bf16[1,6,1024,128]{3,2,1,0:T(8,128)(2,1)S(1)} copy-done((bf16[1,6,1024,128]{3,2,1,0:T(8,128)(2,1)S(1)}, bf16[1,6,1024,128]{3,2,1,0:T(8,128)(2,1)}, u32[]{:S(2)}) %copy-start) | copy-done | bytes 1572888
  5.7 1.1 %copy-done.3 = bf16[5,5,128,128]{3,2,1,0:T(8,128)(2,1)S(1)} copy-done((bf16[5,5,128,128]{3,2,1,0:T(8,128)(2,1)S(1)}, bf16[5,5,128,128]{3,2,1,0:T(8,128)(2,1)}, u32[]{:S(2)}) %copy-start.3) | copy-done | bytes 819224
  6.8 0.7 copy-done.5
  7.5 5.0 %conv_stage.3 = (bf16[1,16,1024]{2,1,0:T(8,128)(2,1)S(1)}, f32[4,1024,128]{2,1,0:T(8,128)S(1)}) custom-call(s32[1]{0:T(128)} %bitcast.flip_ref, bf16[6,1024,128]{2,1,0:T(8,128)(2,1)S(1)} %bitcast.50, bf16[5,640,128]{2,1,0:T(8,128)(2,1)S(1)} %bitcast.51, bf16[16,128]{1,0:T(8,128)(2,1)S(1)} %bitcast.54), custom_call_target="tpu_custom_call" | custom-call | flops 4026531840 | bytes 4194304 | tf_op jit(solution)/shard_map/conv_stage/pallas_call | solution.py:78
  12.5 3.5 %collective-permute-done.refs_0_ = bf16[2,1024,128]{2,1,0:T(8,128)(2,1)S(1)} collective-permute-done((bf16[2,1024,128]{2,1,0:T(8,128)(2,1)S(1)}, bf16[2,1024,128]{2,1,0:T(8,128)(2,1)S(1)}, u32[]{:S(2)}, u32[]{:S(2)}) %collective-permute-start) | collective-permute-done | bytes 524320 | tf_op jit(solution)/shard_map/ppermute | solution.py:193
  16.0 4.0 %conv_stage.4 = (bf16[2,16,1024]{2,1,0:T(8,128)(2,1)S(1)}, f32[3,1024,128]{2,1,0:T(8,128)S(1)}) custom-call(s32[1]{0:T(128)} %bitcast.flip_ref, bf16[2,1024,128]{2,1,0:T(8,128)(2,1)S(1)} %collective-permute-done.refs_0_, bf16[5,640,128]{2,1,0:T(8,128)(2,1)S(1)} %bitcast.52, bf16[16,128]{1,0:T(8,128)(2,1)S(1)} %bitcast.55, ...), custom_call_target="tpu_custom_call" | custom-call | flops 3019898880 | bytes 4194304 | tf_op jit(solution)/shard_map/conv_stage/pallas_call | solution.py:78
  20.0 0.0 copy-start.7
  20.0 0.4 collective-permute-done.1.refs_0_
  20.4 2.0 %conv_stage.5 = bf16[3,16,1024]{2,1,0:T(8,128)(2,1)S(1)} custom-call(s32[1]{0:T(128)} %bitcast.flip_ref, bf16[1,1024,128]{2,1,0:T(8,128)(2,1)S(1)} %collective-permute-done.1.refs_0_, bf16[5,640,128]{2,1,0:T(8,128)(2,1)S(1)} %bitcast.53, bf16[16,128]{1,0:T(8,128)(2,1)S(1)} %bitcast.56, f32[3,1024,128]{2,1,0:T(8,128)S(1)} %get-tuple-element.24.refs_3_), custom_call_target="tpu_custom_call" | custom-call | flops 1006632960 | bytes 4194304 | tf_op jit(solution)/shard_map/conv_stage/pallas_call | solution.py:78
  22.4 0.1 pad_add_fusion.place_ref
  22.6 0.1 reshape.70
  22.6 0.1 copy.40
  22.8 15.5 %all_to_all.15 = bf16[8,2,6,1024]{3,1,2,0:T(2,128)(2,1)S(1)} all-to-all(bf16[8,2,6,1024]{3,1,2,0:T(2,128)(2,1)S(1)} %bitcast.57), channel_id=1, replica_groups=mesh['s'=2,'y'=4,'xh'=2,'xl'=2,'z'=4,'c'=2] {'y','xh'}, dimensions={0} | all-to-all | bytes 393216 | tf_op jit(solution)/shard_map/all_to_all | solution.py:219
  38.3 0.1 copy.39
  38.3 0.9 collective-permute-start.3
  39.2 21.4 %all_gather.3.refs_0_ = bf16[8,48,1024]{2,1,0:T(8,128)(2,1)S(1)} all-gather(bf16[2,48,1024]{2,1,0:T(8,128)(2,1)S(1)} %bitcast.60), channel_id=1, replica_groups=mesh['s'=2,'y'=4,'xh'=2,'xl'=2,'z'=4,'c'=2] {'z'}, dimensions={0}, use_global_device_ids=true | all-gather | bytes 983040 | tf_op jit(solution)/shard_map/all_gather | solution.py:222
  60.7 1.6 %collective-permute-start.5 = (bf16[4,48,1024]{2,1,0:T(8,128)(2,1)S(1)}, bf16[4,48,1024]{2,1,0:T(8,128)(2,1)S(1)}, u32[]{:S(2)}, u32[]{:S(2)}) collective-permute-start(bf16[4,48,1024]{2,1,0:T(8,128)(2,1)S(1)} %pad_maximum_fusion), channel_id=1, source_target_pairs={{0,8},{8,0},{1,9},{9,1},{2,10},{10,2},{3,11},{11,3},{4,12},{12,4},... | collective-permute-start | bytes 1179656 | tf_op jit(solution)/shard_map/ppermute | solution.py:225
  62.3 0.1 copy.30.order_ref
  62.5 0.6 collective-permute-start.4
  63.1 3.5 %resident.1 = (bf16[1024,2048]{1,0:T(8,128)(2,1)S(1)}, bf16[1024,2048]{1,0:T(8,128)(2,1)S(1)}) custom-call(bf16[1024,2048]{1,0:T(8,128)(2,1)} %bitcast.12.first_ref, bf16[1024,2048]{1,0:T(8,128)(2,1)} %collective-permute-done.2.second_ref), custom_call_target="tpu_custom_call" | custom-call | bytes 16777216 | tf_op jit(solution)/shard_map/resident/pallas_call | solution.py:171
  66.6 5.2 %socs_image.3.refs_1_ = bf16[240,1024]{1,0:T(8,128)(2,1)S(1)} custom-call(f32[8]{0:T(128)S(1)} %copy-done.2, s32[2]{0:T(128)S(1)} %pad_add_fusion.place_ref, bf16[192,192]{1,0:T(8,128)(2,1)S(1)} %copy-done.1, bf16[1024,2048]{1,0:T(8,128)(2,1)S(1)} %get-tuple-element.29.first_ref, bf16[1024,2048]{1,0:T(8,128)(2,1)S(1)} %get-tuple-element.30.second_ref, ...), custom_call_target="tpu_custom_call" | custom-call | flops 4026531840 | bytes 9437184 | tf_op jit(solution)/shard_map/socs_image/pallas_call | solution.py:141
  71.8 2.4 %socs_image.4.refs_2_ = bf16[96,1024]{1,0:T(8,128)(2,1)S(1)} custom-call(f32[8]{0:T(128)S(1)} %copy-done.2, s32[2]{0:T(128)S(1)} %pad_add_fusion.place_ref, bf16[192,192]{1,0:T(8,128)(2,1)S(1)} %copy-done.1, bf16[1024,2048]{1,0:T(8,128)(2,1)S(1)} %get-tuple-element.29.first_ref, bf16[1024,2048]{1,0:T(8,128)(2,1)S(1)} %get-tuple-element.30.second_ref, ...), custom_call_target="tpu_custom_call" | custom-call | flops 1610612736 | bytes 9437184 | tf_op jit(solution)/shard_map/socs_image/pallas_call | solution.py:141
  74.3 2.4 %socs_image.5 = bf16[8,2,24,1024]{3,2,1,0:T(8,128)(2,1)S(1)} custom-call(f32[8]{0:T(128)S(1)} %copy-done.2, s32[2]{0:T(128)S(1)} %pad_add_fusion.place_ref, bf16[192,192]{1,0:T(8,128)(2,1)S(1)} %copy.30.order_ref, bf16[1024,2048]{1,0:T(8,128)(2,1)S(1)} %get-tuple-element.29.first_ref, bf16[1024,2048]{1,0:T(8,128)(2,1)S(1)} %get-tuple-element.30.second_ref, ...), custom_call_target="tpu_custom_call" | custom-call | flops 805306368 | bytes 9437184 | tf_op jit(solution)/shard_map/socs_image/pallas_call | solution.py:141
  76.7 15.6 %all_to_all.16 = bf16[16,24,1024]{2,1,0:T(8,128)(2,1)S(1)} all-to-all(bf16[16,24,1024]{2,1,0:T(8,128)(2,1)S(1)} %bitcast.47), channel_id=1, replica_groups=mesh['s'=2,'y'=4,'xh'=2,'xl'=2,'z'=4,'c'=2] {'y','xh','xl'}, dimensions={0} | all-to-all | bytes 1572864 | tf_op jit(solution)/shard_map/all_to_all | solution.py:232
  92.2 0.1 convert_reduce_fusion
  92.5 0.1 reshape.75
  92.6 12.3 %all_to_all.17 = f32[8,24,128]{2,1,0:T(8,128)S(1)} all-to-all(f32[8,24,128]{2,1,0:T(8,128)S(1)} %reshape.75), channel_id=1, replica_groups=mesh['s'=2,'y'=4,'xh'=2,'xl'=2,'z'=4,'c'=2] {'s','z'}, dimensions={0} | all-to-all | bytes 196608 | tf_op jit(solution)/shard_map/all_to_all | solution.py:237
  104.9 0.6 pad_maximum_fusion.3
  (28 shorter events, 0.3 us)
Async XLA Ops:
  1.1 14.9 %collective-permute-start = (bf16[2,1024,128]{2,1,0:T(8,128)(2,1)S(1)}, bf16[2,1024,128]{2,1,0:T(8,128)(2,1)S(1)}, u32[]{:S(2)}, u32[]{:S(2)}) collective-permute-start(bf16[2,1024,128]{2,1,0:T(8,128)(2,1)S(1)} %dynamic-slice_bitcast_fusion), channel_id=1, source_target_pairs={{0,128},{128,0},{1,129},{129,1},{2,130},{130,2},{3,131},{131,3},{4... | collective-permute-start | bytes 1572872 | tf_op jit(solution)/shard_map/ppermute | solution.py:193
  4.0 16.5 %collective-permute-start.1 = (bf16[1,1024,128]{2,1,0:T(8,128)(2,1)S(1)}, bf16[1,1024,128]{2,1,0:T(8,128)(2,1)S(1)}, u32[]{:S(2)}, u32[]{:S(2)}) collective-permute-start(bf16[1,1024,128]{2,1,0:T(8,128)(2,1)S(1)} %dynamic-slice_bitcast_fusion.1), channel_id=1, source_target_pairs={{0,128},{128,0},{1,129},{129,1},{2,130},{130,2},{3,131},{131,3},{4... | collective-permute-start | bytes 786440 | tf_op jit(solution)/shard_map/ppermute | solution.py:193
  4.3 1.4 %copy-start = (bf16[1,6,1024,128]{3,2,1,0:T(8,128)(2,1)S(1)}, bf16[1,6,1024,128]{3,2,1,0:T(8,128)(2,1)}, u32[]{:S(2)}) copy-start(bf16[1,6,1024,128]{3,2,1,0:T(8,128)(2,1)} %param.7) | copy-start | bytes 4718596
  5.7 1.1 %copy-start.3 = (bf16[5,5,128,128]{3,2,1,0:T(8,128)(2,1)S(1)}, bf16[5,5,128,128]{3,2,1,0:T(8,128)(2,1)}, u32[]{:S(2)}) copy-start(bf16[5,5,128,128]{3,2,1,0:T(8,128)(2,1)} %param.8) | copy-start | bytes 2457604
  6.8 0.7 copy-start.5
  7.5 8.5 %copy-start.4 = (bf16[5,5,128,128]{3,2,1,0:T(8,128)(2,1)S(1)}, bf16[5,5,128,128]{3,2,1,0:T(8,128)(2,1)}, u32[]{:S(2)}) copy-start(bf16[5,5,128,128]{3,2,1,0:T(8,128)(2,1)} %param.8) | copy-start | bytes 2457604
  7.5 8.5 %copy-start.6 = (bf16[128,16]{0,1:T(8,128)(2,1)S(1)}, bf16[128,16]{0,1:T(8,128)(2,1)}, u32[]{:S(2)}) copy-start(bf16[128,16]{0,1:T(8,128)(2,1)} %param.9) | copy-start | bytes 12292
  20.0 2.5 %copy-start.7 = (bf16[8,192,48]{1,2,0:T(8,128)(2,1)S(1)}, bf16[8,192,48]{1,2,0:T(8,128)(2,1)}, u32[]{:S(2)}) copy-start(bf16[8,192,48]{1,2,0:T(8,128)(2,1)} %constant.62.clone) | copy-start | bytes 442372
  22.4 40.7 %collective-permute-start.2 = (bf16[1024,2048]{1,0:T(8,128)(2,1)}, bf16[1024,2048]{1,0:T(8,128)(2,1)}, u32[]{:S(2)}, u32[]{:S(2)}) collective-permute-start(bf16[1024,2048]{1,0:T(8,128)(2,1)} %bitcast.12.first_ref), channel_id=1, source_target_pairs={{0,1},{1,0},{2,3},{3,2},{4,5},{5,4},{6,7},{7,6},{8,9},{9,8},{10,11... | collective-permute-start | bytes 12582920 | tf_op jit(solution)/shard_map/ppermute | solution.py:206
  38.3 22.3 %collective-permute-start.3 = (bf16[2,48,1024]{2,1,0:T(8,128)(2,1)S(1)}, bf16[2,48,1024]{2,1,0:T(8,128)(2,1)S(1)}, u32[]{:S(2)}, u32[]{:S(2)}) collective-permute-start(bf16[2,48,1024]{2,1,0:T(8,128)(2,1)S(1)} %bitcast.59), channel_id=1, source_target_pairs={{0,8},{8,0},{1,9},{9,1},{2,10},{10,2},{3,11},{11,3},{4,12},{12,4},... | collective-permute-start | bytes 589832 | tf_op jit(solution)/shard_map/ppermute | solution.py:221
  60.7 11.1 %collective-permute-start.5 = (bf16[4,48,1024]{2,1,0:T(8,128)(2,1)S(1)}, bf16[4,48,1024]{2,1,0:T(8,128)(2,1)S(1)}, u32[]{:S(2)}, u32[]{:S(2)}) collective-permute-start(bf16[4,48,1024]{2,1,0:T(8,128)(2,1)S(1)} %pad_maximum_fusion), channel_id=1, source_target_pairs={{0,8},{8,0},{1,9},{9,1},{2,10},{10,2},{3,11},{11,3},{4,12},{12,4},... | collective-permute-start | bytes 1179656 | tf_op jit(solution)/shard_map/ppermute | solution.py:225
  62.4 4.2 %copy-start.1 = (bf16[192,192]{1,0:T(8,128)(2,1)S(1)}, bf16[192,192]{1,0:T(8,128)(2,1)}, u32[]{:S(2)}) copy-start(bf16[192,192]{1,0:T(8,128)(2,1)} %constant.63.clone.order_ref) | copy-start | bytes 221188
  62.5 4.2 %copy-start.2 = (f32[8]{0:T(128)S(1)}, f32[8]{0:T(128)}, u32[]{:S(2)}) copy-start(f32[8]{0:T(128)} %weight_ref.5) | copy-start | bytes 100
  62.5 11.8 %collective-permute-start.4 = (bf16[2,48,1024]{2,1,0:T(8,128)(2,1)S(1)}, bf16[2,48,1024]{2,1,0:T(8,128)(2,1)S(1)}, u32[]{:S(2)}, u32[]{:S(2)}) collective-permute-start(bf16[2,48,1024]{2,1,0:T(8,128)(2,1)S(1)} %get-tuple-element.39), channel_id=1, source_target_pairs={{0,8},{8,0},{1,9},{9,1},{2,10},{10,2},{3,11},{11,3},{4,12},{12,4},... | collective-permute-start | bytes 589832 | tf_op jit(solution)/shard_map/ppermute | solution.py:226
